TPU v7x, 128 devices: a whole 4x4x4 slice. The times are simulated.
128 devices in a mesh: img: 4 (over z_lo, core), exp: 32 (over x, y, z_hi).
Axes of the slice: x: 4, y: 4, z: 4 (z_hi: 2, z_lo: 2; z = z_hi * 2 + z_lo), core: 2. Of those that a mesh axis runs over, the one named last changes fastest.
Arguments:
- context: bfloat16 [256, 256, 1024], P(('img', 'exp')), may hold values from -1.5 to 1.5
- residual: bfloat16 [256, 256, 1024], P(('img', 'exp')), may hold values from -1.5 to 1.5
- cotangent: bfloat16 [256, 256, 1024], P(('img', 'exp')), may hold values from -6 to 6
- proj_weight: bfloat16 [1024, 1024], P('img'), may hold values from -0.1875 to 0.1875
- slot_params: bfloat16 [1024, 64], replicated, may hold values from -0.1875 to 0.1875
- expert_in: bfloat16 [64, 1024, 4096], P('exp', None, 'img'), may hold values from -0.1875 to 0.1875
- expert_out: bfloat16 [64, 4096, 1024], P('exp', 'img'), may hold values from -0.09375 to 0.09375
Outputs:
- grad_context: bfloat16 [256, 256, 1024], P(('img', 'exp'))
- grad_residual: bfloat16 [256, 256, 1024], P(('img', 'exp'))
- grad_proj: float32 [1024, 1024], P('img')
- grad_slots: float32 [1024, 64], replicated
- grad_expert_in: bfloat16 [64, 1024, 4096], P('exp', None, 'img')
- grad_expert_out: bfloat16 [64, 4096, 1024], P('exp', 'img')
All inputs are finite; a program needn't handle non-finite values.
Results may differ from a plain program's by a relative error of at most 0.025.
Values may be sent and summed in bfloat16 or wider, within the bound.
A program may use at most 128 MiB of HBM per device.

v0:
```python
import math

import jax
import jax.numpy as jnp
from jax import lax
from jax.sharding import Mesh
from jax.sharding import PartitionSpec as P

IMG = ("img_0", "img_1")
IMG_EXP = ("img_0", "img_1", "exp")


logit_scale = 48.0
epsilon = 1e-06


def copy_for_each(shard, axis):
    devices = lax.axis_size(axis)
    return lax.all_to_all(
        jnp.broadcast_to(shard[None], (devices, *shard.shape)), axis, 0, 0, tiled=True
    )


def laid_out(pieces, dim):
    pieces = jnp.moveaxis(pieces, 0, dim)
    dims = pieces.shape
    return pieces.reshape(*dims[:dim], dims[dim] * dims[dim + 1], *dims[dim + 2 :])


def gather_directly(shard, axis, dim):
    pieces = copy_for_each(shard, axis)
    return laid_out(pieces, dim)


def split_up(shard, dim, devices):
    before, after = (shard.shape[:dim], shard.shape[dim + 1 :])
    return jnp.moveaxis(shard.reshape(*before, devices, -1, *after), dim, 0)


def summed_on_arrival(shard, axis, dim):
    devices = lax.axis_size(axis)
    pieces = lax.all_to_all(split_up(shard, dim, devices), axis, 0, 0, tiled=True)
    return jnp.sum(pieces.astype(jnp.float32), axis=0)


def sum_in_two_steps(shard, axes, dim):
    far, near = axes
    own = summed_on_arrival(split_up(shard, dim, lax.axis_size(far)), near, dim + 1)
    return jnp.sum(
        lax.all_to_all(own.astype(jnp.bfloat16), far, 0, 0, tiled=True).astype(jnp.float32), axis=0
    )


def padded_to(lines, devices):
    spare = -lines.shape[0] % devices
    if not spare:
        return lines
    return jnp.concatenate([lines, jnp.zeros((spare, *lines.shape[1:]), lines.dtype)])


def nested_sum(shard, axes):
    lines = shard.reshape(-1, shard.shape[-1])
    own = summed_on_arrival(padded_to(lines, lax.axis_size(axes)), axes, 0)
    whole = gather_directly(own.astype(jnp.bfloat16), axes, 0)
    return whole[: len(lines)].reshape(shard.shape).astype(jnp.float32)


def gelu_back(pre, upstream):
    return jax.vjp(jax.nn.gelu, pre)[1](upstream)[0]


def shards(context, residual, cotangent, proj_weight, slot_params, expert_in, expert_out):
    images, tokens, width = context.shape
    rows = images * tokens
    factor = logit_scale / math.sqrt(width)
    flat_ctx = context.reshape(rows, width)
    columns = flat_ctx
    mixed = jnp.dot(
        columns, gather_directly(proj_weight, IMG, 0), preferred_element_type=jnp.float32
    )
    stream = (residual.reshape(rows, width).astype(jnp.float32) + mixed).astype(jnp.bfloat16)
    stream32 = stream.astype(jnp.float32)
    inverse = lax.rsqrt(jnp.mean(stream32 * stream32, axis=-1, keepdims=True) + epsilon)
    normed32 = stream32 * inverse
    normed = normed32.astype(jnp.bfloat16)
    params32 = slot_params.astype(jnp.float32)
    slot_norm = jnp.sqrt(jnp.sum(params32 * params32, axis=0, keepdims=True) + epsilon)
    unit32 = params32 / slot_norm
    unit = unit32.astype(jnp.bfloat16)
    logits = factor * jnp.dot(normed, unit, preferred_element_type=jnp.float32)
    logits = logits.reshape(images, tokens, -1)
    expo = jnp.exp(logits)
    dispatch32 = expo / jnp.sum(expo, axis=1, keepdims=True)
    combine32 = expo / jnp.sum(expo, axis=2, keepdims=True)
    dispatch = dispatch32.astype(jnp.bfloat16)
    combine = combine32.astype(jnp.bfloat16)
    normed3 = normed.reshape(images, tokens, width)
    slot_in = jnp.einsum(
        "bms,bmd->bsd", dispatch, normed3, preferred_element_type=jnp.float32
    ).astype(jnp.bfloat16)
    sent = lax.all_to_all(slot_in, "exp", split_axis=1, concat_axis=0, tiled=True)
    slot_rows = gather_directly(sent, IMG, 0)
    pre = jnp.einsum("gjd,jdf->gjf", slot_rows, expert_in, preferred_element_type=jnp.float32)
    act = jax.nn.gelu(pre).astype(jnp.bfloat16)
    piece = act
    summed = summed_on_arrival(
        jnp.einsum("gjf,jfd->gjd", piece, expert_out, preferred_element_type=jnp.float32).astype(
            jnp.bfloat16
        ),
        IMG,
        0,
    )
    slot_out = lax.all_to_all(
        summed.astype(jnp.bfloat16), "exp", split_axis=0, concat_axis=1, tiled=True
    )
    grad_slot_out = jnp.einsum(
        "bms,bmd->bsd", combine, cotangent, preferred_element_type=jnp.float32
    ).astype(jnp.bfloat16)
    grad_sent = lax.all_to_all(grad_slot_out, "exp", split_axis=1, concat_axis=0, tiled=True)
    grad_gathered = gather_directly(grad_sent, IMG, 0)
    grad_combine = jnp.einsum(
        "bmd,bsd->bms", cotangent, slot_out, preferred_element_type=jnp.float32
    )
    grad_act = jnp.einsum(
        "gjd,jfd->gjf", grad_gathered, expert_out, preferred_element_type=jnp.float32
    )
    grad_pre = gelu_back(pre, grad_act).astype(jnp.bfloat16)
    grad_expert_out = jnp.einsum(
        "gjf,gjd->jfd", act, grad_gathered, preferred_element_type=jnp.float32
    ).astype(jnp.bfloat16)
    grad_expert_in = jnp.einsum(
        "gjd,gjf->jdf", slot_rows, grad_pre, preferred_element_type=jnp.float32
    ).astype(jnp.bfloat16)
    piece = grad_pre
    grad_summed = summed_on_arrival(
        jnp.einsum("gjf,jdf->gjd", piece, expert_in, preferred_element_type=jnp.float32).astype(
            jnp.bfloat16
        ),
        IMG,
        0,
    )
    grad_slot_in = lax.all_to_all(
        grad_summed.astype(jnp.bfloat16), "exp", split_axis=0, concat_axis=1, tiled=True
    )
    grad_dispatch = jnp.einsum(
        "bmd,bsd->bms", normed3, grad_slot_in, preferred_element_type=jnp.float32
    )
    grad_logits32 = combine32 * (
        grad_combine - jnp.sum(combine32 * grad_combine, axis=2, keepdims=True)
    )
    grad_logits32 = grad_logits32 + dispatch32 * (
        grad_dispatch - jnp.sum(dispatch32 * grad_dispatch, axis=1, keepdims=True)
    )
    grad_logits = grad_logits32.astype(jnp.bfloat16).reshape(rows, -1)
    grad_normed = jnp.einsum(
        "bms,bsd->bmd", dispatch, grad_slot_in, preferred_element_type=jnp.float32
    ).reshape(rows, width)
    grad_normed = grad_normed + factor * jnp.dot(
        grad_logits, unit.T, preferred_element_type=jnp.float32
    )
    local_unit = factor * jnp.dot(normed.T, grad_logits, preferred_element_type=jnp.float32)
    grad_unit = lax.psum(local_unit, IMG_EXP)
    grad_slots = (
        grad_unit - unit32 * jnp.sum(unit32 * grad_unit, axis=0, keepdims=True)
    ) / slot_norm
    upstream = cotangent.reshape(rows, width).astype(jnp.float32)
    grad_stream = upstream + inverse * (
        grad_normed - normed32 * jnp.mean(normed32 * grad_normed, axis=-1, keepdims=True)
    )
    grad_residual = grad_stream.astype(jnp.bfloat16)
    grad_context = jnp.dot(
        grad_residual, gather_directly(proj_weight, IMG, 0).T, preferred_element_type=jnp.float32
    ).astype(jnp.bfloat16)
    columns = flat_ctx
    owned = sum_in_two_steps(
        jnp.dot(columns.T, grad_residual, preferred_element_type=jnp.float32).astype(jnp.bfloat16),
        ("img_0", "img_1"),
        0,
    )
    grad_proj = nested_sum(owned.astype(jnp.bfloat16), "exp")
    return (
        grad_context.reshape(images, tokens, width),
        grad_residual.reshape(images, tokens, width),
        grad_proj,
        grad_slots,
        grad_expert_in,
        grad_expert_out,
    )


def solution(mesh):
    torus = Mesh(mesh.devices.reshape(2, 2, mesh.shape["exp"]), ("img_0", "img_1", "exp"))
    placed = (
        P(IMG_EXP, None, None),
        P(IMG_EXP, None, None),
        P(IMG_EXP, None, None),
        P(IMG, None),
        P(),
        P("exp", None, IMG),
        P("exp", IMG, None),
    )
    return jax.shard_map(
        shards,
        mesh=torus,
        in_specs=placed,
        out_specs=(
            P(IMG_EXP, None, None),
            P(IMG_EXP, None, None),
            P(IMG, None),
            P(),
            P("exp", None, IMG),
            P("exp", IMG, None),
        ),
        check_vma=False,
    )
```

profile of v0, /device:TPU:0, one launch (start us, length us, event | category | flops | bytes accessed | tf_op | source)
XLA Modules:
  0.0 416.6 jit_solution(16925801770048762867)
XLA Ops:
  13.8 25.5 %all-to-all-done = bf16[4,256,1024]{2,1,0:T(8,128)(2,1)S(1)} async-done(((bf16[4,256,1024]{2,1,0:T(8,128)(2,1)}), bf16[4,256,1024]{2,1,0:T(8,128)(2,1)S(1)}, u32[]{:S(2)}, u32[]{:S(2)}) %all-to-all-start) | async-done | bytes 2097184 | tf_op jit(solution)/shard_map/all_to_all | solution.py:19
  47.6 10.9 %all-to-all-start.3 = ((bf16[2,64,1024]{2,0,1:T(2,128)(2,1)}), bf16[2,64,1024]{2,0,1:T(2,128)(2,1)}, u32[]{:S(2)}, u32[]{:S(2)}) async-start(bf16[2,64,1024]{2,0,1:T(2,128)(2,1)} %copy.81), calls=%async_computation.3 | async-start | bytes 524288 | tf_op jit(solution)/shard_map/all_to_all | solution.py:101
  61.0 8.1 %all-to-all-done.3 = bf16[2,64,1024]{2,0,1:T(2,128)(2,1)} async-done(((bf16[2,64,1024]{2,0,1:T(2,128)(2,1)}), bf16[2,64,1024]{2,0,1:T(2,128)(2,1)}, u32[]{:S(2)}, u32[]{:S(2)}) %all-to-all-start.3) | async-done | bytes 262176 | tf_op jit(solution)/shard_map/all_to_all | solution.py:101
  69.2 4.6 %all-to-all-start.1 = ((bf16[2,64,1024]{2,0,1:T(2,128)(2,1)}), bf16[2,64,1024]{2,0,1:T(2,128)(2,1)}, u32[]{:S(2)}, u32[]{:S(2)}) async-start(bf16[2,64,1024]{2,0,1:T(2,128)(2,1)} %copy.77), calls=%async_computation.1 | async-start | bytes 524288 | tf_op jit(solution)/shard_map/all_to_all | solution.py:119
  75.7 8.7 %all-to-all-done.1 = bf16[2,64,1024]{2,0,1:T(2,128)(2,1)} async-done(((bf16[2,64,1024]{2,0,1:T(2,128)(2,1)}), bf16[2,64,1024]{2,0,1:T(2,128)(2,1)}, u32[]{:S(2)}, u32[]{:S(2)}) %all-to-all-start.1) | async-done | bytes 262176 | tf_op jit(solution)/shard_map/all_to_all | solution.py:119
  92.6 12.6 %all-to-all-done.4 = bf16[4,64,2,1024]{3,1,2,0:T(8,128)(2,1)} async-done(((bf16[4,64,2,1024]{3,1,2,0:T(8,128)(2,1)}), bf16[4,64,2,1024]{3,1,2,0:T(8,128)(2,1)}, u32[]{:S(2)}, u32[]{:S(2)}) %all-to-all-start.4) | async-done | bytes 1048608 | tf_op jit(solution)/shard_map/all_to_all | solution.py:19
  113.8 4.8 %fusion.45 = f32[2,256,1024]{2,1,0:T(8,128)} fusion(bf16[256,2,1024]{2,0,1:T(8,128)(2,1)S(1)} %bitcast.141, bf16[2,1024,1024]{2,1,0:T(8,128)(2,1)} %param.12), kind=kOutput, calls=%fused_computation.75 | convolution fusion | flops 1073741824 | bytes 7340032 | tf_op jit(solution)/shard_map/gjd,jdf->gjf/dot_general | solution.py:103
  118.6 7.4 %all-to-all-done.2 = bf16[4,64,2,1024]{3,1,2,0:T(8,128)(2,1)} async-done(((bf16[4,64,2,1024]{3,1,2,0:T(8,128)(2,1)}), bf16[4,64,2,1024]{3,1,2,0:T(8,128)(2,1)}, u32[]{:S(2)}, u32[]{:S(2)}) %all-to-all-start.2) | async-done | bytes 1048608 | tf_op jit(solution)/shard_map/all_to_all | solution.py:19
  127.9 4.7 %fusion.17 = bf16[256,2,1024]{2,0,1:T(8,128)(2,1)S(1)} fusion(f32[2,256,1024]{2,1,0:T(8,128)S(1)} %copy-done.5, bf16[256,2,1024]{2,0,1:T(8,128)(2,1)S(1)} %bitcast.153, bf16[2,1024,1024]{2,1,0:T(8,128)(2,1)} %param.13), kind=kOutput, calls=%fused_computation.23 | convolution fusion | flops 1084227584 | bytes 8388608 | tf_op jit(solution)/shard_map/gjd,jfd->gjf/dot_general | solution.py:124
  144.6 9.2 %all-to-all-done.5 = bf16[4,64,2,1024]{3,1,2,0:T(8,128)(2,1)} async-done(((bf16[4,64,2,1024]{3,1,2,0:T(8,128)(2,1)}), bf16[4,64,2,1024]{3,1,2,0:T(8,128)(2,1)}, u32[]{:S(2)}, u32[]{:S(2)}) %all-to-all-start.5) | async-done | bytes 1048608 | tf_op jit(solution)/shard_map/all_to_all | solution.py:42
  153.8 4.4 %all-to-all-start.7 = ((bf16[4,64,2,1024]{3,1,2,0:T(8,128)(2,1)}), bf16[4,64,2,1024]{3,1,2,0:T(8,128)(2,1)}, u32[]{:S(2)}, u32[]{:S(2)}) async-start(bf16[4,64,2,1024]{3,1,2,0:T(8,128)(2,1)} %copy.89), calls=%async_computation.7 | async-start | bytes 2097152 | tf_op jit(solution)/shard_map/all_to_all | solution.py:42
  162.4 10.2 %all-to-all-done.7 = bf16[4,64,2,1024]{3,1,2,0:T(8,128)(2,1)} async-done(((bf16[4,64,2,1024]{3,1,2,0:T(8,128)(2,1)}), bf16[4,64,2,1024]{3,1,2,0:T(8,128)(2,1)}, u32[]{:S(2)}, u32[]{:S(2)}) %all-to-all-start.7) | async-done | bytes 1048608 | tf_op jit(solution)/shard_map/all_to_all | solution.py:42
  172.6 4.6 %all-to-all-start.6 = ((bf16[64,2,1024]{2,1,0:T(2,128)(2,1)}), bf16[64,2,1024]{2,1,0:T(2,128)(2,1)}, u32[]{:S(2)}, u32[]{:S(2)}) async-start(bf16[64,2,1024]{2,1,0:T(2,128)(2,1)} %copy.87), calls=%async_computation.6 | async-start | bytes 524288 | tf_op jit(solution)/shard_map/all_to_all | solution.py:142
  181.3 6.8 %all-to-all-done.6 = bf16[64,2,1024]{2,1,0:T(2,128)(2,1)} async-done(((bf16[64,2,1024]{2,1,0:T(2,128)(2,1)}), bf16[64,2,1024]{2,1,0:T(2,128)(2,1)}, u32[]{:S(2)}, u32[]{:S(2)}) %all-to-all-start.6) | async-done | bytes 262176 | tf_op jit(solution)/shard_map/all_to_all | solution.py:142
  188.1 4.6 %all-to-all-start.8 = ((bf16[64,2,1024]{2,1,0:T(2,128)(2,1)}), bf16[64,2,1024]{2,1,0:T(2,128)(2,1)}, u32[]{:S(2)}, u32[]{:S(2)}) async-start(bf16[64,2,1024]{2,1,0:T(2,128)(2,1)} %copy.91), calls=%async_computation.8 | async-start | bytes 524288 | tf_op jit(solution)/shard_map/all_to_all | solution.py:113
  196.2 7.1 %all-to-all-done.8 = bf16[64,2,1024]{2,1,0:T(2,128)(2,1)} async-done(((bf16[64,2,1024]{2,1,0:T(2,128)(2,1)}), bf16[64,2,1024]{2,1,0:T(2,128)(2,1)}, u32[]{:S(2)}, u32[]{:S(2)}) %all-to-all-start.8) | async-done | bytes 262176 | tf_op jit(solution)/shard_map/all_to_all | solution.py:113
  217.7 6.3 %all_to_all.112 = bf16[2,2,256,1024]{3,2,1,0:T(8,128)(2,1)} all-to-all(bf16[2,2,256,1024]{3,2,1,0:T(8,128)(2,1)S(1)} %bitcast.143), channel_id=1, replica_groups=mesh['img_0'=2,'img_1'=2,'exp'=32] {'img_1'}, dimensions={0} | all-to-all | bytes 4194304 | tf_op jit(solution)/shard_map/all_to_all | solution.py:42
  227.4 4.4 %all-to-all-start.10 = ((bf16[2,256,1024]{2,1,0:T(8,128)(2,1)}), bf16[2,256,1024]{2,1,0:T(8,128)(2,1)}, u32[]{:S(2)}, u32[]{:S(2)}) async-start(bf16[2,256,1024]{2,1,0:T(8,128)(2,1)} %reduce_sum.141), calls=%async_computation.10 | async-start | bytes 2097152 | tf_op jit(solution)/shard_map/all_to_all | solution.py:50
  231.8 5.1 %convolution_convert_fusion = bf16[2,1024,1024]{2,1,0:T(8,128)(2,1)} fusion(bf16[256,2,1024]{2,0,1:T(8,128)(2,1)S(1)} %bitcast.154, f32[2,256,1024]{2,1,0:T(8,128)} %fusion.45), kind=kOutput, calls=%fused_computation.4 | convolution fusion | flops 1080557568 | bytes 7340032 | tf_op jit(solution)/shard_map/gjf,gjd->jfd/dot_general | solution.py:128
  236.9 9.1 %all-to-all-done.10 = bf16[2,256,1024]{2,1,0:T(8,128)(2,1)} async-done(((bf16[2,256,1024]{2,1,0:T(8,128)(2,1)}), bf16[2,256,1024]{2,1,0:T(8,128)(2,1)}, u32[]{:S(2)}, u32[]{:S(2)}) %all-to-all-start.10) | async-done | bytes 1048608 | tf_op jit(solution)/shard_map/all_to_all | solution.py:50
  248.4 4.6 %all-to-all-start.11 = ((bf16[32,8,1024]{2,1,0:T(8,128)(2,1)}), bf16[32,8,1024]{2,1,0:T(8,128)(2,1)}, u32[]{:S(2)}, u32[]{:S(2)}) async-start(bf16[32,8,1024]{2,1,0:T(8,128)(2,1)} %bitcast.147), calls=%async_computation.11 | async-start | bytes 1048576 | tf_op jit(solution)/shard_map/all_to_all | solution.py:42
  253.1 4.5 %convolution_convert_fusion.1 = bf16[2,1024,1024]{2,1,0:T(8,128)(2,1)} fusion(bf16[256,2,1024]{2,0,1:T(8,128)(2,1)S(1)} %bitcast.142, bf16[256,2,1024]{2,0,1:T(8,128)(2,1)} %copy-done.11), kind=kOutput, calls=%fused_computation.5 | convolution fusion | flops 1075838976 | bytes 6291456 | tf_op jit(solution)/shard_map/gjd,gjf->jdf/dot_general | solution.py:131
  258.7 7.6 %all-to-all-done.11 = bf16[32,8,1024]{2,1,0:T(8,128)(2,1)} async-done(((bf16[32,8,1024]{2,1,0:T(8,128)(2,1)}), bf16[32,8,1024]{2,1,0:T(8,128)(2,1)}, u32[]{:S(2)}, u32[]{:S(2)}) %all-to-all-start.11) | async-done | bytes 524320 | tf_op jit(solution)/shard_map/all_to_all | solution.py:42
  276.1 129.7 %all-reduce.2.cloned.1.call-done = f32[1024,64]{0,1:T(8,128)} async-done(((f32[1024,64]{0,1:T(8,128)}), f32[1024,64]{0,1:T(8,128)}) %all-reduce.2.cloned.1.call-update) | async-done | bytes 262160 | tf_op jit(solution)/shard_map/psum | solution.py:162
  (90 shorter events, 96.6 us)
Async XLA Ops:
  7.2 32.1 %copy-start = (bf16[2,256,1024]{2,1,0:T(8,128)(2,1)S(1)}, bf16[2,256,1024]{2,1,0:T(8,128)(2,1)}, u32[]{:S(2)}) copy-start(bf16[2,256,1024]{2,1,0:T(8,128)(2,1)} %param.7) | copy-start | bytes 3145732
  9.9 3.8 copy-start.6
  9.9 29.4 %all-to-all-start = ((bf16[4,256,1024]{2,1,0:T(8,128)(2,1)}), bf16[4,256,1024]{2,1,0:T(8,128)(2,1)S(1)}, u32[]{:S(2)}, u32[]{:S(2)}) async-start(bf16[4,256,1024]{2,1,0:T(8,128)(2,1)} %broadcast_in_dim.12), calls=%async_computation | async-start | bytes 4194304 | tf_op jit(solution)/shard_map/all_to_all | solution.py:19
  39.3 1.3 copy-start.7
  47.6 21.5 %all-to-all-start.3 = ((bf16[2,64,1024]{2,0,1:T(2,128)(2,1)}), bf16[2,64,1024]{2,0,1:T(2,128)(2,1)}, u32[]{:S(2)}, u32[]{:S(2)}) async-start(bf16[2,64,1024]{2,0,1:T(2,128)(2,1)} %copy.81), calls=%async_computation.3 | async-start | bytes 524288 | tf_op jit(solution)/shard_map/all_to_all | solution.py:101
  69.2 15.2 %all-to-all-start.1 = ((bf16[2,64,1024]{2,0,1:T(2,128)(2,1)}), bf16[2,64,1024]{2,0,1:T(2,128)(2,1)}, u32[]{:S(2)}, u32[]{:S(2)}) async-start(bf16[2,64,1024]{2,0,1:T(2,128)(2,1)} %copy.77), calls=%async_computation.1 | async-start | bytes 524288 | tf_op jit(solution)/shard_map/all_to_all | solution.py:119
  86.4 18.7 %all-to-all-start.4 = ((bf16[4,64,2,1024]{3,1,2,0:T(8,128)(2,1)}), bf16[4,64,2,1024]{3,1,2,0:T(8,128)(2,1)}, u32[]{:S(2)}, u32[]{:S(2)}) async-start(bf16[4,64,2,1024]{3,1,2,0:T(8,128)(2,1)} %broadcast_in_dim.16), calls=%async_computation.4 | async-start | bytes 2097152 | tf_op jit(solution)/shard_map/all_to_all | solution.py:19
  107.2 18.8 %all-to-all-start.2 = ((bf16[4,64,2,1024]{3,1,2,0:T(8,128)(2,1)}), bf16[4,64,2,1024]{3,1,2,0:T(8,128)(2,1)}, u32[]{:S(2)}, u32[]{:S(2)}) async-start(bf16[4,64,2,1024]{3,1,2,0:T(8,128)(2,1)} %broadcast_in_dim.14), calls=%async_computation.2 | async-start | bytes 2097152 | tf_op jit(solution)/shard_map/all_to_all | solution.py:19
  126.0 1.9 copy-start.5
  127.5 5.2 %copy-start.9 = (bf16[4,64,2,1024]{3,1,0,2:T(8,128)(2,1)}, bf16[4,64,2,1024]{3,1,0,2:T(8,128)(2,1)S(1)}, u32[]{:S(2)}) copy-start(bf16[4,64,2,1024]{3,1,0,2:T(8,128)(2,1)S(1)} %copy.80) | copy-start | bytes 3145732
  127.9 4.8 %copy-start.4 = (bf16[2,1024,1024]{2,1,0:T(8,128)(2,1)S(1)}, bf16[2,1024,1024]{2,1,0:T(8,128)(2,1)}, u32[]{:S(2)}) copy-start(bf16[2,1024,1024]{2,1,0:T(8,128)(2,1)} %param.12) | copy-start | bytes 12582916
  135.0 18.7 %all-to-all-start.5 = ((bf16[4,64,2,1024]{3,1,2,0:T(8,128)(2,1)}), bf16[4,64,2,1024]{3,1,2,0:T(8,128)(2,1)}, u32[]{:S(2)}, u32[]{:S(2)}) async-start(bf16[4,64,2,1024]{3,1,2,0:T(8,128)(2,1)} %copy.85), calls=%async_computation.5 | async-start | bytes 2097152 | tf_op jit(solution)/shard_map/all_to_all | solution.py:42
  153.8 18.8 %all-to-all-start.7 = ((bf16[4,64,2,1024]{3,1,2,0:T(8,128)(2,1)}), bf16[4,64,2,1024]{3,1,2,0:T(8,128)(2,1)}, u32[]{:S(2)}, u32[]{:S(2)}) async-start(bf16[4,64,2,1024]{3,1,2,0:T(8,128)(2,1)} %copy.89), calls=%async_computation.7 | async-start | bytes 2097152 | tf_op jit(solution)/shard_map/all_to_all | solution.py:42
  172.6 15.5 %all-to-all-start.6 = ((bf16[64,2,1024]{2,1,0:T(2,128)(2,1)}), bf16[64,2,1024]{2,1,0:T(2,128)(2,1)}, u32[]{:S(2)}, u32[]{:S(2)}) async-start(bf16[64,2,1024]{2,1,0:T(2,128)(2,1)} %copy.87), calls=%async_computation.6 | async-start | bytes 524288 | tf_op jit(solution)/shard_map/all_to_all | solution.py:142
  188.1 15.2 %all-to-all-start.8 = ((bf16[64,2,1024]{2,1,0:T(2,128)(2,1)}), bf16[64,2,1024]{2,1,0:T(2,128)(2,1)}, u32[]{:S(2)}, u32[]{:S(2)}) async-start(bf16[64,2,1024]{2,1,0:T(2,128)(2,1)} %copy.91), calls=%async_computation.8 | async-start | bytes 524288 | tf_op jit(solution)/shard_map/all_to_all | solution.py:113
  206.9 2.5 copy-start.8
  213.1 2.4 copy-start.3
  224.0 7.8 %copy-start.10 = (bf16[4,64,2,1024]{3,1,0,2:T(8,128)(2,1)S(1)}, bf16[4,64,2,1024]{3,1,0,2:T(8,128)(2,1)}, u32[]{:S(2)}) copy-start(bf16[4,64,2,1024]{3,1,0,2:T(8,128)(2,1)} %copy-done.9) | copy-start | bytes 3145732
  227.4 18.7 %all-to-all-start.10 = ((bf16[2,256,1024]{2,1,0:T(8,128)(2,1)}), bf16[2,256,1024]{2,1,0:T(8,128)(2,1)}, u32[]{:S(2)}, u32[]{:S(2)}) async-start(bf16[2,256,1024]{2,1,0:T(8,128)(2,1)} %reduce_sum.141), calls=%async_computation.10 | async-start | bytes 2097152 | tf_op jit(solution)/shard_map/all_to_all | solution.py:50
  236.9 16.2 %copy-start.2 = (bf16[4,64,2,1024]{3,1,0,2:T(8,128)(2,1)S(1)}, bf16[4,64,2,1024]{3,1,0,2:T(8,128)(2,1)}, u32[]{:S(2)}) copy-start(bf16[4,64,2,1024]{3,1,0,2:T(8,128)(2,1)} %copy-done.1) | copy-start | bytes 3145732
  248.4 17.9 %all-to-all-start.11 = ((bf16[32,8,1024]{2,1,0:T(8,128)(2,1)}), bf16[32,8,1024]{2,1,0:T(8,128)(2,1)}, u32[]{:S(2)}, u32[]{:S(2)}) async-start(bf16[32,8,1024]{2,1,0:T(8,128)(2,1)} %bitcast.147), calls=%async_computation.11 | async-start | bytes 1048576 | tf_op jit(solution)/shard_map/all_to_all | solution.py:42
  253.1 152.7 %all-reduce.2.cloned.1.call-start = ((), (), s32[]{:S(2)}) async-start(), calls=%async_computation.13 | async-start | bytes 524288 | tf_op jit(solution)/shard_map/psum | solution.py:162
  257.7 14.5 %copy-start.13 = (bf16[512,1024]{1,0:T(8,128)(2,1)S(1)}, bf16[512,1024]{1,0:T(8,128)(2,1)}, u32[]{:S(2)}) copy-start(bf16[512,1024]{1,0:T(8,128)(2,1)} %copy-done.12) | copy-start | bytes 3145732
  268.3 140.4 %all-to-all-start.12 = ((bf16[32,8,1024]{2,1,0:T(8,128)(2,1)}), bf16[32,8,1024]{2,1,0:T(8,128)(2,1)S(1)}, u32[]{:S(2)}, u32[]{:S(2)}) async-start(bf16[32,8,1024]{2,1,0:T(8,128)(2,1)} %broadcast_in_dim.17), calls=%async_computation.12 | async-start | bytes 1048576 | tf_op jit(solution)/shard_map/all_to_all | solution.py:19
  (3 other events, 3.6 us)
Sparse Core Ops, SparseCore 0:
  259.2 146.4 all-reduce.1
where the time goes:
time: 419 us; the launch traced here: 417 us
  waiting for transfers between devices  242 us (58%)
  starting transfers between devices  58.5 us (14%)
  matrix products  44.4 us (11%)
  local copies, waits for them, and re-layouts  33.2 us (8%)
  other arithmetic  17.8 us (4%)
  between operations  14.4 us (3%)
  blocking collectives  6.32 us (2%)
    psum x1, waiting for transfers between devices, shards(): grad_unit = lax.psum(local_unit, IMG_EXP)  130 us
    all_to_all x4, waiting for transfers between devices, copy_for_each(): lax.all_to_all(jnp.broadcast_to(shard[None], (devices, *shard.shape)), ax...  45.5 us
    all_to_all x3, waiting for transfers between devices, summed_on_arrival(): lax.all_to_all(split_up(shard, dim, devices), axis, 0, 0, tiled=True)  27 us
    all_to_all x4, starting transfers between devices, copy_for_each(): lax.all_to_all(jnp.broadcast_to(shard[None], (devices, *shard.shape)), ax...  16.1 us
    all_to_all x3, starting transfers between devices, summed_on_arrival(): lax.all_to_all(split_up(shard, dim, devices), axis, 0, 0, tiled=True)  13.3 us
    all_to_all x1, starting transfers between devices, shards(): lax.all_to_all(slot_in, 'exp', split_axis=1, concat_axis=0, tiled=True)  10.9 us
    broadcast_in_dim x6, local copies, waits for them, and re-layouts, copy_for_each(): jnp.broadcast_to(shard[None], (devices, *shard.shape))  9.18 us
    all_to_all x1, waiting for transfers between devices, sum_in_two_steps(): lax.all_to_all(own.astype(jnp.bfloat16), far, 0, 0, tiled=True)  9.11 us
  transfers between devices with their start and end apart: 13, of which 12 were waited for; matrix products, arithmetic and copies ran while one was open for 11% of the time, Pallas kernels for 0%

commit v1 on v0

v1 whole, which is shorter than its diff:
```python
import math

import jax
import jax.numpy as jnp
from jax import lax
from jax.experimental import pallas as pl
from jax.experimental.pallas import tpu as pltpu
from jax.sharding import Mesh
from jax.sharding import PartitionSpec as P

AXES = ("zl", "core", "x", "y", "zh")
IMG = ("zl", "core")
EXP = ("x", "y", "zh")
IMG_EXP = IMG + EXP
MESH = pl.DeviceIdType.MESH
VMEM = pltpu.VMEM
BF16 = jnp.bfloat16
F32 = jnp.float32


logit_scale = 48.0
epsilon = 1e-06


def place():
    zl, core, x, y, zh = (lax.axis_index(a) for a in AXES)
    return 2 * zh + zl, core, 4 * x + y


def flip(bit):
    return 1 - bit


def mate(z):
    return z + 1 - 2 * lax.rem(z, 2)


def cross(z):
    return 3 - z


def far(z):
    return lax.rem(z + 2, 4)


def at_z(z):
    return {"zl": lax.rem(z, 2), "zh": lax.div(z, 2)}


def at_core(core):
    return {"core": core}


def at_xy(k):
    return {"x": lax.div(k, 4), "y": lax.rem(k, 4)}


def remote(src, dst, send, recv, device):
    return pltpu.make_async_remote_copy(
        src_ref=src, dst_ref=dst, send_sem=send, recv_sem=recv, device_id=device, device_id_type=MESH
    )


def greet(devices, xy=None):
    barrier = pltpu.get_barrier_semaphore()
    for device in devices:
        pl.semaphore_signal(barrier, inc=1, device_id=device, device_id_type=MESH)
    count = len(devices)
    if xy is not None:

        def one(d, carry):
            pl.semaphore_signal(
                barrier, inc=1, device_id=at_xy(lax.rem(xy + d, 16)), device_id_type=MESH
            )
            return carry

        lax.fori_loop(1, 16, one, 0)
        count += 15
    pl.semaphore_wait(barrier, count)


def xy_copy(d, xy, src, dst, send, recv):
    k = lax.rem(xy + d, 16)
    return remote(src(k), dst(xy), send.at[d], recv.at[d], at_xy(k))


def xy_start(*args):
    def one(d, carry):
        xy_copy(d, *args).start()
        return carry

    lax.fori_loop(1, 16, one, 0)


def xy_wait(*args):
    def one(d, carry):
        xy_copy(d, *args).wait()
        return carry

    lax.fori_loop(1, 16, one, 0)


def rows8(ref, kind, k):
    return ref.at[kind, pl.ds(pl.multiple_of(8 * k, 8), 8)]


def one_hot(wanted):
    rows = lax.broadcasted_iota(jnp.int32, (128, 128), 0)
    columns = lax.broadcasted_iota(jnp.int32, (128, 128), 1)
    return (columns == wanted(rows)).astype(F32).astype(BF16)


def bits(value, low, count):
    return lax.rem(lax.div(value, 2**low), 2**count)


def to_pairs(r):
    return bits(r, 0, 1) * 64 + bits(r, 1, 6)


def from_pairs(r):
    return bits(r, 0, 6) * 2 + bits(r, 6, 1)


def to_blocks(r):
    return bits(r, 1, 4) * 8 + bits(r, 6, 1) * 4 + bits(r, 5, 1) * 2 + bits(r, 0, 1)


def from_blocks(r):
    return bits(r, 2, 1) * 64 + bits(r, 1, 1) * 32 + bits(r, 3, 4) * 2 + bits(r, 0, 1)


def reorder(wanted, rows):
    return jnp.dot(one_hot(wanted), rows, preferred_element_type=F32).astype(BF16)


def params(number, limit=None):
    return pltpu.CompilerParams(
        collective_id=number, has_side_effects=True, vmem_limit_bytes=limit or (40 << 20)
    )


def weight_kernel(own, out, s_sem, r_sem):
    z, core, _ = place()
    block = 2 * lax.rem(z, 2) + core
    other = 2 * flip(lax.rem(z, 2)) + core
    half = own.shape[0] // 2

    def rows(blk, start, size):
        return out.at[pl.ds(pl.multiple_of(blk * 2 * half + start, half), size)]

    partner = at_core(flip(core))
    greet([at_z(mate(z)), at_z(cross(z)), partner])
    to_mate = remote(own.at[pl.ds(0, half)], rows(block, 0, half), s_sem.at[0], r_sem.at[0], at_z(mate(z)))
    to_cross = remote(
        own.at[pl.ds(half, half)], rows(block, half, half), s_sem.at[1], r_sem.at[1], at_z(cross(z))
    )
    to_core = remote(own, rows(block, 0, 2 * half), s_sem.at[2], r_sem.at[2], partner)
    to_mate.start()
    to_cross.start()
    to_core.start()
    mine = pltpu.make_async_copy(own, rows(block, 0, 2 * half), s_sem.at[5])
    mine.start()
    first = remote(rows(other, 0, half), rows(other, 0, half), s_sem.at[3], r_sem.at[3], partner)
    second = remote(rows(other, half, half), rows(other, half, half), s_sem.at[4], r_sem.at[4], partner)
    to_mate.wait_recv()
    first.start()
    to_cross.wait_recv()
    second.start()
    mine.wait()
    to_mate.wait_send()
    to_cross.wait_send()
    to_core.wait()
    first.wait()
    second.wait()


def whole_weight(own):
    rows, width = own.shape
    return pl.pallas_call(
        weight_kernel,
        out_shape=jax.ShapeDtypeStruct((4 * rows, width), own.dtype),
        in_specs=[pl.BlockSpec(memory_space=VMEM)],
        out_specs=pl.BlockSpec(memory_space=VMEM),
        scratch_shapes=[pltpu.SemaphoreType.DMA((6,)), pltpu.SemaphoreType.DMA((5,))],
        compiler_params=params(1),
        name="whole_weight",
    )(own)


def out_kernel(a_ref, b_ref, x_ref, pairs, came, blocks, s1, r1, s2, r2):
    z, core, xy = place()
    zh = lax.div(z, 2)
    partner = at_core(flip(core))
    greet([at_z(mate(z)), at_z(cross(z)), partner], xy)

    def swap(kind):
        return (
            xy,
            lambda k: rows8(pairs, kind, k),
            lambda k: rows8(came, kind, k),
            s1.at[kind],
            r1.at[kind],
        )

    def keep(kind):
        return pltpu.make_async_copy(
            rows8(pairs, kind, xy), rows8(came, kind, xy), s1.at[kind, 0]
        )

    for kind, ref in enumerate((a_ref, b_ref)):
        pairs[kind] = reorder(to_pairs, ref[...])
        keep(kind).start()
        xy_start(*swap(kind))

    def there(kind, zz):
        return x_ref.at[kind, :, zz, core]

    def send(kind, number, src, zz, device):
        return remote(src, there(kind, zz), s2.at[kind, number], r2.at[kind, number], device)

    def firsts(kind):
        return (
            send(kind, 0, blocks.at[kind, zh], z, at_z(mate(z))),
            send(kind, 1, blocks.at[kind, flip(zh)], z, at_z(cross(z))),
            send(kind, 3, blocks.at[kind, zh], z, partner),
        )

    def passed(kind):
        c, m, f = cross(z), mate(z), far(z)
        return (
            send(kind, 2, there(kind, c), c, at_z(m)),
            send(kind, 4, there(kind, c), c, partner),
            send(kind, 5, there(kind, m), m, partner),
            send(kind, 6, there(kind, f), f, partner),
        )

    def mine(kind):
        return pltpu.make_async_copy(blocks.at[kind, zh], there(kind, z), s2.at[kind, 7])

    for kind in range(2):
        keep(kind).wait()
        xy_wait(*swap(kind))
        ordered = reorder(to_blocks, came[kind])
        for i in range(2):
            for e in range(2):
                blocks[kind, i, e] = ordered[i * 64 + e * 32 : i * 64 + e * 32 + 32]
        for copy in firsts(kind):
            copy.start()
        mine(kind).start()
    for kind in range(2):
        to_mate, to_cross, to_core = firsts(kind)
        on_mate, on_core_c, on_core_m, on_core_f = passed(kind)
        to_cross.wait_recv()
        on_mate.start()
        on_core_c.start()
        to_mate.wait_recv()
        on_core_m.start()
        on_mate.wait_recv()
        on_core_f.start()
    for kind in range(2):
        to_mate, to_cross, to_core = firsts(kind)
        on_mate, on_core_c, on_core_m, on_core_f = passed(kind)
        mine(kind).wait()
        to_mate.wait_send()
        to_cross.wait_send()
        on_mate.wait_send()
        to_core.wait()
        on_core_c.wait()
        on_core_m.wait()
        on_core_f.wait()


def to_experts(first, second):
    width = first.shape[-1]
    return pl.pallas_call(
        out_kernel,
        out_shape=jax.ShapeDtypeStruct((2, 2, 4, 2, 32, width), BF16),
        in_specs=[pl.BlockSpec(memory_space=VMEM)] * 2,
        out_specs=pl.BlockSpec(memory_space=VMEM),
        scratch_shapes=[
            VMEM((2, 128, width), BF16),
            VMEM((2, 128, width), BF16),
            VMEM((2, 2, 2, 32, width), BF16),
            pltpu.SemaphoreType.DMA((2, 16)),
            pltpu.SemaphoreType.DMA((2, 16)),
            pltpu.SemaphoreType.DMA((2, 8)),
            pltpu.SemaphoreType.DMA((2, 8)),
        ],
        compiler_params=params(2),
        name="to_experts",
    )(first, second)


def back_kernel(
    o0, o1, out, halves, chip, paired, crossing, blocks, pairs, came, sa, ra, sb, rb, sc, rc
):
    z, core, xy = place()
    zh = lax.div(z, 2)
    partner = at_core(flip(core))
    greet([at_z(mate(z)), at_z(cross(z)), partner], xy)
    parts = (o0, o1)

    def to_core(kind):
        return remote(
            parts[kind].at[:, :, flip(core)], halves.at[kind], sa.at[kind], ra.at[kind], partner
        )

    def to_mate(kind):
        m = mate(z)
        return [
            remote(chip.at[kind, zz], paired.at[kind, i], sb.at[kind, i], rb.at[kind, i], at_z(m))
            for i, zz in enumerate((far(z), m))
        ]

    def to_cross(kind):
        return remote(
            crossing.at[kind], blocks.at[kind, zh], sb.at[kind, 2], rb.at[kind, 2], at_z(cross(z))
        )

    def swap(kind):
        return (
            xy,
            lambda k: rows8(pairs, kind, k),
            lambda k: rows8(came, kind, k),
            sc.at[kind],
            rc.at[kind],
        )

    def keep(kind):
        return pltpu.make_async_copy(
            rows8(pairs, kind, xy), rows8(came, kind, xy), sc.at[kind, 0]
        )

    for kind in range(2):
        to_core(kind).start()
    for kind in range(2):
        to_core(kind).wait()
        for e in range(2):
            for zz in range(4):
                chip[kind, zz, e] = (
                    parts[kind][e, zz, core].astype(F32) + halves[kind, e, zz].astype(F32)
                ).astype(BF16)
        for copy in to_mate(kind):
            copy.start()
    for kind in range(2):
        on, own = to_mate(kind)
        on.wait_recv()
        for e in range(2):
            crossing[kind, e] = (
                chip[kind, cross(z), e].astype(F32) + paired[kind, 0, e].astype(F32)
            ).astype(BF16)
        to_cross(kind).start()
        own.wait_recv()
        for e in range(2):
            blocks[kind, zh, e] = (
                chip[kind, z, e].astype(F32) + paired[kind, 1, e].astype(F32)
            ).astype(BF16)
    for kind in range(2):
        to_cross(kind).wait_recv()
        rows = jnp.concatenate([blocks[kind, i, e] for i in range(2) for e in range(2)], axis=0)
        pairs[kind] = reorder(from_blocks, rows)
        keep(kind).start()
        xy_start(*swap(kind))
    for kind in range(2):
        keep(kind).wait()
        xy_wait(*swap(kind))
        out[kind] = reorder(from_pairs, came[kind])
    for kind in range(2):
        for copy in to_mate(kind):
            copy.wait_send()
        to_cross(kind).wait_send()


def to_images(first, second):
    width = first.shape[-1]
    return pl.pallas_call(
        back_kernel,
        out_shape=jax.ShapeDtypeStruct((2, 128, width), BF16),
        in_specs=[pl.BlockSpec(memory_space=VMEM)] * 2,
        out_specs=pl.BlockSpec(memory_space=VMEM),
        scratch_shapes=[
            VMEM((2, 2, 4, 32, width), BF16),
            VMEM((2, 4, 2, 32, width), BF16),
            VMEM((2, 2, 2, 32, width), BF16),
            VMEM((2, 2, 32, width), BF16),
            VMEM((2, 2, 2, 32, width), BF16),
            VMEM((2, 128, width), BF16),
            VMEM((2, 128, width), BF16),
            pltpu.SemaphoreType.DMA((2,)),
            pltpu.SemaphoreType.DMA((2,)),
            pltpu.SemaphoreType.DMA((2, 3)),
            pltpu.SemaphoreType.DMA((2, 3)),
            pltpu.SemaphoreType.DMA((2, 16)),
            pltpu.SemaphoreType.DMA((2, 16)),
        ],
        compiler_params=params(3),
        name="to_images",
    )(first, second)


def sum_kernel(
    g, u, out, u_out,
    ga, gq, gb, gh, gc, gt, gf, gv, gall,
    ua, uw, uc, ut, uz, uv, uall, uother,
    sg, rg, su, ru, s1, r1, s2, r2, s3, r3, s4, r4,
):
    z, core, xy = place()
    zl = lax.rem(z, 2)
    partner = at_core(flip(core))
    ring = [at_z(lax.rem(z + d, 4)) for d in range(1, 4)]
    greet([*ring, partner], xy)
    half = g.shape[2] // 2
    width = g.shape[3]
    chunk = 2 * half // 16
    wide = width // 4

    u_core = remote(u.at[flip(core)], ua, su.at[0], ru.at[0], partner)
    g_core = remote(g.at[:, flip(core)], ga, sg.at[0], rg.at[0], partner)
    u_core.start()
    g_core.start()

    u_swap = (xy, lambda k: uw.at[k], lambda k: uc.at[k], s1, r1)
    u_keep = pltpu.make_async_copy(uw.at[xy], uc.at[xy], s1.at[0])
    u_core.wait()
    for i in range(4):
        for j in range(4):
            where = (slice(8 * i, 8 * i + 8), slice(wide * j, wide * j + wide))
            uw[4 * i + j] = u[core, where[0], where[1]] + ua[where[0], where[1]]
    u_keep.start()
    xy_start(*u_swap)

    g_core.wait()
    gq[...] = (g[flip(zl), core].astype(F32) + ga[flip(zl)].astype(F32)).astype(BF16)
    g_mate = remote(
        gq.at[pl.ds(0, half)], gb.at[pl.ds(0, half)], sg.at[1], rg.at[1], at_z(mate(z))
    )
    g_cross = remote(
        gq.at[pl.ds(half, half)], gb.at[pl.ds(half, half)], sg.at[2], rg.at[2], at_z(cross(z))
    )
    g_mate.start()
    g_cross.start()

    u_keep.wait()
    xy_wait(*u_swap)
    ut[...] = jnp.sum(uc[...], axis=0)
    u_ring = [
        remote(ut, uz.at[z], su.at[d + 1], ru.at[d + 1], ring[d]) for d in range(3)
    ]
    u_mine = pltpu.make_async_copy(ut, uz.at[z], su.at[4])
    u_mine.start()
    for copy in u_ring:
        copy.start()

    g_mate.wait()
    g_cross.wait()
    gh[...] = (
        g[zl, core].astype(F32) + ga[zl].astype(F32) + gb[...].astype(F32)
    ).astype(BF16)
    g_swap = (
        xy,
        lambda k: gh.at[pl.ds(pl.multiple_of(chunk * k, chunk), chunk)],
        lambda k: gc.at[k],
        s2,
        r2,
    )
    g_keep = pltpu.make_async_copy(g_swap[1](xy), gc.at[xy], s2.at[0])
    g_keep.start()
    xy_start(*g_swap)

    u_mine.wait()
    for copy in u_ring:
        copy.wait()
    uv[...] = jnp.sum(uz[...], axis=0)
    u_back = (xy, lambda k: uv, lambda k: uall.at[k], s3, r3)
    u_stay = pltpu.make_async_copy(uv, uall.at[xy], s3.at[0])
    u_stay.start()
    xy_start(*u_back)

    g_keep.wait()
    xy_wait(*g_swap)
    total = gc[0].astype(F32)
    for k in range(1, 16):
        total = total + gc[k].astype(F32)
    gt[...] = total.astype(BF16)
    g_far = remote(gt, gf, sg.at[3], rg.at[3], at_z(far(z)))
    g_far.start()

    u_stay.wait()
    xy_wait(*u_back)
    u_other = remote(uall, uother, su.at[5], ru.at[5], partner)
    u_other.start()

    g_far.wait()
    gv[...] = (gt[...].astype(F32) + gf[...].astype(F32)).astype(BF16)
    g_back = (xy, lambda k: gv, lambda k: gall.at[k], s4, r4)
    g_stay = pltpu.make_async_copy(gv, gall.at[xy], s4.at[0])
    g_stay.start()
    xy_start(*g_back)

    u_other.wait()
    for i in range(4):
        for j in range(4):
            columns = slice(wide * j, wide * j + wide)
            rows = slice(8 * i, 8 * i + 8)
            u_out[core, rows, columns] = uall[4 * i + j]
            u_out[flip(core), rows, columns] = uother[4 * i + j]
    g_stay.wait()
    xy_wait(*g_back)
    for k in range(16):
        out[chunk * k : chunk * k + chunk] = gall[k].astype(F32)


def sums(partial, unit_partial):
    width = partial.shape[-1]
    rows = partial.shape[0] // 4
    chunk = rows // 16
    wide = width // 4
    dma = pltpu.SemaphoreType.DMA
    return pl.pallas_call(
        sum_kernel,
        out_shape=(
            jax.ShapeDtypeStruct((rows, width), F32),
            jax.ShapeDtypeStruct((2, 32, width), F32),
        ),
        in_specs=[pl.BlockSpec(memory_space=VMEM)] * 2,
        out_specs=(pl.BlockSpec(memory_space=VMEM), pl.BlockSpec(memory_space=VMEM)),
        scratch_shapes=[
            VMEM((2, rows, width), BF16),
            VMEM((rows, width), BF16),
            VMEM((rows, width), BF16),
            VMEM((rows, width), BF16),
            VMEM((16, chunk, width), BF16),
            VMEM((chunk, width), BF16),
            VMEM((chunk, width), BF16),
            VMEM((chunk, width), BF16),
            VMEM((16, chunk, width), BF16),
            VMEM((32, width), F32),
            VMEM((16, 8, wide), F32),
            VMEM((16, 8, wide), F32),
            VMEM((8, wide), F32),
            VMEM((4, 8, wide), F32),
            VMEM((8, wide), F32),
            VMEM((16, 8, wide), F32),
            VMEM((16, 8, wide), F32),
            dma((4,)),
            dma((4,)),
            dma((6,)),
            dma((6,)),
            *[dma((16,))] * 8,
        ],
        compiler_params=params(4),
        name="sums",
    )(partial.reshape(2, 2, rows, width), unit_partial.reshape(2, 32, width))


def gelu_back(pre, upstream):
    return jax.vjp(jax.nn.gelu, pre)[1](upstream)[0]


def shards(context, residual, cotangent, proj_weight, slot_params, expert_in, expert_out):
    images, tokens, width = context.shape
    rows = images * tokens
    slots = slot_params.shape[1]
    factor = logit_scale / math.sqrt(width)
    flat_ctx = context.reshape(rows, width)
    weight = whole_weight(proj_weight)
    mixed = jnp.dot(flat_ctx, weight, preferred_element_type=jnp.float32)
    stream = (residual.reshape(rows, width).astype(jnp.float32) + mixed).astype(jnp.bfloat16)
    stream32 = stream.astype(jnp.float32)
    inverse = lax.rsqrt(jnp.mean(stream32 * stream32, axis=-1, keepdims=True) + epsilon)
    normed32 = stream32 * inverse
    normed = normed32.astype(jnp.bfloat16)
    params32 = slot_params.astype(jnp.float32)
    slot_norm = jnp.sqrt(jnp.sum(params32 * params32, axis=0, keepdims=True) + epsilon)
    unit32 = params32 / slot_norm
    unit = unit32.astype(jnp.bfloat16)
    logits = factor * jnp.dot(normed, unit, preferred_element_type=jnp.float32)
    logits = logits.reshape(images, tokens, -1)
    expo = jnp.exp(logits)
    dispatch32 = expo / jnp.sum(expo, axis=1, keepdims=True)
    combine32 = expo / jnp.sum(expo, axis=2, keepdims=True)
    dispatch = dispatch32.astype(jnp.bfloat16)
    combine = combine32.astype(jnp.bfloat16)
    normed3 = normed.reshape(images, tokens, width)
    slot_in = jnp.einsum(
        "bms,bmd->bsd", dispatch, normed3, preferred_element_type=jnp.float32
    ).astype(jnp.bfloat16)
    grad_slot_out = jnp.einsum(
        "bms,bmd->bsd", combine, cotangent, preferred_element_type=jnp.float32
    ).astype(jnp.bfloat16)
    arrived = to_experts(
        slot_in.reshape(images * slots, width), grad_slot_out.reshape(images * slots, width)
    ).reshape(2, 2, 256, width)
    slot_rows, grad_rows = arrived[0], arrived[1]
    pre = jnp.einsum("jgd,jdf->jgf", slot_rows, expert_in, preferred_element_type=jnp.float32)
    act = jax.nn.gelu(pre).astype(jnp.bfloat16)
    out_part = jnp.einsum(
        "jgf,jfd->jgd", act, expert_out, preferred_element_type=jnp.float32
    ).astype(jnp.bfloat16)
    grad_act = jnp.einsum(
        "jgd,jfd->jgf", grad_rows, expert_out, preferred_element_type=jnp.float32
    )
    grad_pre = gelu_back(pre, grad_act).astype(jnp.bfloat16)
    grad_part = jnp.einsum(
        "jgf,jdf->jgd", grad_pre, expert_in, preferred_element_type=jnp.float32
    ).astype(jnp.bfloat16)
    returned = to_images(
        out_part.reshape(2, 4, 2, 32, width), grad_part.reshape(2, 4, 2, 32, width)
    ).reshape(2, images, slots, width)
    slot_out, grad_slot_in = returned[0], returned[1]
    grad_expert_out = jnp.einsum(
        "jgf,jgd->jfd", act, grad_rows, preferred_element_type=jnp.float32
    ).astype(jnp.bfloat16)
    grad_expert_in = jnp.einsum(
        "jgd,jgf->jdf", slot_rows, grad_pre, preferred_element_type=jnp.float32
    ).astype(jnp.bfloat16)
    grad_combine = jnp.einsum(
        "bmd,bsd->bms", cotangent, slot_out, preferred_element_type=jnp.float32
    )
    grad_dispatch = jnp.einsum(
        "bmd,bsd->bms", normed3, grad_slot_in, preferred_element_type=jnp.float32
    )
    grad_logits32 = combine32 * (
        grad_combine - jnp.sum(combine32 * grad_combine, axis=2, keepdims=True)
    )
    grad_logits32 = grad_logits32 + dispatch32 * (
        grad_dispatch - jnp.sum(dispatch32 * grad_dispatch, axis=1, keepdims=True)
    )
    grad_logits = grad_logits32.astype(jnp.bfloat16).reshape(rows, -1)
    grad_normed = jnp.einsum(
        "bms,bsd->bmd", dispatch, grad_slot_in, preferred_element_type=jnp.float32
    ).reshape(rows, width)
    grad_normed = grad_normed + factor * jnp.dot(
        grad_logits, unit.T, preferred_element_type=jnp.float32
    )
    local_unit = jnp.dot(grad_logits.T, normed, preferred_element_type=jnp.float32)
    upstream = cotangent.reshape(rows, width).astype(jnp.float32)
    grad_stream = upstream + inverse * (
        grad_normed - normed32 * jnp.mean(normed32 * grad_normed, axis=-1, keepdims=True)
    )
    grad_residual = grad_stream.astype(jnp.bfloat16)
    grad_context = jnp.dot(
        grad_residual, weight.T, preferred_element_type=jnp.float32
    ).astype(jnp.bfloat16)
    partial = jnp.dot(
        flat_ctx.T, grad_residual, preferred_element_type=jnp.float32
    ).astype(jnp.bfloat16)
    grad_proj, unit_sum = sums(partial, local_unit)
    grad_unit = factor * unit_sum.reshape(slots, width).T
    grad_slots = (
        grad_unit - unit32 * jnp.sum(unit32 * grad_unit, axis=0, keepdims=True)
    ) / slot_norm
    return (
        grad_context.reshape(images, tokens, width),
        grad_residual.reshape(images, tokens, width),
        grad_proj,
        grad_slots,
        grad_expert_in,
        grad_expert_out,
    )


def solution(mesh):
    torus = Mesh(mesh.devices.reshape(2, 2, 4, 4, 2), AXES)
    placed = (
        P(IMG_EXP, None, None),
        P(IMG_EXP, None, None),
        P(IMG_EXP, None, None),
        P(IMG, None),
        P(),
        P(EXP, None, IMG),
        P(EXP, IMG, None),
    )
    return jax.shard_map(
        shards,
        mesh=torus,
        in_specs=placed,
        out_specs=(
            P(IMG_EXP, None, None),
            P(IMG_EXP, None, None),
            P(IMG, None),
            P(),
            P(EXP, None, IMG),
            P(EXP, IMG, None),
        ),
        check_vma=False,
    )
```

time: 419 us -> 155 us (0.37)
  waiting for transfers between devices: 242 us -> 0 us
  Pallas kernels: 0 us -> 108 us
  starting transfers between devices: 58.5 us -> 0 us
  local copies, waits for them, and re-layouts: 33.2 us -> 12.2 us
  matrix products: 44.4 us -> 29.5 us
  between operations: 14.4 us -> 0.96 us
  other arithmetic: 17.8 us -> 4.41 us
  blocking collectives: 6.32 us -> 0 us
    psum x1 -> x0, waiting for transfers between devices: 130 us -> none  [shards(): grad_unit = lax.psum(local_unit, IMG_EXP)]
    all_to_all x12 -> x0, waiting for transfers between devices: 112 us -> none  [the longest x4 45.5 us: copy_for_each(): lax.all_to_all(jnp.broadcast_to(shard[None], (devices, *shard.shape)), ax...]
    pallas_call x0 -> x4, Pallas kernels: none -> 108 us  [the longest x1 36.6 us: sums(): pl.pallas_call(sum_kernel, out_shape=(jax.ShapeDtypeStruct((rows, width),...]
    all_to_all x12 -> x0, starting transfers between devices: 58.5 us -> none  [the longest x4 16.1 us: copy_for_each(): lax.all_to_all(jnp.broadcast_to(shard[None], (devices, *shard.shape)), ax...]
    dot_general x10, matrix products: 34.1 us -> 21.7 us  [the longest x1 5.43 us: shards(): jnp.einsum('jgf,jgd->jfd', act, grad_rows, preferred_element_type=jnp.flo...]
    all_to_all x8 -> x0, local copies, waits for them, and re-layouts: 12.2 us -> none  [the longest x2 3.58 us: shards(): lax.all_to_all(grad_summed.astype(jnp.bfloat16), 'exp', split_axis=0, con...]
    reduce_sum x5 -> x0, other arithmetic: 11.3 us -> none  [the longest x4 8.89 us: summed_on_arrival(): return jnp.sum(pieces.astype(jnp.float32), axis=0)]
    broadcast_in_dim x6 -> x0, local copies, waits for them, and re-layouts: 9.18 us -> none  [copy_for_each(): jnp.broadcast_to(shard[None], (devices, *shard.shape))]
  transfers between devices with their start and end apart: 13 -> 0, of which waited for: 12 -> 0; matrix products, arithmetic and copies ran while one was open for 11% -> 0% of each run, Pallas kernels for 0% -> 0%
where the time goes in v1:
time: 155 us
  Pallas kernels  108 us (70%)
  matrix products  29.5 us (19%)
  local copies, waits for them, and re-layouts  12.2 us (8%)
  other arithmetic  4.41 us (3%)
    pallas_call x1, Pallas kernels, sums(): pl.pallas_call(sum_kernel, out_shape=(jax.ShapeDtypeStruct((rows, width),...  36.6 us
    pallas_call x1, Pallas kernels, to_experts(): pl.pallas_call(out_kernel, out_shape=jax.ShapeDtypeStruct((2, 2, 4, 2, 32...  29.8 us
    pallas_call x1, Pallas kernels, to_images(): pl.pallas_call(back_kernel, out_shape=jax.ShapeDtypeStruct((2, 128, width...  28.8 us
    pallas_call x1, Pallas kernels, whole_weight(): pl.pallas_call(weight_kernel, out_shape=jax.ShapeDtypeStruct((4 * rows, w...  12.4 us
    unnamed x39, local copies, waits for them, and re-layouts  10.3 us
    dot_general x1, matrix products, shards(): jnp.einsum('jgf,jgd->jfd', act, grad_rows, preferred_element_type=jnp.flo...  5.43 us
    dot_general x1, matrix products, shards(): jnp.einsum('jgd,jgf->jdf', slot_rows, grad_pre, preferred_element_type=jn...  3.31 us

profile of v1, /device:TPU:0, one launch (start us, length us, event | category | flops | bytes accessed | tf_op | source)
XLA Modules:
  0.0 154.6 jit_solution(17500487679205105205)
XLA Ops:
  0.6 1.2 copy-done
  1.9 1.0 fusion.29
  2.9 1.0 copy-done.1
  4.0 12.4 %whole_weight.1 = bf16[1024,1024]{1,0:T(8,128)(2,1)S(1)} custom-call(bf16[256,1024]{1,0:T(8,128)(2,1)S(1)} %copy-done.1), custom_call_target="tpu_custom_call" | custom-call | tf_op jit(solution)/shard_map/whole_weight/pallas_call | solution.py:180
  16.4 1.4 fusion.10
  17.8 0.9 copy-done.2
  19.0 1.0 copy-done.4
  22.1 1.6 %convolution_convert_fusion.7 = bf16[2,64,1024]{2,1,0:T(8,128)(2,1)S(1)} fusion(bf16[2,256,1024]{2,1,0:T(8,128)(2,1)} %bitcast.109, f32[8,2,8,256]{3,2,1,0:T(8,128)S(1)} %bitcast.115, f32[2,64]{1,0:T(2,128)S(1)} %copy.22), kind=kOutput, calls=%fused_computation.33 | convolution fusion | flops 67305472 | bytes 1442304 | tf_op jit(solution)/shard_map/bms,bmd->bsd/dot_general | solution.py:586
  23.7 1.5 convolution_convert_fusion.6
  25.2 29.8 %to_experts.1 = bf16[2,2,4,2,32,1024]{5,4,3,2,1,0:T(8,128)(2,1)S(1)} custom-call(bf16[128,1024]{1,0:T(8,128)(2,1)S(1)} %bitcast.105, bf16[128,1024]{1,0:T(8,128)(2,1)S(1)} %bitcast.108), custom_call_target="tpu_custom_call" | custom-call | tf_op jit(solution)/shard_map/to_experts/pallas_call | solution.py:276
  55.4 2.7 %copy-done.7 = bf16[2,1024,1024]{2,1,0:T(8,128)(2,1)S(1)} copy-done((bf16[2,1024,1024]{2,1,0:T(8,128)(2,1)S(1)}, bf16[2,1024,1024]{2,1,0:T(8,128)(2,1)}, u32[]{:S(2)}) %copy-start.7) | copy-done | bytes 4194328
  58.0 1.3 fusion.45
  60.2 2.5 %fusion.17 = (bf16[2,256,1024]{2,1,0:T(8,128)(2,1)S(1)}, f32[2,256,1024]{2,1,0:T(8,128)S(1)}) fusion(f32[2,256,1024]{2,1,0:T(8,128)S(1)} %fusion.45, bf16[2,256,1024]{2,1,0:T(8,128)(2,1)S(1)} %bitcast.113, bf16[2,1024,1024]{2,1,0:T(8,128)(2,1)S(1)} %copy-done.16), kind=kOutput, calls=%fused_computation.23 | convolution fusion | flops 1084227584 | bytes 10485760 | tf_op jit(solution)/shard_map/jgd,jdf->jgf/dot_general | solution.py:596
  62.8 1.3 convolution_convert_fusion.4
  64.4 1.4 convolution_convert_fusion.5
  65.8 28.8 %to_images.1 = bf16[2,128,1024]{2,1,0:T(8,128)(2,1)S(1)} custom-call(bf16[2,4,2,32,1024]{4,3,2,1,0:T(8,128)(2,1)S(1)} %bitcast.107, bf16[2,4,2,32,1024]{4,3,2,1,0:T(8,128)(2,1)S(1)} %bitcast.106), custom_call_target="tpu_custom_call" | custom-call | tf_op jit(solution)/shard_map/to_images/pallas_call | solution.py:377
  96.5 2.5 %fusion.26 = bf16[2,8,8,256]{3,2,1,0:T(8,128)(2,1)S(1)} fusion(f32[2,256,64]{1,2,0:T(8,128)} %fusion.24, f32[2,64]{1,0:T(2,128)S(1)} %copy.22, f32[8,2,8,256]{3,2,1,0:T(8,128)S(1)} %bitcast.118, bf16[2,256,1024]{2,1,0:T(8,128)(2,1)} %bitcast.110, bf16[2,64,1024]{2,1,0:T(8,128)(2,1)} %bitcast.120), kind=kOutput, calls=%fused_computation.43 | convolution fusion | flops 134447488 | bytes 1638912 | tf_op jit(solution)/shard_map/sub | solution.py:628
  99.0 1.5 fusion.27.u
  100.6 5.4 %convolution_convert_fusion = bf16[2,1024,1024]{2,1,0:T(8,128)(2,1)} fusion(bf16[2,256,1024]{2,1,0:T(8,128)(2,1)} %bitcast.112, f32[2,256,1024]{2,1,0:T(8,128)} %copy-done.18), kind=kOutput, calls=%fused_computation.4 | convolution fusion | flops 1080557568 | bytes 7340032 | tf_op jit(solution)/shard_map/jgf,jgd->jfd/dot_general | solution.py:612
  109.1 2.3 %convolution_convert_fusion.3 = bf16[512,1024]{1,0:T(8,128)(2,1)} fusion(bf16[512,1024]{1,0:T(8,128)(2,1)S(1)} %fusion.9, bf16[1024,1024]{1,0:T(8,128)(2,1)S(1)} %whole_weight.1), kind=kOutput, calls=%fused_computation.29 | convolution fusion | flops 1074266112 | bytes 4194304 | tf_op jit(solution)/shard_map/dot_general | solution.py:643
  111.4 1.3 convolution_convert_fusion.2
  112.7 36.6 %sums.1 = (f32[256,1024]{1,0:T(8,128)S(1)}, f32[2,32,1024]{2,1,0:T(8,128)S(1)}) custom-call(bf16[2,2,256,1024]{3,2,1,0:T(8,128)(2,1)S(1)} %bitcast.104, f32[2,32,1024]{2,1,0:T(8,128)S(1)} %fusion.27.u), custom_call_target="tpu_custom_call" | custom-call | tf_op jit(solution)/shard_map/sums/pallas_call | solution.py:520
  150.3 3.3 %convolution_convert_fusion.1 = bf16[2,1024,1024]{2,1,0:T(8,128)(2,1)} fusion(bf16[2,256,1024]{2,1,0:T(8,128)(2,1)S(1)} %bitcast.114, bf16[2,256,1024]{2,1,0:T(8,128)(2,1)S(1)} %copy-done.14), kind=kOutput, calls=%fused_computation.5 | convolution fusion | flops 1075838976 | bytes 6291456 | tf_op jit(solution)/shard_map/jgd,jgf->jdf/dot_general | solution.py:615
  153.7 1.0 copy.60
  (53 shorter events, 9.9 us)
Async XLA Ops:
  0.6 1.2 copy-start
  2.9 1.1 copy-start.1
  4.0 12.4 %copy-start.17 = (bf16[2,256,1024]{2,1,0:T(8,128)(2,1)S(1)}, bf16[2,256,1024]{2,1,0:T(8,128)(2,1)}, u32[]{:S(2)}) copy-start(bf16[2,256,1024]{2,1,0:T(8,128)(2,1)} %param.8) | copy-start | bytes 3145732
  17.8 1.0 copy-start.2
  17.8 2.2 %copy-start.11 = (bf16[1024,64]{0,1:T(8,128)(2,1)S(1)}, bf16[1024,64]{0,1:T(8,128)(2,1)}, u32[]{:S(2)}) copy-start(bf16[1024,64]{0,1:T(8,128)(2,1)} %param.11) | copy-start | bytes 393220
  19.0 1.0 copy-start.4
  55.1 2.9 %copy-start.7 = (bf16[2,1024,1024]{2,1,0:T(8,128)(2,1)S(1)}, bf16[2,1024,1024]{2,1,0:T(8,128)(2,1)}, u32[]{:S(2)}) copy-start(bf16[2,1024,1024]{2,1,0:T(8,128)(2,1)} %param.13) | copy-start | bytes 12582916
  55.4 4.0 %copy-start.8 = (bf16[1,2,4,2,32,1024]{5,4,3,2,1,0:T(8,128)(2,1)}, bf16[1,2,4,2,32,1024]{5,4,3,2,1,0:T(8,128)(2,1)S(1)}, u32[]{:S(2)}) copy-start(bf16[1,2,4,2,32,1024]{5,4,3,2,1,0:T(8,128)(2,1)S(1)} %get-tuple-element.10) | copy-start | bytes 3145732
  55.4 4.0 %copy-start.9 = (bf16[1,2,4,2,32,1024]{5,4,3,2,1,0:T(8,128)(2,1)}, bf16[1,2,4,2,32,1024]{5,4,3,2,1,0:T(8,128)(2,1)S(1)}, u32[]{:S(2)}) copy-start(bf16[1,2,4,2,32,1024]{5,4,3,2,1,0:T(8,128)(2,1)S(1)} %get-tuple-element.11) | copy-start | bytes 3145732
  58.0 2.2 %copy-start.16 = (bf16[2,1024,1024]{2,1,0:T(8,128)(2,1)S(1)}, bf16[2,1024,1024]{2,1,0:T(8,128)(2,1)}, u32[]{:S(2)}) copy-start(bf16[2,1024,1024]{2,1,0:T(8,128)(2,1)} %param.12) | copy-start | bytes 12582916
  62.7 1.3 copy-start.13
  62.7 1.7 %copy-start.18 = (f32[2,256,1024]{2,1,0:T(8,128)}, f32[2,256,1024]{2,1,0:T(8,128)S(1)}, u32[]{:S(2)}) copy-start(f32[2,256,1024]{2,1,0:T(8,128)S(1)} %get-tuple-element.19) | copy-start | bytes 6291460
  65.8 29.5 %copy-start.5 = (bf16[2,256,1024]{2,1,0:T(8,128)(2,1)S(1)}, bf16[2,256,1024]{2,1,0:T(8,128)(2,1)}, u32[]{:S(2)}) copy-start(bf16[2,256,1024]{2,1,0:T(8,128)(2,1)} %param.9) | copy-start | bytes 3145732
  100.6 5.4 %copy-start.12 = (bf16[1,128,1024]{2,1,0:T(8,128)(2,1)S(1)}, bf16[1,128,1024]{2,1,0:T(8,128)(2,1)}, u32[]{:S(2)}) copy-start(bf16[1,128,1024]{2,1,0:T(8,128)(2,1)} %get-tuple-element.13) | copy-start | bytes 786436
  106.0 1.2 copy-start.3
  107.3 1.2 copy-start.6
  109.1 2.3 %copy-start.15 = (bf16[512,1024]{1,0:T(8,128)(2,1)}, bf16[512,1024]{1,0:T(8,128)(2,1)S(1)}, u32[]{:S(2)}) copy-start(bf16[512,1024]{1,0:T(8,128)(2,1)S(1)} %fusion.9) | copy-start | bytes 3145732
  112.7 37.7 %copy-start.10 = (bf16[1,2,4,2,32,1024]{5,4,3,2,1,0:T(8,128)(2,1)S(1)}, bf16[1,2,4,2,32,1024]{5,4,3,2,1,0:T(8,128)(2,1)}, u32[]{:S(2)}) copy-start(bf16[1,2,4,2,32,1024]{5,4,3,2,1,0:T(8,128)(2,1)} %copy-done.9) | copy-start | bytes 3145732
  112.7 37.7 %copy-start.14 = (bf16[2,256,1024]{2,1,0:T(8,128)(2,1)S(1)}, bf16[2,256,1024]{2,1,0:T(8,128)(2,1)}, u32[]{:S(2)}) copy-start(bf16[2,256,1024]{2,1,0:T(8,128)(2,1)} %copy-done.13) | copy-start | bytes 3145732

commit v2 on v1

--- a/solution.py
+++ b/solution.py
@@ -188,10 +188,45 @@
     )(own)
 
 
-def out_kernel(a_ref, b_ref, x_ref, pairs, came, blocks, s1, r1, s2, r2):
+def curve(x):
+    slope = math.sqrt(2 / math.pi)
+    square = x * x
+    t = jnp.tanh(slope * (x + 0.044715 * (square * x)))
+    cdf = 0.5 * (1.0 + t)
+    return x * cdf, cdf + x * (0.5 * (1.0 - t * t)) * (slope * (1.0 + 3 * 0.044715 * square))
+
+
+def times(a, b):
+    return jnp.dot(a, b, preferred_element_type=F32)
+
+
+def times_t(a, b):
+    return lax.dot_general(a, b, (((1,), (1,)), ((), ())), preferred_element_type=F32)
+
+
+def t_times(a, b):
+    return lax.dot_general(a, b, (((0,), (0,)), ((), ())), preferred_element_type=F32)
+
+
+def expert_kernel(
+    a_ref, b_ref, win, wout,
+    out, gin, gout,
+    pairs, came, blocks, x, wi, wo, act, slope, gpre, o,
+    halves, chip, paired, crossing, blocks2, pairs2, came2, gi, go,
+    s1, r1, s2, r2, sa, ra, sb, rb, sc, rc, sw, sg,
+):
     z, core, xy = place()
     zh = lax.div(z, 2)
     partner = at_core(flip(core))
+    width = x.shape[-1]
+    hidden = act.shape[-1]
+    load_in = pltpu.make_async_copy(win, wi, sw.at[0])
+    load_out = pltpu.make_async_copy(wout, wo, sw.at[1])
+    load_in.start()
+    load_out.start()
+
+    for kind, ref in enumerate((a_ref, b_ref)):
+        pairs[kind] = reorder(to_pairs, ref[...])
     greet([at_z(mate(z)), at_z(cross(z)), partner], xy)
 
     def swap(kind):
@@ -208,178 +243,251 @@
             rows8(pairs, kind, xy), rows8(came, kind, xy), s1.at[kind, 0]
         )
 
-    for kind, ref in enumerate((a_ref, b_ref)):
-        pairs[kind] = reorder(to_pairs, ref[...])
+    for kind in range(2):
         keep(kind).start()
         xy_start(*swap(kind))
 
     def there(kind, zz):
-        return x_ref.at[kind, :, zz, core]
+        return x.at[kind, :, zz, core]
 
     def send(kind, number, src, zz, device):
         return remote(src, there(kind, zz), s2.at[kind, number], r2.at[kind, number], device)
 
-    def firsts(kind):
-        return (
-            send(kind, 0, blocks.at[kind, zh], z, at_z(mate(z))),
-            send(kind, 1, blocks.at[kind, flip(zh)], z, at_z(cross(z))),
-            send(kind, 3, blocks.at[kind, zh], z, partner),
-        )
-
-    def passed(kind):
-        c, m, f = cross(z), mate(z), far(z)
-        return (
-            send(kind, 2, there(kind, c), c, at_z(m)),
-            send(kind, 4, there(kind, c), c, partner),
-            send(kind, 5, there(kind, m), m, partner),
-            send(kind, 6, there(kind, f), f, partner),
-        )
+    c, m, f = cross(z), mate(z), far(z)
+
+    def to_mate(kind):
+        return send(kind, 0, blocks.at[kind, zh], z, at_z(m))
+
+    def to_cross(kind):
+        return send(kind, 1, blocks.at[kind, flip(zh)], z, at_z(c))
+
+    def on_mate(kind):
+        return send(kind, 2, there(kind, c), c, at_z(m))
+
+    def to_core(kind, number):
+        if number == 3:
+            return send(kind, 3, blocks.at[kind, zh], z, partner)
+        zz = (c, m, f)[number - 4]
+        return send(kind, number, there(kind, zz), zz, partner)
 
     def mine(kind):
         return pltpu.make_async_copy(blocks.at[kind, zh], there(kind, z), s2.at[kind, 7])
 
-    for kind in range(2):
+    def spread(kind):
         keep(kind).wait()
         xy_wait(*swap(kind))
         ordered = reorder(to_blocks, came[kind])
         for i in range(2):
             for e in range(2):
                 blocks[kind, i, e] = ordered[i * 64 + e * 32 : i * 64 + e * 32 + 32]
-        for copy in firsts(kind):
+        to_cross(kind).start()
+        to_mate(kind).start()
+        to_core(kind, 3).start()
+        mine(kind).start()
+
+    def relay(kind):
+        to_cross(kind).wait_recv()
+        on_mate(kind).start()
+        to_core(kind, 4).start()
+        to_mate(kind).wait_recv()
+        to_core(kind, 5).start()
+
+    def relay_last(kind):
+        on_mate(kind).wait_recv()
+        to_core(kind, 6).start()
+
+    def arrived(kind):
+        mine(kind).wait()
+        for number in range(3, 7):
+            to_core(kind, number).wait_recv()
+
+    def sent(kind):
+        to_mate(kind).wait_send()
+        to_cross(kind).wait_send()
+        on_mate(kind).wait_send()
+        for number in range(3, 7):
+            to_core(kind, number).wait_send()
+
+    spread(0)
+    spread(1)
+    relay(0)
+    relay(1)
+    relay_last(0)
+    arrived(0)
+    load_in.wait()
+    load_out.wait()
+
+    def rows_of(kind, e):
+        return x[kind, e].reshape(256, width)
+
+    cut = 512
+
+    def up(e):
+        rows = rows_of(0, e)
+        for n in range(0, hidden, cut):
+            value, rise = curve(times(rows, wi[e, :, n : n + cut]))
+            act[e, :, n : n + cut] = value.astype(BF16)
+            slope[e, :, n : n + cut] = rise
+
+    def down(e):
+        rows = act[e]
+        for n in range(0, width, cut):
+            part = times(rows, wo[e, :, n : n + cut]).astype(BF16)
+            o[0, e, :, :, :, n : n + cut] = part.reshape(4, 2, 32, cut)
+
+    def back_down(e):
+        rows = rows_of(1, e)
+        for n in range(0, hidden, cut):
+            rise = times_t(rows, wo[e, n : n + cut, :])
+            gpre[e, :, n : n + cut] = (rise * slope[e, :, n : n + cut]).astype(BF16)
+
+    def back_up(e):
+        rows = gpre[e]
+        for n in range(0, width, cut):
+            part = times_t(rows, wi[e, n : n + cut, :]).astype(BF16)
+            o[1, e, :, :, :, n : n + cut] = part.reshape(4, 2, 32, cut)
+
+    def home_core(kind, e):
+        return remote(
+            o.at[kind, e, :, flip(core)], halves.at[kind, e], sa.at[kind, e], ra.at[kind, e], partner
+        )
+
+    def home_mate(kind):
+        return [
+            remote(chip.at[kind, zz], paired.at[kind, i], sb.at[kind, i], rb.at[kind, i], at_z(m))
+            for i, zz in enumerate((f, m))
+        ]
+
+    def home_cross(kind):
+        return remote(
+            crossing.at[kind], blocks2.at[kind, zh], sb.at[kind, 2], rb.at[kind, 2], at_z(c)
+        )
+
+    def home_swap(kind):
+        return (
+            xy,
+            lambda k: rows8(pairs2, kind, k),
+            lambda k: rows8(came2, kind, k),
+            sc.at[kind],
+            rc.at[kind],
+        )
+
+    def home_keep(kind):
+        return pltpu.make_async_copy(
+            rows8(pairs2, kind, xy), rows8(came2, kind, xy), sc.at[kind, 0]
+        )
+
+    def chip_sum(kind):
+        for e in range(2):
+            home_core(kind, e).wait()
+            for zz in range(4):
+                chip[kind, zz, e] = (
+                    o[kind, e, zz, core].astype(F32) + halves[kind, e, zz].astype(F32)
+                ).astype(BF16)
+        for copy in home_mate(kind):
             copy.start()
-        mine(kind).start()
+
+    def pair_sum(kind):
+        on, own = home_mate(kind)
+        on.wait_recv()
+        for e in range(2):
+            crossing[kind, e] = (
+                chip[kind, c, e].astype(F32) + paired[kind, 0, e].astype(F32)
+            ).astype(BF16)
+        home_cross(kind).start()
+        own.wait_recv()
+        for e in range(2):
+            blocks2[kind, zh, e] = (
+                chip[kind, z, e].astype(F32) + paired[kind, 1, e].astype(F32)
+            ).astype(BF16)
+
+    def home(kind):
+        home_cross(kind).wait_recv()
+        rows = jnp.concatenate([blocks2[kind, i, e] for i in range(2) for e in range(2)], axis=0)
+        pairs2[kind] = reorder(from_blocks, rows)
+        home_keep(kind).start()
+        xy_start(*home_swap(kind))
+
+    def landed(kind):
+        home_keep(kind).wait()
+        xy_wait(*home_swap(kind))
+        out[kind] = reorder(from_pairs, came2[kind])
+
+    def out_gradient(e):
+        right = rows_of(1, e)
+        for n in range(0, hidden, cut):
+            go[e, n : n + cut, :] = t_times(act[e, :, n : n + cut], right).astype(BF16)
+        pltpu.make_async_copy(go.at[e], gout.at[e], sg.at[0, e]).start()
+
+    def in_gradient(e):
+        left = rows_of(0, e)
+        right = gpre[e]
+        for n in range(0, width, cut):
+            gi[e, n : n + cut, :] = t_times(left[:, n : n + cut], right).astype(BF16)
+        pltpu.make_async_copy(gi.at[e], gin.at[e], sg.at[1, e]).start()
+
+    up(0)
+    up(1)
+    relay_last(1)
+    for e in range(2):
+        down(e)
+        home_core(0, e).start()
+    arrived(1)
+    back_down(0)
+    back_down(1)
+    chip_sum(0)
+    for e in range(2):
+        back_up(e)
+        home_core(1, e).start()
+    out_gradient(0)
+    chip_sum(1)
+    pair_sum(0)
+    out_gradient(1)
+    pair_sum(1)
+    home(0)
+    in_gradient(0)
+    home(1)
+    in_gradient(1)
+    landed(0)
+    landed(1)
     for kind in range(2):
-        to_mate, to_cross, to_core = firsts(kind)
-        on_mate, on_core_c, on_core_m, on_core_f = passed(kind)
-        to_cross.wait_recv()
-        on_mate.start()
-        on_core_c.start()
-        to_mate.wait_recv()
-        on_core_m.start()
-        on_mate.wait_recv()
-        on_core_f.start()
-    for kind in range(2):
-        to_mate, to_cross, to_core = firsts(kind)
-        on_mate, on_core_c, on_core_m, on_core_f = passed(kind)
-        mine(kind).wait()
-        to_mate.wait_send()
-        to_cross.wait_send()
-        on_mate.wait_send()
-        to_core.wait()
-        on_core_c.wait()
-        on_core_m.wait()
-        on_core_f.wait()
-
-
-def to_experts(first, second):
+        sent(kind)
+        for copy in home_mate(kind):
+            copy.wait_send()
+        home_cross(kind).wait_send()
+    for e in range(2):
+        pltpu.make_async_copy(go.at[e], gout.at[e], sg.at[0, e]).wait()
+        pltpu.make_async_copy(gi.at[e], gin.at[e], sg.at[1, e]).wait()
+
+
+def experts(first, second, expert_in, expert_out):
     width = first.shape[-1]
+    hidden = expert_in.shape[-1]
+    dma = pltpu.SemaphoreType.DMA
     return pl.pallas_call(
-        out_kernel,
-        out_shape=jax.ShapeDtypeStruct((2, 2, 4, 2, 32, width), BF16),
-        in_specs=[pl.BlockSpec(memory_space=VMEM)] * 2,
-        out_specs=pl.BlockSpec(memory_space=VMEM),
+        expert_kernel,
+        out_shape=(
+            jax.ShapeDtypeStruct((2, 128, width), BF16),
+            jax.ShapeDtypeStruct(expert_in.shape, BF16),
+            jax.ShapeDtypeStruct(expert_out.shape, BF16),
+        ),
+        in_specs=[pl.BlockSpec(memory_space=VMEM)] * 2 + [pl.BlockSpec(memory_space=pl.ANY)] * 2,
+        out_specs=(
+            pl.BlockSpec(memory_space=VMEM),
+            pl.BlockSpec(memory_space=pl.ANY),
+            pl.BlockSpec(memory_space=pl.ANY),
+        ),
         scratch_shapes=[
             VMEM((2, 128, width), BF16),
             VMEM((2, 128, width), BF16),
             VMEM((2, 2, 2, 32, width), BF16),
-            pltpu.SemaphoreType.DMA((2, 16)),
-            pltpu.SemaphoreType.DMA((2, 16)),
-            pltpu.SemaphoreType.DMA((2, 8)),
-            pltpu.SemaphoreType.DMA((2, 8)),
-        ],
-        compiler_params=params(2),
-        name="to_experts",
-    )(first, second)
-
-
-def back_kernel(
-    o0, o1, out, halves, chip, paired, crossing, blocks, pairs, came, sa, ra, sb, rb, sc, rc
-):
-    z, core, xy = place()
-    zh = lax.div(z, 2)
-    partner = at_core(flip(core))
-    greet([at_z(mate(z)), at_z(cross(z)), partner], xy)
-    parts = (o0, o1)
-
-    def to_core(kind):
-        return remote(
-            parts[kind].at[:, :, flip(core)], halves.at[kind], sa.at[kind], ra.at[kind], partner
-        )
-
-    def to_mate(kind):
-        m = mate(z)
-        return [
-            remote(chip.at[kind, zz], paired.at[kind, i], sb.at[kind, i], rb.at[kind, i], at_z(m))
-            for i, zz in enumerate((far(z), m))
-        ]
-
-    def to_cross(kind):
-        return remote(
-            crossing.at[kind], blocks.at[kind, zh], sb.at[kind, 2], rb.at[kind, 2], at_z(cross(z))
-        )
-
-    def swap(kind):
-        return (
-            xy,
-            lambda k: rows8(pairs, kind, k),
-            lambda k: rows8(came, kind, k),
-            sc.at[kind],
-            rc.at[kind],
-        )
-
-    def keep(kind):
-        return pltpu.make_async_copy(
-            rows8(pairs, kind, xy), rows8(came, kind, xy), sc.at[kind, 0]
-        )
-
-    for kind in range(2):
-        to_core(kind).start()
-    for kind in range(2):
-        to_core(kind).wait()
-        for e in range(2):
-            for zz in range(4):
-                chip[kind, zz, e] = (
-                    parts[kind][e, zz, core].astype(F32) + halves[kind, e, zz].astype(F32)
-                ).astype(BF16)
-        for copy in to_mate(kind):
-            copy.start()
-    for kind in range(2):
-        on, own = to_mate(kind)
-        on.wait_recv()
-        for e in range(2):
-            crossing[kind, e] = (
-                chip[kind, cross(z), e].astype(F32) + paired[kind, 0, e].astype(F32)
-            ).astype(BF16)
-        to_cross(kind).start()
-        own.wait_recv()
-        for e in range(2):
-            blocks[kind, zh, e] = (
-                chip[kind, z, e].astype(F32) + paired[kind, 1, e].astype(F32)
-            ).astype(BF16)
-    for kind in range(2):
-        to_cross(kind).wait_recv()
-        rows = jnp.concatenate([blocks[kind, i, e] for i in range(2) for e in range(2)], axis=0)
-        pairs[kind] = reorder(from_blocks, rows)
-        keep(kind).start()
-        xy_start(*swap(kind))
-    for kind in range(2):
-        keep(kind).wait()
-        xy_wait(*swap(kind))
-        out[kind] = reorder(from_pairs, came[kind])
-    for kind in range(2):
-        for copy in to_mate(kind):
-            copy.wait_send()
-        to_cross(kind).wait_send()
-
-
-def to_images(first, second):
-    width = first.shape[-1]
-    return pl.pallas_call(
-        back_kernel,
-        out_shape=jax.ShapeDtypeStruct((2, 128, width), BF16),
-        in_specs=[pl.BlockSpec(memory_space=VMEM)] * 2,
-        out_specs=pl.BlockSpec(memory_space=VMEM),
-        scratch_shapes=[
+            VMEM((2, 2, 4, 2, 32, width), BF16),
+            VMEM(expert_in.shape, BF16),
+            VMEM(expert_out.shape, BF16),
+            VMEM((2, 256, hidden), BF16),
+            VMEM((2, 256, hidden), F32),
+            VMEM((2, 256, hidden), BF16),
+            VMEM((2, 2, 4, 2, 32, width), BF16),
             VMEM((2, 2, 4, 32, width), BF16),
             VMEM((2, 4, 2, 32, width), BF16),
             VMEM((2, 2, 2, 32, width), BF16),
@@ -387,16 +495,24 @@
             VMEM((2, 2, 2, 32, width), BF16),
             VMEM((2, 128, width), BF16),
             VMEM((2, 128, width), BF16),
-            pltpu.SemaphoreType.DMA((2,)),
-            pltpu.SemaphoreType.DMA((2,)),
-            pltpu.SemaphoreType.DMA((2, 3)),
-            pltpu.SemaphoreType.DMA((2, 3)),
-            pltpu.SemaphoreType.DMA((2, 16)),
-            pltpu.SemaphoreType.DMA((2, 16)),
+            VMEM(expert_in.shape, BF16),
+            VMEM(expert_out.shape, BF16),
+            dma((2, 16)),
+            dma((2, 16)),
+            dma((2, 8)),
+            dma((2, 8)),
+            dma((2, 2)),
+            dma((2, 2)),
+            dma((2, 3)),
+            dma((2, 3)),
+            dma((2, 16)),
+            dma((2, 16)),
+            dma((2,)),
+            dma((2, 2)),
         ],
-        compiler_params=params(3),
-        name="to_images",
-    )(first, second)
+        compiler_params=params(2, 50 << 20),
+        name="experts",
+    )(first, second, expert_in, expert_out)
 
 
 def sum_kernel(
@@ -554,10 +670,6 @@
     )(partial.reshape(2, 2, rows, width), unit_partial.reshape(2, 32, width))
 
 
-def gelu_back(pre, upstream):
-    return jax.vjp(jax.nn.gelu, pre)[1](upstream)[0]
-
-
 def shards(context, residual, cotangent, proj_weight, slot_params, expert_in, expert_out):
     images, tokens, width = context.shape
     rows = images * tokens
@@ -589,32 +701,14 @@
     grad_slot_out = jnp.einsum(
         "bms,bmd->bsd", combine, cotangent, preferred_element_type=jnp.float32
     ).astype(jnp.bfloat16)
-    arrived = to_experts(
-        slot_in.reshape(images * slots, width), grad_slot_out.reshape(images * slots, width)
-    ).reshape(2, 2, 256, width)
-    slot_rows, grad_rows = arrived[0], arrived[1]
-    pre = jnp.einsum("jgd,jdf->jgf", slot_rows, expert_in, preferred_element_type=jnp.float32)
-    act = jax.nn.gelu(pre).astype(jnp.bfloat16)
-    out_part = jnp.einsum(
-        "jgf,jfd->jgd", act, expert_out, preferred_element_type=jnp.float32
-    ).astype(jnp.bfloat16)
-    grad_act = jnp.einsum(
-        "jgd,jfd->jgf", grad_rows, expert_out, preferred_element_type=jnp.float32
-    )
-    grad_pre = gelu_back(pre, grad_act).astype(jnp.bfloat16)
-    grad_part = jnp.einsum(
-        "jgf,jdf->jgd", grad_pre, expert_in, preferred_element_type=jnp.float32
-    ).astype(jnp.bfloat16)
-    returned = to_images(
-        out_part.reshape(2, 4, 2, 32, width), grad_part.reshape(2, 4, 2, 32, width)
-    ).reshape(2, images, slots, width)
+    returned, grad_expert_in, grad_expert_out = experts(
+        slot_in.reshape(images * slots, width),
+        grad_slot_out.reshape(images * slots, width),
+        expert_in,
+        expert_out,
+    )
+    returned = returned.reshape(2, images, slots, width)
     slot_out, grad_slot_in = returned[0], returned[1]
-    grad_expert_out = jnp.einsum(
-        "jgf,jgd->jfd", act, grad_rows, preferred_element_type=jnp.float32
-    ).astype(jnp.bfloat16)
-    grad_expert_in = jnp.einsum(
-        "jgd,jgf->jdf", slot_rows, grad_pre, preferred_element_type=jnp.float32
-    ).astype(jnp.bfloat16)
     grad_combine = jnp.einsum(
         "bmd,bsd->bms", cotangent, slot_out, preferred_element_type=jnp.float32
     )

time: 155 us -> 138 us (0.89)
  matrix products: 29.5 us -> 15.3 us
  Pallas kernels: 108 us -> 104 us
    dot_general x6 -> x0, matrix products: 15.2 us -> none  [the longest x1 5.43 us: shards(): jnp.einsum('jgf,jgd->jfd', act, grad_rows, preferred_element_type=jnp.flo...]
    pallas_call x2 -> x1, Pallas kernels: 58.6 us -> 55 us  [experts(): pl.pallas_call(expert_kernel, out_shape=(jax.ShapeDtypeStruct((2, 128, wi...]
    unnamed x39 -> x27, local copies, waits for them, and re-layouts: 10.3 us -> 11.4 us
where the time goes in v2:
time: 138 us
  Pallas kernels  104 us (75%)
  matrix products  15.3 us (11%)
  local copies, waits for them, and re-layouts  13 us (9%)
  other arithmetic  4.41 us (3%)
    pallas_call x1, Pallas kernels, experts(): pl.pallas_call(expert_kernel, out_shape=(jax.ShapeDtypeStruct((2, 128, wi...  55 us
    pallas_call x1, Pallas kernels, sums(): pl.pallas_call(sum_kernel, out_shape=(jax.ShapeDtypeStruct((rows, width),...  36.7 us
    pallas_call x1, Pallas kernels, whole_weight(): pl.pallas_call(weight_kernel, out_shape=jax.ShapeDtypeStruct((4 * rows, w...  12.4 us
    unnamed x27, local copies, waits for them, and re-layouts  11.4 us

profile of v2, /device:TPU:0, one launch (start us, length us, event | category | flops | bytes accessed | tf_op | source)
XLA Modules:
  0.0 137.6 jit_solution(9356660458863377755)
XLA Ops:
  0.6 1.2 copy-done
  1.9 1.0 fusion.22
  2.9 1.0 copy-done.1
  4.0 12.4 %whole_weight.1 = bf16[1024,1024]{1,0:T(8,128)(2,1)S(1)} custom-call(bf16[256,1024]{1,0:T(8,128)(2,1)S(1)} %copy-done.1), custom_call_target="tpu_custom_call" | custom-call | tf_op jit(solution)/shard_map/whole_weight/pallas_call | solution.py:180
  16.4 1.4 %fusion.10 = (f32[512]{0:T(512)S(1)}, bf16[512,1024]{1,0:T(8,128)(2,1)S(1)}) fusion(bf16[512,1024]{1,0:T(8,128)(2,1)S(1)} %bitcast.88, bf16[1024,1024]{1,0:T(8,128)(2,1)S(1)} %whole_weight.1, bf16[512,1024]{1,0:T(8,128)(2,1)S(1)} %bitcast.106), kind=kOutput, calls=%fused_computation.12 | convolution fusion | flops 1076887040 | bytes 5244928 | tf_op jit(solution)/shard_map/dot_general | solution.py:680
  17.8 0.9 copy-done.2
  19.0 1.0 copy-done.4
  20.5 0.8 reduce_sum.74
  21.3 0.8 copy.18
  22.1 1.6 %convolution_convert_fusion.3 = bf16[2,64,1024]{2,1,0:T(8,128)(2,1)S(1)} fusion(bf16[2,256,1024]{2,1,0:T(8,128)(2,1)} %bitcast.93, f32[8,2,8,256]{3,2,1,0:T(8,128)S(1)} %bitcast.95, f32[2,64]{1,0:T(2,128)S(1)} %copy.18), kind=kOutput, calls=%fused_computation.19 | convolution fusion | flops 67305472 | bytes 1442304 | tf_op jit(solution)/shard_map/bms,bmd->bsd/dot_general | solution.py:698
  23.7 1.5 %convolution_convert_fusion.2 = bf16[2,64,1024]{2,1,0:T(8,128)(2,1)S(1)} fusion(bf16[2,256,1024]{2,1,0:T(8,128)(2,1)} %param.9, f32[8,2,8,256]{3,2,1,0:T(8,128)S(1)} %bitcast.96, f32[2,256]{1,0:T(2,128)S(1)} %div.43), kind=kOutput, calls=%fused_computation.18 | convolution fusion | flops 67305472 | bytes 1443840 | tf_op jit(solution)/shard_map/bms,bmd->bsd/dot_general | solution.py:701
  25.3 55.0 %experts.1 = (bf16[2,128,1024]{2,1,0:T(8,128)(2,1)S(1)}, bf16[2,1024,1024]{2,1,0:T(8,128)(2,1)}, bf16[2,1024,1024]{2,1,0:T(8,128)(2,1)}) custom-call(bf16[128,1024]{1,0:T(8,128)(2,1)S(1)} %bitcast.91, bf16[128,1024]{1,0:T(8,128)(2,1)S(1)} %bitcast.92, bf16[2,1024,1024]{2,1,0:T(8,128)(2,1)} %win.1, bf16[2,1024,1024]{2,1,0:T(8,128)(2,1)} %wout.1), custom_call_target="tpu_custom_call" | custom-call | tf_op jit(solution)/shard_map/experts/pallas_call | solution.py:467
  80.2 0.7 fusion.33
  82.1 2.5 %fusion.19 = bf16[2,8,8,256]{3,2,1,0:T(8,128)(2,1)S(1)} fusion(f32[2,256,64]{1,2,0:T(8,128)} %fusion.17, f32[2,64]{1,0:T(2,128)S(1)} %copy.18, f32[8,2,8,256]{3,2,1,0:T(8,128)S(1)} %bitcast.98, bf16[2,256,1024]{2,1,0:T(8,128)(2,1)} %bitcast.94, bf16[2,64,1024]{2,1,0:T(8,128)(2,1)} %bitcast.100), kind=kOutput, calls=%fused_computation.29 | convolution fusion | flops 134447488 | bytes 1638912 | tf_op jit(solution)/shard_map/sub | solution.py:722
  84.6 1.6 %fusion.20.u = f32[2,32,1024]{2,1,0:T(8,128)S(1)} fusion(bf16[2,32,512]{2,1,0:T(8,128)(2,1)S(1)} %bitcast.104, bf16[512,1024]{1,0:T(8,128)(2,1)} %copy-done.4), kind=kOutput, calls=%fused_computation.30 | convolution fusion | flops 67108864 | bytes 1376256 | tf_op jit(solution)/shard_map/dot_general | solution.py:731
  86.3 1.5 %fusion.30 = f32[2,256,1024]{2,1,0:T(8,128)S(1)} fusion(bf16[2,64,1024]{2,1,0:T(8,128)(2,1)} %bitcast.101, f32[8,2,8,256]{3,2,1,0:T(8,128)S(1)} %bitcast.99, f32[2,64]{1,0:T(2,128)S(1)} %copy.18), kind=kOutput, calls=%fused_computation.49 | convolution fusion | flops 67174400 | bytes 2490880 | tf_op jit(solution)/shard_map/bms,bsd->bmd/dot_general | solution.py:725
  89.6 2.3 %convolution_convert_fusion.1 = bf16[512,1024]{1,0:T(8,128)(2,1)} fusion(bf16[512,1024]{1,0:T(8,128)(2,1)S(1)} %fusion.9, bf16[1024,1024]{1,0:T(8,128)(2,1)S(1)} %whole_weight.1), kind=kOutput, calls=%fused_computation.17 | convolution fusion | flops 1074266112 | bytes 4194304 | tf_op jit(solution)/shard_map/dot_general | solution.py:737
  91.9 1.3 convolution_convert_fusion
  93.2 36.7 %sums.1 = (f32[256,1024]{1,0:T(8,128)S(1)}, f32[2,32,1024]{2,1,0:T(8,128)S(1)}) custom-call(bf16[2,2,256,1024]{3,2,1,0:T(8,128)(2,1)S(1)} %bitcast.90, f32[2,32,1024]{2,1,0:T(8,128)S(1)} %fusion.20.u), custom_call_target="tpu_custom_call" | custom-call | tf_op jit(solution)/shard_map/sums/pallas_call | solution.py:636
  130.1 0.8 fusion.24
  131.0 1.0 copy.54
  131.9 2.1 %copy.55 = bf16[2,1024,1024]{2,1,0:T(8,128)(2,1)} copy(bf16[2,1024,1024]{2,1,0:T(8,128)(2,1)S(1)} %copy-done.8) | data formatting | bytes 8388608
  134.1 1.6 %copy-done.7 = bf16[2,1024,1024]{2,1,0:T(8,128)(2,1)S(1)} copy-done((bf16[2,1024,1024]{2,1,0:T(8,128)(2,1)S(1)}, bf16[2,1024,1024]{2,1,0:T(8,128)(2,1)}, u32[]{:S(2)}) %copy-start.7) | copy-done | bytes 4194328
  135.6 2.0 %copy.56 = bf16[2,1024,1024]{2,1,0:T(8,128)(2,1)} copy(bf16[2,1024,1024]{2,1,0:T(8,128)(2,1)S(1)} %copy-done.7) | data formatting | bytes 8388608
  (33 shorter events, 4.1 us)
Async XLA Ops:
  0.6 1.2 copy-start
  2.9 1.1 copy-start.1
  4.0 12.4 %copy-start.11 = (bf16[2,256,1024]{2,1,0:T(8,128)(2,1)S(1)}, bf16[2,256,1024]{2,1,0:T(8,128)(2,1)}, u32[]{:S(2)}) copy-start(bf16[2,256,1024]{2,1,0:T(8,128)(2,1)} %param.8) | copy-start | bytes 3145732
  17.8 1.0 copy-start.2
  17.8 2.2 %copy-start.9 = (bf16[1024,64]{0,1:T(8,128)(2,1)S(1)}, bf16[1024,64]{0,1:T(8,128)(2,1)}, u32[]{:S(2)}) copy-start(bf16[1024,64]{0,1:T(8,128)(2,1)} %param.11) | copy-start | bytes 393220
  19.0 1.0 copy-start.4
  25.2 55.7 %copy-start.5 = (bf16[2,256,1024]{2,1,0:T(8,128)(2,1)S(1)}, bf16[2,256,1024]{2,1,0:T(8,128)(2,1)}, u32[]{:S(2)}) copy-start(bf16[2,256,1024]{2,1,0:T(8,128)(2,1)} %param.9) | copy-start | bytes 3145732
  84.6 3.1 %copy-start.3 = (bf16[512,1024]{1,0:T(8,128)(2,1)S(1)}, bf16[512,1024]{1,0:T(8,128)(2,1)}, u32[]{:S(2)}) copy-start(bf16[512,1024]{1,0:T(8,128)(2,1)} %copy-done.2) | copy-start | bytes 3145732
  87.8 1.2 copy-start.6
  89.6 2.3 %copy-start.10 = (bf16[512,1024]{1,0:T(8,128)(2,1)}, bf16[512,1024]{1,0:T(8,128)(2,1)S(1)}, u32[]{:S(2)}) copy-start(bf16[512,1024]{1,0:T(8,128)(2,1)S(1)} %fusion.9) | copy-start | bytes 3145732
  93.2 38.7 %copy-start.8 = (bf16[2,1024,1024]{2,1,0:T(8,128)(2,1)S(1)}, bf16[2,1024,1024]{2,1,0:T(8,128)(2,1)}, u32[]{:S(2)}) copy-start(bf16[2,1024,1024]{2,1,0:T(8,128)(2,1)} %get-tuple-element.34) | copy-start | bytes 12582916
  131.9 3.7 %copy-start.7 = (bf16[2,1024,1024]{2,1,0:T(8,128)(2,1)S(1)}, bf16[2,1024,1024]{2,1,0:T(8,128)(2,1)}, u32[]{:S(2)}) copy-start(bf16[2,1024,1024]{2,1,0:T(8,128)(2,1)} %get-tuple-element.35) | copy-start | bytes 12582916

commit v3 on v2

--- a/solution.py
+++ b/solution.py
@@ -61,22 +61,19 @@
     )
 
 
-def greet(devices, xy=None):
+def greet(devices, xy):
     barrier = pltpu.get_barrier_semaphore()
     for device in devices:
         pl.semaphore_signal(barrier, inc=1, device_id=device, device_id_type=MESH)
-    count = len(devices)
-    if xy is not None:
-
-        def one(d, carry):
-            pl.semaphore_signal(
-                barrier, inc=1, device_id=at_xy(lax.rem(xy + d, 16)), device_id_type=MESH
-            )
-            return carry
-
-        lax.fori_loop(1, 16, one, 0)
-        count += 15
-    pl.semaphore_wait(barrier, count)
+
+    def one(d, carry):
+        pl.semaphore_signal(
+            barrier, inc=1, device_id=at_xy(lax.rem(xy + d, 16)), device_id_type=MESH
+        )
+        return carry
+
+    lax.fori_loop(1, 16, one, 0)
+    return lambda: pl.semaphore_wait(barrier, len(devices) + 15)
 
 
 def xy_copy(d, xy, src, dst, send, recv):
@@ -138,54 +135,6 @@
     return pltpu.CompilerParams(
         collective_id=number, has_side_effects=True, vmem_limit_bytes=limit or (40 << 20)
     )
-
-
-def weight_kernel(own, out, s_sem, r_sem):
-    z, core, _ = place()
-    block = 2 * lax.rem(z, 2) + core
-    other = 2 * flip(lax.rem(z, 2)) + core
-    half = own.shape[0] // 2
-
-    def rows(blk, start, size):
-        return out.at[pl.ds(pl.multiple_of(blk * 2 * half + start, half), size)]
-
-    partner = at_core(flip(core))
-    greet([at_z(mate(z)), at_z(cross(z)), partner])
-    to_mate = remote(own.at[pl.ds(0, half)], rows(block, 0, half), s_sem.at[0], r_sem.at[0], at_z(mate(z)))
-    to_cross = remote(
-        own.at[pl.ds(half, half)], rows(block, half, half), s_sem.at[1], r_sem.at[1], at_z(cross(z))
-    )
-    to_core = remote(own, rows(block, 0, 2 * half), s_sem.at[2], r_sem.at[2], partner)
-    to_mate.start()
-    to_cross.start()
-    to_core.start()
-    mine = pltpu.make_async_copy(own, rows(block, 0, 2 * half), s_sem.at[5])
-    mine.start()
-    first = remote(rows(other, 0, half), rows(other, 0, half), s_sem.at[3], r_sem.at[3], partner)
-    second = remote(rows(other, half, half), rows(other, half, half), s_sem.at[4], r_sem.at[4], partner)
-    to_mate.wait_recv()
-    first.start()
-    to_cross.wait_recv()
-    second.start()
-    mine.wait()
-    to_mate.wait_send()
-    to_cross.wait_send()
-    to_core.wait()
-    first.wait()
-    second.wait()
-
-
-def whole_weight(own):
-    rows, width = own.shape
-    return pl.pallas_call(
-        weight_kernel,
-        out_shape=jax.ShapeDtypeStruct((4 * rows, width), own.dtype),
-        in_specs=[pl.BlockSpec(memory_space=VMEM)],
-        out_specs=pl.BlockSpec(memory_space=VMEM),
-        scratch_shapes=[pltpu.SemaphoreType.DMA((6,)), pltpu.SemaphoreType.DMA((5,))],
-        compiler_params=params(1),
-        name="whole_weight",
-    )(own)
 
 
 def curve(x):
@@ -208,26 +157,112 @@
     return lax.dot_general(a, b, (((0,), (0,)), ((), ())), preferred_element_type=F32)
 
 
+def unit_of(slots_ref):
+    params32 = slots_ref[...].astype(F32)
+    norm = jnp.sqrt(jnp.sum(params32 * params32, axis=1, keepdims=True) + epsilon)
+    return params32 / norm, norm
+
+
+def inverse_of(stream32):
+    return lax.rsqrt(jnp.mean(stream32 * stream32, axis=1, keepdims=True) + epsilon)
+
+
 def expert_kernel(
-    a_ref, b_ref, win, wout,
-    out, gin, gout,
+    context, residual, cotangent, own, slots, win, wout,
+    out, stream, normed, expo, whole, gin, gout,
+    ctx, res, cot, natural,
     pairs, came, blocks, x, wi, wo, act, slope, gpre, o,
     halves, chip, paired, crossing, blocks2, pairs2, came2, gi, go,
-    s1, r1, s2, r2, sa, ra, sb, rb, sc, rc, sw, sg,
+    s1, r1, s2, r2, sa, ra, sb, rb, sc, rc, sw, sg, sp, rp,
 ):
     z, core, xy = place()
     zh = lax.div(z, 2)
+    zl = lax.rem(z, 2)
     partner = at_core(flip(core))
     width = x.shape[-1]
     hidden = act.shape[-1]
+    quarter = own.shape[0]
+    half = quarter // 2
+    entered = greet([at_z(mate(z)), at_z(cross(z)), partner], xy)
+
+    def block_rows(block, start, size):
+        return whole.at[pl.ds(pl.multiple_of(block * quarter + start, half), size)]
+
+    block = 2 * zl + core
+    load_ctx = pltpu.make_async_copy(context, ctx, sw.at[2])
+    load_own = pltpu.make_async_copy(own, block_rows(block, 0, quarter), sw.at[3])
+    load_res = pltpu.make_async_copy(residual, res, sw.at[4])
+    load_cot = pltpu.make_async_copy(cotangent, cot, sw.at[5])
     load_in = pltpu.make_async_copy(win, wi, sw.at[0])
     load_out = pltpu.make_async_copy(wout, wo, sw.at[1])
+    load_own.start()
+    load_ctx.start()
+    load_res.start()
+    unit32, _ = unit_of(slots)
+    unit = unit32.astype(BF16)
+    entered()
+
+    across = 2 * flip(zl) + core
+    w_mate = remote(
+        own.at[pl.ds(0, half)], block_rows(block, 0, half), sp.at[0], rp.at[0], at_z(mate(z))
+    )
+    w_cross = remote(
+        own.at[pl.ds(half, half)], block_rows(block, half, half), sp.at[1], rp.at[1], at_z(cross(z))
+    )
+    w_core = remote(own, block_rows(block, 0, quarter), sp.at[2], rp.at[2], partner)
+    w_first = remote(
+        block_rows(across, 0, half), block_rows(across, 0, half), sp.at[3], rp.at[3], partner
+    )
+    w_second = remote(
+        block_rows(across, half, half), block_rows(across, half, half), sp.at[4], rp.at[4], partner
+    )
+    w_mate.start()
+    w_cross.start()
+    w_core.start()
+    load_cot.start()
     load_in.start()
     load_out.start()
-
-    for kind, ref in enumerate((a_ref, b_ref)):
-        pairs[kind] = reorder(to_pairs, ref[...])
-    greet([at_z(mate(z)), at_z(cross(z)), partner], xy)
+    load_ctx.wait()
+    load_res.wait()
+    load_own.wait()
+
+    def project(block, first=False):
+        rows = whole[pl.ds(pl.multiple_of(block * quarter, quarter), quarter), :]
+        for b in range(2):
+            columns = ctx[b, :, pl.ds(pl.multiple_of(block * quarter, quarter), quarter)]
+            start = res[b].astype(F32) if first else slope[b]
+            slope[b] = start + times(columns, rows)
+
+    project(block, True)
+    w_core.wait_recv()
+    project(2 * zl + flip(core))
+    w_mate.wait_recv()
+    w_first.start()
+    w_cross.wait_recv()
+    w_second.start()
+    project(across)
+    w_first.wait_recv()
+    w_second.wait_recv()
+    project(2 * flip(zl) + flip(core))
+
+    def settle(i, carry):
+        for b in range(2):
+            rows = pl.ds(pl.multiple_of(i * 64, 64), 64)
+            rounded = slope[b, rows, :].astype(BF16)
+            stream[b, rows, :] = rounded
+            stream32 = rounded.astype(F32)
+            normed[b, rows, :] = (stream32 * inverse_of(stream32)).astype(BF16)
+        return carry
+
+    lax.fori_loop(0, 4, settle, 0)
+    factor = logit_scale / math.sqrt(width)
+    for b in range(2):
+        rows = normed[b]
+        ex = jnp.exp(factor * times_t(unit, rows))
+        expo[b] = ex
+        dispatch = (ex / jnp.sum(ex, axis=1, keepdims=True)).astype(BF16)
+        natural[0, 64 * b : 64 * b + 64] = times(dispatch, rows).astype(BF16)
+    pairs[0] = reorder(to_pairs, natural[0])
 
     def swap(kind):
         return (
@@ -243,9 +278,16 @@
             rows8(pairs, kind, xy), rows8(came, kind, xy), s1.at[kind, 0]
         )
 
-    for kind in range(2):
-        keep(kind).start()
-        xy_start(*swap(kind))
+    keep(0).start()
+    xy_start(*swap(0))
+    load_cot.wait()
+    for b in range(2):
+        ex = expo[b]
+        combine = (ex / jnp.sum(ex, axis=0, keepdims=True)).astype(BF16)
+        natural[1, 64 * b : 64 * b + 64] = times(combine, cot[b]).astype(BF16)
+    pairs[1] = reorder(to_pairs, natural[1])
+    keep(1).start()
+    xy_start(*swap(1))
 
     def there(kind, zz):
         return x.at[kind, :, zz, core]
@@ -450,6 +492,8 @@
     in_gradient(1)
     landed(0)
     landed(1)
+    for copy in (w_mate, w_cross, w_core, w_first, w_second):
+        copy.wait_send()
     for kind in range(2):
         sent(kind)
         for copy in home_mate(kind):
@@ -460,24 +504,30 @@
         pltpu.make_async_copy(gi.at[e], gin.at[e], sg.at[1, e]).wait()
 
 
-def experts(first, second, expert_in, expert_out):
-    width = first.shape[-1]
+def experts(context, residual, cotangent, own, slots, expert_in, expert_out):
+    width = context.shape[-1]
     hidden = expert_in.shape[-1]
     dma = pltpu.SemaphoreType.DMA
+    whole = pl.BlockSpec(memory_space=VMEM)
+    anywhere = pl.BlockSpec(memory_space=pl.ANY)
     return pl.pallas_call(
         expert_kernel,
         out_shape=(
             jax.ShapeDtypeStruct((2, 128, width), BF16),
+            jax.ShapeDtypeStruct(context.shape, BF16),
+            jax.ShapeDtypeStruct(context.shape, BF16),
+            jax.ShapeDtypeStruct((2, 64, 256), F32),
+            jax.ShapeDtypeStruct((width, width), BF16),
             jax.ShapeDtypeStruct(expert_in.shape, BF16),
             jax.ShapeDtypeStruct(expert_out.shape, BF16),
         ),
-        in_specs=[pl.BlockSpec(memory_space=VMEM)] * 2 + [pl.BlockSpec(memory_space=pl.ANY)] * 2,
-        out_specs=(
-            pl.BlockSpec(memory_space=VMEM),
-            pl.BlockSpec(memory_space=pl.ANY),
-            pl.BlockSpec(memory_space=pl.ANY),
-        ),
+        in_specs=[anywhere] * 4 + [whole] + [anywhere] * 2,
+        out_specs=(whole,) * 5 + (anywhere,) * 2,
         scratch_shapes=[
+            VMEM(context.shape, BF16),
+            VMEM(context.shape, BF16),
+            VMEM(context.shape, BF16),
+            VMEM((2, 128, width), BF16),
             VMEM((2, 128, width), BF16),
             VMEM((2, 128, width), BF16),
             VMEM((2, 2, 2, 32, width), BF16),
@@ -507,82 +557,171 @@
             dma((2, 3)),
             dma((2, 16)),
             dma((2, 16)),
-            dma((2,)),
+            dma((6,)),
             dma((2, 2)),
+            dma((5,)),
+            dma((5,)),
         ],
         compiler_params=params(2, 50 << 20),
         name="experts",
-    )(first, second, expert_in, expert_out)
+    )(context, residual, cotangent, own, slots, expert_in, expert_out)
 
 
 def sum_kernel(
-    g, u, out, u_out,
-    ga, gq, gb, gh, gc, gt, gf, gv, gall,
+    back, stream, normed, expo, whole, slots, context, cotangent,
+    gctx, gres, out, u_out,
+    ctx, cot, gn, unit_part,
+    gs, ga, mine, gq, gb, gh, gc, gt, gf, gv, gall,
     ua, uw, uc, ut, uz, uv, uall, uother,
-    sg, rg, su, ru, s1, r1, s2, r2, s3, r3, s4, r4,
+    sw, sg, rg, su, ru, s1, r1, s2, r2, s3, r3, s4, r4,
 ):
     z, core, xy = place()
     zl = lax.rem(z, 2)
     partner = at_core(flip(core))
     ring = [at_z(lax.rem(z + d, 4)) for d in range(1, 4)]
-    greet([*ring, partner], xy)
-    half = g.shape[2] // 2
-    width = g.shape[3]
-    chunk = 2 * half // 16
+    entered = greet([*ring, partner], xy)
+    width = stream.shape[-1]
+    quarter = width // 4
+    half = quarter // 2
+    chunk = quarter // 16
     wide = width // 4
-
-    u_core = remote(u.at[flip(core)], ua, su.at[0], ru.at[0], partner)
-    g_core = remote(g.at[:, flip(core)], ga, sg.at[0], rg.at[0], partner)
+    cut = width // 2
+    factor = logit_scale / math.sqrt(width)
+    load_ctx = pltpu.make_async_copy(context, ctx, sw.at[0])
+    load_cot = pltpu.make_async_copy(cotangent, cot, sw.at[1])
+    load_cot.start()
+    load_ctx.start()
+    unit32, norm = unit_of(slots)
+    unit = unit32.astype(BF16)
+    load_cot.wait()
+    for b in range(2):
+        ex = expo[b]
+        dispatch32 = ex / jnp.sum(ex, axis=1, keepdims=True)
+        combine32 = ex / jnp.sum(ex, axis=0, keepdims=True)
+        grad_in = back[1, 64 * b : 64 * b + 64]
+        grad_combine = times_t(back[0, 64 * b : 64 * b + 64], cot[b])
+        grad_dispatch = times_t(grad_in, normed[b])
+        grad_logits = combine32 * (
+            grad_combine - jnp.sum(combine32 * grad_combine, axis=0, keepdims=True)
+        )
+        grad_logits = grad_logits + dispatch32 * (
+            grad_dispatch - jnp.sum(dispatch32 * grad_dispatch, axis=1, keepdims=True)
+        )
+        grad_logits = grad_logits.astype(BF16)
+        part = times(grad_logits, normed[b])
+        for i in range(2):
+            rows = part[32 * i : 32 * i + 32]
+            unit_part[i] = rows if b == 0 else unit_part[i] + rows
+        gn[b] = t_times(dispatch32.astype(BF16), grad_in) + factor * t_times(grad_logits, unit)
+    entered()
+    u_core = remote(unit_part.at[flip(core)], ua, su.at[0], ru.at[0], partner)
     u_core.start()
-    g_core.start()
-
+
+    def settle(i, carry):
+        for b in range(2):
+            rows = pl.ds(pl.multiple_of(i * 64, 64), 64)
+            stream32 = stream[b, rows, :].astype(F32)
+            inverse = inverse_of(stream32)
+            normed32 = stream32 * inverse
+            grad = gn[b, rows, :]
+            pull = jnp.mean(normed32 * grad, axis=1, keepdims=True)
+            gres[b, rows, :] = (
+                cot[b, rows, :].astype(F32) + inverse * (grad - normed32 * pull)
+            ).astype(BF16)
+        return carry
+
+    lax.fori_loop(0, 4, settle, 0)
+
+    load_ctx.wait()
+
+    def proj(block, h):
+        left = ctx[:, :, pl.ds(pl.multiple_of(block * quarter, quarter), quarter)]
+        right = gres[:, :, cut * h : cut * h + cut]
+        return t_times(left.reshape(512, quarter), right.reshape(512, cut))
+
+    def g_core(h, i):
+        return remote(gs.at[h, i], ga.at[h, i], sg.at[h, i], rg.at[h, i], partner)
+
+    def g_mate(h):
+        return remote(
+            gq.at[h, pl.ds(0, half)], gb.at[h, pl.ds(0, half)], sg.at[h, 2], rg.at[h, 2], at_z(mate(z))
+        )
+
+    def g_cross(h):
+        return remote(
+            gq.at[h, pl.ds(half, half)],
+            gb.at[h, pl.ds(half, half)],
+            sg.at[h, 3],
+            rg.at[h, 3],
+            at_z(cross(z)),
+        )
+
+    def g_swap(h):
+        return (
+            xy,
+            lambda k: gh.at[h, pl.ds(pl.multiple_of(chunk * k, chunk), chunk)],
+            lambda k: gc.at[h, k],
+            s2.at[h],
+            r2.at[h],
+        )
+
+    def g_keep(h):
+        return pltpu.make_async_copy(g_swap(h)[1](xy), gc.at[h, xy], s2.at[h, 0])
+
+    def g_far(h):
+        return remote(gt.at[h], gf.at[h], sg.at[h, 4], rg.at[h, 4], at_z(far(z)))
+
+    def g_back(h):
+        return (xy, lambda k: gv.at[h], lambda k: gall.at[h, k], s4.at[h], r4.at[h])
+
+    def g_stay(h):
+        return pltpu.make_async_copy(gv.at[h], gall.at[h, xy], s4.at[h, 0])
+
+    blocks = (2 * flip(zl), 2 * zl)
     u_swap = (xy, lambda k: uw.at[k], lambda k: uc.at[k], s1, r1)
     u_keep = pltpu.make_async_copy(uw.at[xy], uc.at[xy], s1.at[0])
+
+    for h in range(2):
+        gs[h, 0] = proj(blocks[0] + flip(core), h).astype(BF16)
+        g_core(h, 0).start()
     u_core.wait()
     for i in range(4):
         for j in range(4):
-            where = (slice(8 * i, 8 * i + 8), slice(wide * j, wide * j + wide))
-            uw[4 * i + j] = u[core, where[0], where[1]] + ua[where[0], where[1]]
+            rows, columns = slice(8 * i, 8 * i + 8), slice(wide * j, wide * j + wide)
+            uw[4 * i + j] = unit_part[core, rows, columns] + ua[rows, columns]
     u_keep.start()
     xy_start(*u_swap)
-
-    g_core.wait()
-    gq[...] = (g[flip(zl), core].astype(F32) + ga[flip(zl)].astype(F32)).astype(BF16)
-    g_mate = remote(
-        gq.at[pl.ds(0, half)], gb.at[pl.ds(0, half)], sg.at[1], rg.at[1], at_z(mate(z))
-    )
-    g_cross = remote(
-        gq.at[pl.ds(half, half)], gb.at[pl.ds(half, half)], sg.at[2], rg.at[2], at_z(cross(z))
-    )
-    g_mate.start()
-    g_cross.start()
-
+    for h in range(2):
+        part = proj(blocks[0] + core, h)
+        g_core(h, 0).wait()
+        gq[h] = (part + ga[h, 0].astype(F32)).astype(BF16)
+        g_mate(h).start()
+        g_cross(h).start()
+    for h in range(2):
+        gs[h, 1] = proj(blocks[1] + flip(core), h).astype(BF16)
+        g_core(h, 1).start()
+    for h in range(2):
+        mine[h] = proj(blocks[1] + core, h)
     u_keep.wait()
     xy_wait(*u_swap)
     ut[...] = jnp.sum(uc[...], axis=0)
-    u_ring = [
-        remote(ut, uz.at[z], su.at[d + 1], ru.at[d + 1], ring[d]) for d in range(3)
-    ]
+    u_ring = [remote(ut, uz.at[z], su.at[d + 1], ru.at[d + 1], ring[d]) for d in range(3)]
     u_mine = pltpu.make_async_copy(ut, uz.at[z], su.at[4])
     u_mine.start()
     for copy in u_ring:
         copy.start()
 
-    g_mate.wait()
-    g_cross.wait()
-    gh[...] = (
-        g[zl, core].astype(F32) + ga[zl].astype(F32) + gb[...].astype(F32)
-    ).astype(BF16)
-    g_swap = (
-        xy,
-        lambda k: gh.at[pl.ds(pl.multiple_of(chunk * k, chunk), chunk)],
-        lambda k: gc.at[k],
-        s2,
-        r2,
-    )
-    g_keep = pltpu.make_async_copy(g_swap[1](xy), gc.at[xy], s2.at[0])
-    g_keep.start()
-    xy_start(*g_swap)
+    for h in range(2):
+        g_core(h, 1).wait()
+        g_mate(h).wait()
+        g_cross(h).wait()
+        gh[h] = (mine[h] + ga[h, 1].astype(F32) + gb[h].astype(F32)).astype(BF16)
+        g_keep(h).start()
+        xy_start(*g_swap(h))
+
+    for b in range(2):
+        for n in range(0, width, cut):
+            gctx[b, :, n : n + cut] = times_t(gres[b], whole[n : n + cut, :]).astype(BF16)
 
     u_mine.wait()
     for copy in u_ring:
@@ -593,64 +732,79 @@
     u_stay.start()
     xy_start(*u_back)
 
-    g_keep.wait()
-    xy_wait(*g_swap)
-    total = gc[0].astype(F32)
-    for k in range(1, 16):
-        total = total + gc[k].astype(F32)
-    gt[...] = total.astype(BF16)
-    g_far = remote(gt, gf, sg.at[3], rg.at[3], at_z(far(z)))
-    g_far.start()
+    for h in range(2):
+        g_keep(h).wait()
+        xy_wait(*g_swap(h))
+        total = gc[h, 0].astype(F32)
+        for k in range(1, 16):
+            total = total + gc[h, k].astype(F32)
+        gt[h] = total.astype(BF16)
+        g_far(h).start()
 
     u_stay.wait()
     xy_wait(*u_back)
     u_other = remote(uall, uother, su.at[5], ru.at[5], partner)
     u_other.start()
 
-    g_far.wait()
-    gv[...] = (gt[...].astype(F32) + gf[...].astype(F32)).astype(BF16)
-    g_back = (xy, lambda k: gv, lambda k: gall.at[k], s4, r4)
-    g_stay = pltpu.make_async_copy(gv, gall.at[xy], s4.at[0])
-    g_stay.start()
-    xy_start(*g_back)
+    for h in range(2):
+        g_far(h).wait()
+        gv[h] = (gt[h].astype(F32) + gf[h].astype(F32)).astype(BF16)
+        g_stay(h).start()
+        xy_start(*g_back(h))
 
     u_other.wait()
     for i in range(4):
         for j in range(4):
             columns = slice(wide * j, wide * j + wide)
             rows = slice(8 * i, 8 * i + 8)
-            u_out[core, rows, columns] = uall[4 * i + j]
-            u_out[flip(core), rows, columns] = uother[4 * i + j]
-    g_stay.wait()
-    xy_wait(*g_back)
-    for k in range(16):
-        out[chunk * k : chunk * k + chunk] = gall[k].astype(F32)
-
-
-def sums(partial, unit_partial):
-    width = partial.shape[-1]
-    rows = partial.shape[0] // 4
+            unit_part[core, rows, columns] = uall[4 * i + j]
+            unit_part[flip(core), rows, columns] = uother[4 * i + j]
+    grad_unit = factor * unit_part[...].reshape(64, width)
+    u_out[...] = (
+        grad_unit - unit32 * jnp.sum(unit32 * grad_unit, axis=1, keepdims=True)
+    ) / norm
+    for h in range(2):
+        g_stay(h).wait()
+        xy_wait(*g_back(h))
+        for k in range(16):
+            out[chunk * k : chunk * k + chunk, cut * h : cut * h + cut] = gall[h, k].astype(F32)
+
+
+def sums(back, stream, normed, expo, whole, slots, context, cotangent):
+    width = stream.shape[-1]
+    rows = width // 4
     chunk = rows // 16
     wide = width // 4
+    cut = width // 2
     dma = pltpu.SemaphoreType.DMA
+    here = pl.BlockSpec(memory_space=VMEM)
+    anywhere = pl.BlockSpec(memory_space=pl.ANY)
     return pl.pallas_call(
         sum_kernel,
         out_shape=(
+            jax.ShapeDtypeStruct(context.shape, BF16),
+            jax.ShapeDtypeStruct(context.shape, BF16),
             jax.ShapeDtypeStruct((rows, width), F32),
-            jax.ShapeDtypeStruct((2, 32, width), F32),
+            jax.ShapeDtypeStruct((64, width), F32),
         ),
-        in_specs=[pl.BlockSpec(memory_space=VMEM)] * 2,
-        out_specs=(pl.BlockSpec(memory_space=VMEM), pl.BlockSpec(memory_space=VMEM)),
+        in_specs=[here] * 6 + [anywhere] * 2,
+        out_specs=(here,) * 4,
         scratch_shapes=[
-            VMEM((2, rows, width), BF16),
-            VMEM((rows, width), BF16),
-            VMEM((rows, width), BF16),
-            VMEM((rows, width), BF16),
-            VMEM((16, chunk, width), BF16),
-            VMEM((chunk, width), BF16),
-            VMEM((chunk, width), BF16),
-            VMEM((chunk, width), BF16),
-            VMEM((16, chunk, width), BF16),
+            VMEM(context.shape, BF16),
+            VMEM(context.shape, BF16),
+            VMEM(context.shape, F32),
+            VMEM((2, 32, width), F32),
+            VMEM((2, 2, rows, cut), BF16),
+            VMEM((2, 2, rows, cut), BF16),
+            VMEM((2, rows, cut), F32),
+            VMEM((2, rows, cut), BF16),
+            VMEM((2, rows, cut), BF16),
+            VMEM((2, rows, cut), BF16),
+            VMEM((2, 16, chunk, cut), BF16),
+            VMEM((2, chunk, cut), BF16),
+            VMEM((2, chunk, cut), BF16),
+            VMEM((2, chunk, cut), BF16),
+            VMEM((2, 16, chunk, cut), BF16),
             VMEM((32, width), F32),
             VMEM((16, 8, wide), F32),
             VMEM((16, 8, wide), F32),
@@ -659,100 +813,34 @@
             VMEM((8, wide), F32),
             VMEM((16, 8, wide), F32),
             VMEM((16, 8, wide), F32),
-            dma((4,)),
-            dma((4,)),
+            dma((2,)),
+            dma((2, 5)),
+            dma((2, 5)),
             dma((6,)),
             dma((6,)),
-            *[dma((16,))] * 8,
+            dma((16,)),
+            dma((16,)),
+            dma((2, 16)),
+            dma((2, 16)),
+            dma((16,)),
+            dma((16,)),
+            dma((2, 16)),
+            dma((2, 16)),
         ],
-        compiler_params=params(4),
+        compiler_params=params(4, 36 << 20),
         name="sums",
-    )(partial.reshape(2, 2, rows, width), unit_partial.reshape(2, 32, width))
+    )(back, stream, normed, expo, whole, slots, context, cotangent)
 
 
 def shards(context, residual, cotangent, proj_weight, slot_params, expert_in, expert_out):
-    images, tokens, width = context.shape
-    rows = images * tokens
-    slots = slot_params.shape[1]
-    factor = logit_scale / math.sqrt(width)
-    flat_ctx = context.reshape(rows, width)
-    weight = whole_weight(proj_weight)
-    mixed = jnp.dot(flat_ctx, weight, preferred_element_type=jnp.float32)
-    stream = (residual.reshape(rows, width).astype(jnp.float32) + mixed).astype(jnp.bfloat16)
-    stream32 = stream.astype(jnp.float32)
-    inverse = lax.rsqrt(jnp.mean(stream32 * stream32, axis=-1, keepdims=True) + epsilon)
-    normed32 = stream32 * inverse
-    normed = normed32.astype(jnp.bfloat16)
-    params32 = slot_params.astype(jnp.float32)
-    slot_norm = jnp.sqrt(jnp.sum(params32 * params32, axis=0, keepdims=True) + epsilon)
-    unit32 = params32 / slot_norm
-    unit = unit32.astype(jnp.bfloat16)
-    logits = factor * jnp.dot(normed, unit, preferred_element_type=jnp.float32)
-    logits = logits.reshape(images, tokens, -1)
-    expo = jnp.exp(logits)
-    dispatch32 = expo / jnp.sum(expo, axis=1, keepdims=True)
-    combine32 = expo / jnp.sum(expo, axis=2, keepdims=True)
-    dispatch = dispatch32.astype(jnp.bfloat16)
-    combine = combine32.astype(jnp.bfloat16)
-    normed3 = normed.reshape(images, tokens, width)
-    slot_in = jnp.einsum(
-        "bms,bmd->bsd", dispatch, normed3, preferred_element_type=jnp.float32
-    ).astype(jnp.bfloat16)
-    grad_slot_out = jnp.einsum(
-        "bms,bmd->bsd", combine, cotangent, preferred_element_type=jnp.float32
-    ).astype(jnp.bfloat16)
-    returned, grad_expert_in, grad_expert_out = experts(
-        slot_in.reshape(images * slots, width),
-        grad_slot_out.reshape(images * slots, width),
-        expert_in,
-        expert_out,
-    )
-    returned = returned.reshape(2, images, slots, width)
-    slot_out, grad_slot_in = returned[0], returned[1]
-    grad_combine = jnp.einsum(
-        "bmd,bsd->bms", cotangent, slot_out, preferred_element_type=jnp.float32
-    )
-    grad_dispatch = jnp.einsum(
-        "bmd,bsd->bms", normed3, grad_slot_in, preferred_element_type=jnp.float32
-    )
-    grad_logits32 = combine32 * (
-        grad_combine - jnp.sum(combine32 * grad_combine, axis=2, keepdims=True)
-    )
-    grad_logits32 = grad_logits32 + dispatch32 * (
-        grad_dispatch - jnp.sum(dispatch32 * grad_dispatch, axis=1, keepdims=True)
-    )
-    grad_logits = grad_logits32.astype(jnp.bfloat16).reshape(rows, -1)
-    grad_normed = jnp.einsum(
-        "bms,bsd->bmd", dispatch, grad_slot_in, preferred_element_type=jnp.float32
-    ).reshape(rows, width)
-    grad_normed = grad_normed + factor * jnp.dot(
-        grad_logits, unit.T, preferred_element_type=jnp.float32
-    )
-    local_unit = jnp.dot(grad_logits.T, normed, preferred_element_type=jnp.float32)
-    upstream = cotangent.reshape(rows, width).astype(jnp.float32)
-    grad_stream = upstream + inverse * (
-        grad_normed - normed32 * jnp.mean(normed32 * grad_normed, axis=-1, keepdims=True)
-    )
-    grad_residual = grad_stream.astype(jnp.bfloat16)
-    grad_context = jnp.dot(
-        grad_residual, weight.T, preferred_element_type=jnp.float32
-    ).astype(jnp.bfloat16)
-    partial = jnp.dot(
-        flat_ctx.T, grad_residual, preferred_element_type=jnp.float32
-    ).astype(jnp.bfloat16)
-    grad_proj, unit_sum = sums(partial, local_unit)
-    grad_unit = factor * unit_sum.reshape(slots, width).T
-    grad_slots = (
-        grad_unit - unit32 * jnp.sum(unit32 * grad_unit, axis=0, keepdims=True)
-    ) / slot_norm
-    return (
-        grad_context.reshape(images, tokens, width),
-        grad_residual.reshape(images, tokens, width),
-        grad_proj,
-        grad_slots,
-        grad_expert_in,
-        grad_expert_out,
-    )
+    slots = slot_params.T
+    back, stream, normed, expo, whole, grad_expert_in, grad_expert_out = experts(
+        context, residual, cotangent, proj_weight, slots, expert_in, expert_out
+    )
+    grad_context, grad_residual, grad_proj, grad_slots = sums(
+        back, stream, normed, expo, whole, slots, context, cotangent
+    )
+    return grad_context, grad_residual, grad_proj, grad_slots.T, grad_expert_in, grad_expert_out
 
 
 def solution(mesh):

time: 138 us -> 115 us (0.83)
  matrix products: 15.3 us -> 0 us
  other arithmetic: 4.41 us -> 0 us
  Pallas kernels: 104 us -> 101 us
    pallas_call x2 -> x1, Pallas kernels: 49 us -> 31.9 us  [sums(): pl.pallas_call(sum_kernel, out_shape=(jax.ShapeDtypeStruct(context.shape,...]
    pallas_call x1, Pallas kernels: 55 us -> 69.5 us  [experts(): pl.pallas_call(expert_kernel, out_shape=(jax.ShapeDtypeStruct((2, 128, wi...]
    dot_general x10 -> x0, matrix products: 12.8 us -> none  [the longest x1 2.28 us: shards(): jnp.dot(grad_residual, weight.T, preferred_element_type=jnp.float32)]
    sub x1 -> x0, matrix products: 2.49 us -> none  [shards(): grad_dispatch - jnp.sum(dispatch32 * grad_dispatch, axis=1, keepdims=True)]
    reduce_sum x3 -> x0, other arithmetic: 2 us -> none  [the longest x1 1.03 us: shards(): jnp.sum(params32 * params32, axis=0, keepdims=True) + epsilon]
    unnamed x27 -> x20, local copies, waits for them, and re-layouts: 11.4 us -> 12.9 us
where the time goes in v3:
time: 115 us
  Pallas kernels  101 us (88%)
  local copies, waits for them, and re-layouts  12.9 us (11%)
    pallas_call x1, Pallas kernels, experts(): pl.pallas_call(expert_kernel, out_shape=(jax.ShapeDtypeStruct((2, 128, wi...  69.5 us
    pallas_call x1, Pallas kernels, sums(): pl.pallas_call(sum_kernel, out_shape=(jax.ShapeDtypeStruct(context.shape,...  31.9 us
    unnamed x20, local copies, waits for them, and re-layouts  12.9 us

profile of v3, /device:TPU:0, one launch (start us, length us, event | category | flops | bytes accessed | tf_op | source)
XLA Modules:
  0.0 115.0 jit_solution(7186736593314986857)
XLA Ops:
  0.6 0.0 copy-start.3
  0.6 0.9 copy-done.3
  1.5 0.0 copy-start.4
  1.5 1.0 copy-done.4
  2.6 0.0 copy-start
  2.6 0.0 copy-start.1
  2.6 69.5 %experts.1 = (bf16[2,128,1024]{2,1,0:T(8,128)(2,1)S(1)}, bf16[2,256,1024]{2,1,0:T(8,128)(2,1)S(1)}, bf16[2,256,1024]{2,1,0:T(8,128)(2,1)S(1)}, f32[2,64,256]{2,1...) custom-call(bf16[2,256,1024]{2,1,0:T(8,128)(2,1)} %context.3, ...), custom_call_target="tpu_custom_call" | custom-call | tf_op jit(solution)/shard_map/experts/pallas_call | solution.py:513
  72.1 0.0 copy-done
  72.1 0.0 copy-done.1
  72.1 0.0 copy-start.2
  72.1 1.6 %copy-done.2 = bf16[1024,1024]{1,0:T(8,128)(2,1)S(1)} copy-done((bf16[1024,1024]{1,0:T(8,128)(2,1)S(1)}, bf16[1024,1024]{1,0:T(8,128)(2,1)}, u32[]{:S(2)}) %copy-start.2) | copy-done | bytes 2097176
  73.7 31.9 %sums.1 = (bf16[2,256,1024]{2,1,0:T(8,128)(2,1)S(1)}, bf16[2,256,1024]{2,1,0:T(8,128)(2,1)S(1)}, f32[256,1024]{1,0:T(8,128)S(1)}, f32[64,1024]{1,0:T(8,128)S(1)}) custom-call(bf16[2,128,1024]{2,1,0:T(8,128)(2,1)S(1)} %get-tuple-element.17.back, bf16[2,256,1024]{2,1,0:T(8,128)(2,1)S(1)} %get-tuple-element.18.stream, ...), custom_call_target="tpu_custom_call" | custom-call | tf_op jit(solution)/shard_map/sums/pallas_call | solution.py:782
  105.6 0.0 copy-start.6
  105.6 1.0 copy.19
  106.6 1.0 copy.20
  107.6 1.0 copy.21
  108.5 0.7 copy.22
  109.2 0.0 copy-done.6
  109.2 0.0 copy-start.5
  109.3 2.1 %copy.23 = bf16[2,1024,1024]{2,1,0:T(8,128)(2,1)} copy(bf16[2,1024,1024]{2,1,0:T(8,128)(2,1)S(1)} %copy-done.6) | data formatting | bytes 8388608
  111.4 1.6 %copy-done.5 = bf16[2,1024,1024]{2,1,0:T(8,128)(2,1)S(1)} copy-done((bf16[2,1024,1024]{2,1,0:T(8,128)(2,1)S(1)}, bf16[2,1024,1024]{2,1,0:T(8,128)(2,1)}, u32[]{:S(2)}) %copy-start.5) | copy-done | bytes 4194328
  113.0 2.0 %copy.24 = bf16[2,1024,1024]{2,1,0:T(8,128)(2,1)} copy(bf16[2,1024,1024]{2,1,0:T(8,128)(2,1)S(1)} %copy-done.5) | data formatting | bytes 8388608
Async XLA Ops:
  0.6 0.9 copy-start.3
  1.5 1.0 copy-start.4
  2.6 69.5 %copy-start = (bf16[2,256,1024]{2,1,0:T(8,128)(2,1)S(1)}, bf16[2,256,1024]{2,1,0:T(8,128)(2,1)}, u32[]{:S(2)}) copy-start(bf16[2,256,1024]{2,1,0:T(8,128)(2,1)} %context.3) | copy-start | bytes 3145732
  2.6 69.5 %copy-start.1 = (bf16[2,256,1024]{2,1,0:T(8,128)(2,1)S(1)}, bf16[2,256,1024]{2,1,0:T(8,128)(2,1)}, u32[]{:S(2)}) copy-start(bf16[2,256,1024]{2,1,0:T(8,128)(2,1)} %cotangent.3) | copy-start | bytes 3145732
  72.1 1.6 %copy-start.2 = (bf16[1024,1024]{1,0:T(8,128)(2,1)S(1)}, bf16[1024,1024]{1,0:T(8,128)(2,1)}, u32[]{:S(2)}) copy-start(bf16[1024,1024]{1,0:T(8,128)(2,1)} %get-tuple-element.21.whole) | copy-start | bytes 6291460
  105.6 3.6 %copy-start.6 = (bf16[2,1024,1024]{2,1,0:T(8,128)(2,1)S(1)}, bf16[2,1024,1024]{2,1,0:T(8,128)(2,1)}, u32[]{:S(2)}) copy-start(bf16[2,1024,1024]{2,1,0:T(8,128)(2,1)} %get-tuple-element.38) | copy-start | bytes 12582916
  109.2 3.7 %copy-start.5 = (bf16[2,1024,1024]{2,1,0:T(8,128)(2,1)S(1)}, bf16[2,1024,1024]{2,1,0:T(8,128)(2,1)}, u32[]{:S(2)}) copy-start(bf16[2,1024,1024]{2,1,0:T(8,128)(2,1)} %get-tuple-element.39) | copy-start | bytes 12582916

commit v4 on v3

--- a/solution.py
+++ b/solution.py
@@ -157,6 +157,9 @@
     return lax.dot_general(a, b, (((0,), (0,)), ((), ())), preferred_element_type=F32)
 
 
+PIECES = 4
+
+
 def unit_of(slots_ref):
     params32 = slots_ref[...].astype(F32)
     norm = jnp.sqrt(jnp.sum(params32 * params32, axis=1, keepdims=True) + epsilon)
@@ -169,11 +172,11 @@
 
 def expert_kernel(
     context, residual, cotangent, own, slots, win, wout,
-    out, stream, normed, expo, whole, gin, gout,
-    ctx, res, cot, natural,
-    pairs, came, blocks, x, wi, wo, act, slope, gpre, o,
-    halves, chip, paired, crossing, blocks2, pairs2, came2, gi, go,
-    s1, r1, s2, r2, sa, ra, sb, rb, sc, rc, sw, sg, sp, rp,
+    out, stream, normed, expo, whole, x, act, gpre,
+    ctx, res, cot, slots_here, natural,
+    pairs, came, blocks, wi, wo, slope, o,
+    halves, chip, paired, crossing, blocks2, pairs2, came2,
+    s1, r1, s2, r2, sa, ra, sb, rb, sc, rc, sw, sp, rp,
 ):
     z, core, xy = place()
     zh = lax.div(z, 2)
@@ -195,10 +198,13 @@
     load_cot = pltpu.make_async_copy(cotangent, cot, sw.at[5])
     load_in = pltpu.make_async_copy(win, wi, sw.at[0])
     load_out = pltpu.make_async_copy(wout, wo, sw.at[1])
+    load_slots = pltpu.make_async_copy(slots, slots_here, sw.at[6])
+    load_slots.start()
     load_own.start()
     load_ctx.start()
     load_res.start()
-    unit32, _ = unit_of(slots)
+    load_slots.wait()
+    unit32, _ = unit_of(slots_here)
     unit = unit32.astype(BF16)
     entered()
 
@@ -455,19 +461,6 @@
         xy_wait(*home_swap(kind))
         out[kind] = reorder(from_pairs, came2[kind])
 
-    def out_gradient(e):
-        right = rows_of(1, e)
-        for n in range(0, hidden, cut):
-            go[e, n : n + cut, :] = t_times(act[e, :, n : n + cut], right).astype(BF16)
-        pltpu.make_async_copy(go.at[e], gout.at[e], sg.at[0, e]).start()
-
-    def in_gradient(e):
-        left = rows_of(0, e)
-        right = gpre[e]
-        for n in range(0, width, cut):
-            gi[e, n : n + cut, :] = t_times(left[:, n : n + cut], right).astype(BF16)
-        pltpu.make_async_copy(gi.at[e], gin.at[e], sg.at[1, e]).start()
-
     up(0)
     up(1)
     relay_last(1)
@@ -481,15 +474,11 @@
     for e in range(2):
         back_up(e)
         home_core(1, e).start()
-    out_gradient(0)
     chip_sum(1)
     pair_sum(0)
-    out_gradient(1)
     pair_sum(1)
     home(0)
-    in_gradient(0)
     home(1)
-    in_gradient(1)
     landed(0)
     landed(1)
     for copy in (w_mate, w_cross, w_core, w_first, w_second):
@@ -499,17 +488,14 @@
         for copy in home_mate(kind):
             copy.wait_send()
         home_cross(kind).wait_send()
-    for e in range(2):
-        pltpu.make_async_copy(go.at[e], gout.at[e], sg.at[0, e]).wait()
-        pltpu.make_async_copy(gi.at[e], gin.at[e], sg.at[1, e]).wait()
 
 
 def experts(context, residual, cotangent, own, slots, expert_in, expert_out):
     width = context.shape[-1]
     hidden = expert_in.shape[-1]
     dma = pltpu.SemaphoreType.DMA
-    whole = pl.BlockSpec(memory_space=VMEM)
-    anywhere = pl.BlockSpec(memory_space=pl.ANY)
+    here = pl.BlockSpec(memory_space=VMEM)
+    afar = pl.BlockSpec(memory_space=pltpu.HBM)
     return pl.pallas_call(
         expert_kernel,
         out_shape=(
@@ -518,25 +504,24 @@
             jax.ShapeDtypeStruct(context.shape, BF16),
             jax.ShapeDtypeStruct((2, 64, 256), F32),
             jax.ShapeDtypeStruct((width, width), BF16),
-            jax.ShapeDtypeStruct(expert_in.shape, BF16),
-            jax.ShapeDtypeStruct(expert_out.shape, BF16),
+            jax.ShapeDtypeStruct((2, 2, 4, 2, 32, width), BF16),
+            jax.ShapeDtypeStruct((2, 256, hidden), BF16),
+            jax.ShapeDtypeStruct((2, 256, hidden), BF16),
         ),
-        in_specs=[anywhere] * 4 + [whole] + [anywhere] * 2,
-        out_specs=(whole,) * 5 + (anywhere,) * 2,
+        in_specs=[afar] * 7,
+        out_specs=(here,) * 8,
         scratch_shapes=[
             VMEM(context.shape, BF16),
             VMEM(context.shape, BF16),
             VMEM(context.shape, BF16),
+            VMEM(slots.shape, BF16),
             VMEM((2, 128, width), BF16),
             VMEM((2, 128, width), BF16),
             VMEM((2, 128, width), BF16),
             VMEM((2, 2, 2, 32, width), BF16),
-            VMEM((2, 2, 4, 2, 32, width), BF16),
             VMEM(expert_in.shape, BF16),
             VMEM(expert_out.shape, BF16),
-            VMEM((2, 256, hidden), BF16),
             VMEM((2, 256, hidden), F32),
-            VMEM((2, 256, hidden), BF16),
             VMEM((2, 2, 4, 2, 32, width), BF16),
             VMEM((2, 2, 4, 32, width), BF16),
             VMEM((2, 4, 2, 32, width), BF16),
@@ -545,8 +530,6 @@
             VMEM((2, 2, 2, 32, width), BF16),
             VMEM((2, 128, width), BF16),
             VMEM((2, 128, width), BF16),
-            VMEM(expert_in.shape, BF16),
-            VMEM(expert_out.shape, BF16),
             dma((2, 16)),
             dma((2, 16)),
             dma((2, 8)),
@@ -557,12 +540,11 @@
             dma((2, 3)),
             dma((2, 16)),
             dma((2, 16)),
-            dma((6,)),
-            dma((2, 2)),
+            dma((7,)),
             dma((5,)),
             dma((5,)),
         ],
-        compiler_params=params(2, 50 << 20),
+        compiler_params=params(2, 36 << 20),
         name="experts",
     )(context, residual, cotangent, own, slots, expert_in, expert_out)
 
@@ -570,7 +552,7 @@
 def sum_kernel(
     back, stream, normed, expo, whole, slots, context, cotangent,
     gctx, gres, out, u_out,
-    ctx, cot, gn, unit_part,
+    ctx, cot, slots_here, gn, unit_part,
     gs, ga, mine, gq, gb, gh, gc, gt, gf, gv, gall,
     ua, uw, uc, ut, uz, uv, uall, uother,
     sw, sg, rg, su, ru, s1, r1, s2, r2, s3, r3, s4, r4,
@@ -585,13 +567,16 @@
     half = quarter // 2
     chunk = quarter // 16
     wide = width // 4
-    cut = width // 2
+    cut = width // PIECES
     factor = logit_scale / math.sqrt(width)
     load_ctx = pltpu.make_async_copy(context, ctx, sw.at[0])
     load_cot = pltpu.make_async_copy(cotangent, cot, sw.at[1])
+    load_slots = pltpu.make_async_copy(slots, slots_here, sw.at[2])
+    load_slots.start()
     load_cot.start()
     load_ctx.start()
-    unit32, norm = unit_of(slots)
+    load_slots.wait()
+    unit32, norm = unit_of(slots_here)
     unit = unit32.astype(BF16)
     load_cot.wait()
     for b in range(2):
@@ -681,7 +666,8 @@
     u_swap = (xy, lambda k: uw.at[k], lambda k: uc.at[k], s1, r1)
     u_keep = pltpu.make_async_copy(uw.at[xy], uc.at[xy], s1.at[0])
 
-    for h in range(2):
+    pieces = range(PIECES)
+    for h in pieces:
         gs[h, 0] = proj(blocks[0] + flip(core), h).astype(BF16)
         g_core(h, 0).start()
     u_core.wait()
@@ -691,27 +677,46 @@
             uw[4 * i + j] = unit_part[core, rows, columns] + ua[rows, columns]
     u_keep.start()
     xy_start(*u_swap)
-    for h in range(2):
+    for h in pieces:
         part = proj(blocks[0] + core, h)
         g_core(h, 0).wait()
         gq[h] = (part + ga[h, 0].astype(F32)).astype(BF16)
         g_mate(h).start()
         g_cross(h).start()
-    for h in range(2):
+    for h in pieces:
         gs[h, 1] = proj(blocks[1] + flip(core), h).astype(BF16)
         g_core(h, 1).start()
-    for h in range(2):
+    for h in pieces:
         mine[h] = proj(blocks[1] + core, h)
-    u_keep.wait()
-    xy_wait(*u_swap)
-    ut[...] = jnp.sum(uc[...], axis=0)
+
     u_ring = [remote(ut, uz.at[z], su.at[d + 1], ru.at[d + 1], ring[d]) for d in range(3)]
     u_mine = pltpu.make_async_copy(ut, uz.at[z], su.at[4])
-    u_mine.start()
-    for copy in u_ring:
-        copy.start()
-
-    for h in range(2):
+    u_back = (xy, lambda k: uv, lambda k: uall.at[k], s3, r3)
+    u_stay = pltpu.make_async_copy(uv, uall.at[xy], s3.at[0])
+    u_other = remote(uall, uother, su.at[5], ru.at[5], partner)
+
+    def u_first():
+        u_keep.wait()
+        xy_wait(*u_swap)
+        ut[...] = jnp.sum(uc[...], axis=0)
+        u_mine.start()
+        for copy in u_ring:
+            copy.start()
+
+    def u_second():
+        u_mine.wait()
+        for copy in u_ring:
+            copy.wait()
+        uv[...] = jnp.sum(uz[...], axis=0)
+        u_stay.start()
+        xy_start(*u_back)
+
+    def u_third():
+        u_stay.wait()
+        xy_wait(*u_back)
+        u_other.start()
+
+    def chip_rows(h):
         g_core(h, 1).wait()
         g_mate(h).wait()
         g_cross(h).wait()
@@ -719,20 +724,7 @@
         g_keep(h).start()
         xy_start(*g_swap(h))
 
-    for b in range(2):
-        for n in range(0, width, cut):
-            gctx[b, :, n : n + cut] = times_t(gres[b], whole[n : n + cut, :]).astype(BF16)
-
-    u_mine.wait()
-    for copy in u_ring:
-        copy.wait()
-    uv[...] = jnp.sum(uz[...], axis=0)
-    u_back = (xy, lambda k: uv, lambda k: uall.at[k], s3, r3)
-    u_stay = pltpu.make_async_copy(uv, uall.at[xy], s3.at[0])
-    u_stay.start()
-    xy_start(*u_back)
-
-    for h in range(2):
+    def plane_sum(h):
         g_keep(h).wait()
         xy_wait(*g_swap(h))
         total = gc[h, 0].astype(F32)
@@ -741,17 +733,35 @@
         gt[h] = total.astype(BF16)
         g_far(h).start()
 
-    u_stay.wait()
-    xy_wait(*u_back)
-    u_other = remote(uall, uother, su.at[5], ru.at[5], partner)
-    u_other.start()
-
-    for h in range(2):
+    def far_sum(h):
         g_far(h).wait()
         gv[h] = (gt[h].astype(F32) + gf[h].astype(F32)).astype(BF16)
         g_stay(h).start()
         xy_start(*g_back(h))
 
+    def finish(h):
+        g_stay(h).wait()
+        xy_wait(*g_back(h))
+        for k in range(16):
+            out[chunk * k : chunk * k + chunk, cut * h : cut * h + cut] = gall[h, k].astype(F32)
+
+    def grad_context(h):
+        for b in range(2):
+            columns = slice(cut * h, cut * h + cut)
+            gctx[b, :, columns] = times_t(gres[b], whole[columns, :]).astype(BF16)
+
+    for h in pieces:
+        chip_rows(h)
+        if h == 0:
+            u_first()
+        grad_context(h)
+    u_second()
+    for h in pieces:
+        plane_sum(h)
+        if h:
+            far_sum(h - 1)
+    far_sum(PIECES - 1)
+    u_third()
     u_other.wait()
     for i in range(4):
         for j in range(4):
@@ -763,11 +773,8 @@
     u_out[...] = (
         grad_unit - unit32 * jnp.sum(unit32 * grad_unit, axis=1, keepdims=True)
     ) / norm
-    for h in range(2):
-        g_stay(h).wait()
-        xy_wait(*g_back(h))
-        for k in range(16):
-            out[chunk * k : chunk * k + chunk, cut * h : cut * h + cut] = gall[h, k].astype(F32)
+    for h in pieces:
+        finish(h)
 
 
 def sums(back, stream, normed, expo, whole, slots, context, cotangent):
@@ -775,10 +782,10 @@
     rows = width // 4
     chunk = rows // 16
     wide = width // 4
-    cut = width // 2
+    cut = width // PIECES
     dma = pltpu.SemaphoreType.DMA
     here = pl.BlockSpec(memory_space=VMEM)
-    anywhere = pl.BlockSpec(memory_space=pl.ANY)
+    afar = pl.BlockSpec(memory_space=pltpu.HBM)
     return pl.pallas_call(
         sum_kernel,
         out_shape=(
@@ -787,24 +794,25 @@
             jax.ShapeDtypeStruct((rows, width), F32),
             jax.ShapeDtypeStruct((64, width), F32),
         ),
-        in_specs=[here] * 6 + [anywhere] * 2,
+        in_specs=[here] * 5 + [afar] * 3,
         out_specs=(here,) * 4,
         scratch_shapes=[
             VMEM(context.shape, BF16),
             VMEM(context.shape, BF16),
+            VMEM(slots.shape, BF16),
             VMEM(context.shape, F32),
             VMEM((2, 32, width), F32),
-            VMEM((2, 2, rows, cut), BF16),
-            VMEM((2, 2, rows, cut), BF16),
-            VMEM((2, rows, cut), F32),
-            VMEM((2, rows, cut), BF16),
-            VMEM((2, rows, cut), BF16),
-            VMEM((2, rows, cut), BF16),
-            VMEM((2, 16, chunk, cut), BF16),
-            VMEM((2, chunk, cut), BF16),
-            VMEM((2, chunk, cut), BF16),
-            VMEM((2, chunk, cut), BF16),
-            VMEM((2, 16, chunk, cut), BF16),
+            VMEM((PIECES, 2, rows, cut), BF16),
+            VMEM((PIECES, 2, rows, cut), BF16),
+            VMEM((PIECES, rows, cut), F32),
+            VMEM((PIECES, rows, cut), BF16),
+            VMEM((PIECES, rows, cut), BF16),
+            VMEM((PIECES, rows, cut), BF16),
+            VMEM((PIECES, 16, chunk, cut), BF16),
+            VMEM((PIECES, chunk, cut), BF16),
+            VMEM((PIECES, chunk, cut), BF16),
+            VMEM((PIECES, chunk, cut), BF16),
+            VMEM((PIECES, 16, chunk, cut), BF16),
             VMEM((32, width), F32),
             VMEM((16, 8, wide), F32),
             VMEM((16, 8, wide), F32),
@@ -813,34 +821,101 @@
             VMEM((8, wide), F32),
             VMEM((16, 8, wide), F32),
             VMEM((16, 8, wide), F32),
-            dma((2,)),
-            dma((2, 5)),
-            dma((2, 5)),
+            dma((3,)),
+            dma((PIECES, 5)),
+            dma((PIECES, 5)),
             dma((6,)),
             dma((6,)),
             dma((16,)),
             dma((16,)),
-            dma((2, 16)),
-            dma((2, 16)),
+            dma((PIECES, 16)),
+            dma((PIECES, 16)),
             dma((16,)),
             dma((16,)),
-            dma((2, 16)),
-            dma((2, 16)),
+            dma((PIECES, 16)),
+            dma((PIECES, 16)),
         ],
-        compiler_params=params(4, 36 << 20),
+        compiler_params=params(4, 28 << 20),
         name="sums",
     )(back, stream, normed, expo, whole, slots, context, cotangent)
 
 
+def result_kernel(
+    x, act, gpre, gctx, gres, gproj, gslots,
+    to_ctx, to_res, to_proj, to_slots, to_in, to_out,
+    gi, go, sem, wsem,
+):
+    width = x.shape[-1]
+    cut = width // 2
+    ready = [
+        pltpu.make_async_copy(src, dst, sem.at[i])
+        for i, (src, dst) in enumerate(
+            ((gctx, to_ctx), (gres, to_res), (gproj, to_proj), (gslots, to_slots))
+        )
+    ]
+    for copy in ready:
+        copy.start()
+    copies = []
+    for e in range(2):
+        first, second = (x[kind, e].reshape(256, width) for kind in range(2))
+        for i in range(2):
+            rows = pl.ds(cut * i, cut)
+            go[e, rows, :] = t_times(act[e, :, rows], second).astype(BF16)
+            copies.append(
+                pltpu.make_async_copy(go.at[e, rows], to_out.at[e, rows], wsem.at[0, e, i])
+            )
+            copies[-1].start()
+            gi[e, rows, :] = t_times(first[:, cut * i : cut * i + cut], gpre[e]).astype(BF16)
+            copies.append(
+                pltpu.make_async_copy(gi.at[e, rows], to_in.at[e, rows], wsem.at[1, e, i])
+            )
+            copies[-1].start()
+    for copy in ready + copies:
+        copy.wait()
+
+
+def results(x, act, gpre, gctx, gres, gproj, gslots):
+    width = x.shape[-1]
+    hidden = act.shape[-1]
+    dma = pltpu.SemaphoreType.DMA
+    afar = pl.BlockSpec(memory_space=pltpu.HBM)
+    shapes = (
+        jax.ShapeDtypeStruct((2, width, hidden), BF16),
+        jax.ShapeDtypeStruct((2, hidden, width), BF16),
+    )
+    return pl.pallas_call(
+        result_kernel,
+        out_shape=tuple(
+            jax.ShapeDtypeStruct(a.shape, a.dtype) for a in (gctx, gres, gproj, gslots)
+        )
+        + shapes,
+        in_specs=[pl.BlockSpec(memory_space=VMEM)] * 7,
+        out_specs=(afar,) * 6,
+        scratch_shapes=[
+            VMEM(shapes[0].shape, BF16),
+            VMEM(shapes[1].shape, BF16),
+            dma((4,)),
+            dma((2, 2, 2)),
+        ],
+        compiler_params=pltpu.CompilerParams(vmem_limit_bytes=24 << 20),
+        name="results",
+    )(x, act, gpre, gctx, gres, gproj, gslots)
+
+
 def shards(context, residual, cotangent, proj_weight, slot_params, expert_in, expert_out):
     slots = slot_params.T
-    back, stream, normed, expo, whole, grad_expert_in, grad_expert_out = experts(
+    context, residual, cotangent, proj_weight, slots, expert_in, expert_out = (
+        pltpu.with_memory_space_constraint(a, pltpu.HBM)
+        for a in (context, residual, cotangent, proj_weight, slots, expert_in, expert_out)
+    )
+    back, stream, normed, expo, whole, x, act, gpre = experts(
         context, residual, cotangent, proj_weight, slots, expert_in, expert_out
     )
-    grad_context, grad_residual, grad_proj, grad_slots = sums(
-        back, stream, normed, expo, whole, slots, context, cotangent
-    )
-    return grad_context, grad_residual, grad_proj, grad_slots.T, grad_expert_in, grad_expert_out
+    four = sums(back, stream, normed, expo, whole, slots, context, cotangent)
+    grad_context, grad_residual, grad_proj, grad_slots, grad_in, grad_out = results(
+        x, act, gpre, *four
+    )
+    return grad_context, grad_residual, grad_proj, grad_slots.T, grad_in, grad_out
 
 
 def solution(mesh):

time: 115 us -> 107 us (0.930)
  local copies, waits for them, and re-layouts: 12.9 us -> 0 us
  Pallas kernels: 101 us -> 106 us
    unnamed x20 -> x0, local copies, waits for them, and re-layouts: 12.9 us -> none
    pallas_call x0 -> x1, Pallas kernels: none -> 4.43 us  [results(): pl.pallas_call(result_kernel, out_shape=tuple((jax.ShapeDtypeStruct(a.sha...]
    pallas_call x1, Pallas kernels: 31.9 us -> 33.3 us  [sums(): pl.pallas_call(sum_kernel, out_shape=(jax.ShapeDtypeStruct(context.shape,...]
where the time goes in v4:
time: 107 us
  Pallas kernels  106 us (99%)
    pallas_call x1, Pallas kernels, experts(): pl.pallas_call(expert_kernel, out_shape=(jax.ShapeDtypeStruct((2, 128, wi...  68.5 us
    pallas_call x1, Pallas kernels, sums(): pl.pallas_call(sum_kernel, out_shape=(jax.ShapeDtypeStruct(context.shape,...  33.3 us
    pallas_call x1, Pallas kernels, results(): pl.pallas_call(result_kernel, out_shape=tuple((jax.ShapeDtypeStruct(a.sha...  4.43 us

profile of v4, /device:TPU:0, one launch (start us, length us, event | category | flops | bytes accessed | tf_op | source)
XLA Modules:
  0.0 107.1 jit_solution(7232283024868702466)
XLA Ops:
  0.6 68.5 %experts.1 = (bf16[2,128,1024]{2,1,0:T(8,128)(2,1)S(1)}, bf16[2,256,1024]{2,1,0:T(8,128)(2,1)S(1)}, bf16[2,256,1024]{2,1,0:T(8,128)(2,1)S(1)}, f32[2,64,256]{2,1...) custom-call(bf16[2,256,1024]{2,1,0:T(8,128)(2,1)} %context.3, ...), custom_call_target="tpu_custom_call" | custom-call | tf_op jit(solution)/shard_map/experts/pallas_call | solution.py:499
  69.2 33.3 %sums.1 = (bf16[2,256,1024]{2,1,0:T(8,128)(2,1)S(1)}, bf16[2,256,1024]{2,1,0:T(8,128)(2,1)S(1)}, f32[256,1024]{1,0:T(8,128)S(1)}, f32[64,1024]{1,0:T(8,128)S(1)}) custom-call(bf16[2,128,1024]{2,1,0:T(8,128)(2,1)S(1)} %get-tuple-element.27.back, bf16[2,256,1024]{2,1,0:T(8,128)(2,1)S(1)} %get-tuple-element.28.stream, ...), custom_call_target="tpu_custom_call" | custom-call | tf_op jit(solution)/shard_map/sums/pallas_call | solution.py:789
  102.5 4.4 %results.1 = (bf16[2,256,1024]{2,1,0:T(8,128)(2,1)}, bf16[2,256,1024]{2,1,0:T(8,128)(2,1)}, f32[256,1024]{1,0:T(8,128)}, f32[64,1024]{1,0:T(8,128)}, bf16[2,1024...) custom-call(bf16[2,2,4,2,32,1024]{5,4,3,2,1,0:T(8,128)(2,1)S(1)} %get-tuple-element.24.x, ...), custom_call_target="tpu_custom_call" | custom-call | tf_op jit(solution)/shard_map/results/pallas_call | solution.py:886

commit v5 on v4

--- a/solution.py
+++ b/solution.py
@@ -61,7 +61,7 @@
     )
 
 
-def greet(devices, xy):
+def greet(devices, xy=None):
     barrier = pltpu.get_barrier_semaphore()
     for device in devices:
         pl.semaphore_signal(barrier, inc=1, device_id=device, device_id_type=MESH)
@@ -72,6 +72,8 @@
         )
         return carry
 
+    if xy is None:
+        return lambda: pl.semaphore_wait(barrier, len(devices))
     lax.fori_loop(1, 16, one, 0)
     return lambda: pl.semaphore_wait(barrier, len(devices) + 15)
 
@@ -170,13 +172,117 @@
     return lax.rsqrt(jnp.mean(stream32 * stream32, axis=1, keepdims=True) + epsilon)
 
 
+PARTS = 2
+FIRST = 28
+
+
+def project_kernel(
+    context, residual, cotangent, own,
+    whole, total, ctx, cot,
+    res, sw, sp, rp,
+):
+    z, core, _ = place()
+    zl = lax.rem(z, 2)
+    partner = at_core(flip(core))
+    quarter = own.shape[0]
+    half = quarter // 2
+    piece = half // PARTS
+    entered = greet([at_z(mate(z)), at_z(cross(z)), partner])
+
+    def block_rows(block, start, size):
+        return whole.at[pl.ds(pl.multiple_of(block * quarter + start, piece), size)]
+
+    block = 2 * zl + core
+    load_ctx = pltpu.make_async_copy(context, ctx, sw.at[0])
+    load_own = pltpu.make_async_copy(own, block_rows(block, 0, quarter), sw.at[1])
+    load_res = pltpu.make_async_copy(residual, res, sw.at[2])
+    load_cot = pltpu.make_async_copy(cotangent, cot, sw.at[3])
+    load_own.start()
+    load_ctx.start()
+    load_res.start()
+    entered()
+
+    across = 2 * flip(zl) + core
+    over, on = [], []
+    for p in range(PARTS):
+        for side, device in enumerate((at_z(mate(z)), at_z(cross(z)))):
+            number = 2 * p + side
+            start = side * half + p * piece
+            over.append(
+                remote(
+                    own.at[pl.ds(start, piece)],
+                    block_rows(block, start, piece),
+                    sp.at[number],
+                    rp.at[number],
+                    device,
+                )
+            )
+            rows = block_rows(across, start, piece)
+            on.append(
+                remote(rows, rows, sp.at[2 * PARTS + number], rp.at[2 * PARTS + number], partner)
+            )
+    w_core = remote(own, block_rows(block, 0, quarter), sp.at[4 * PARTS], rp.at[4 * PARTS], partner)
+    for copy in over:
+        copy.start()
+    w_core.start()
+    load_cot.start()
+    load_ctx.wait()
+    load_res.wait()
+    load_own.wait()
+    add_block(ctx, whole, block, total, lambda b: res[b].astype(F32))
+    w_core.wait_recv()
+    add_block(ctx, whole, 2 * zl + flip(core), total, lambda b: total[b])
+    for first, second in zip(over, on):
+        first.wait_recv()
+        second.start()
+    for copy in on:
+        copy.wait()
+    for copy in over:
+        copy.wait_send()
+    w_core.wait_send()
+    load_cot.wait()
+
+
+def add_block(ctx, whole, block, total, start):
+    quarter = whole.shape[0] // 4
+    span = pl.ds(pl.multiple_of(block * quarter, quarter), quarter)
+    rows = whole[span, :]
+    for b in range(2):
+        total[b] = start(b) + times(ctx[b, :, span], rows)
+
+
+def project(context, residual, cotangent, own):
+    width = own.shape[-1]
+    dma = pltpu.SemaphoreType.DMA
+    afar = pl.BlockSpec(memory_space=pltpu.HBM)
+    return pl.pallas_call(
+        project_kernel,
+        out_shape=(
+            jax.ShapeDtypeStruct((width, width), BF16),
+            jax.ShapeDtypeStruct(context.shape, F32),
+            jax.ShapeDtypeStruct(context.shape, BF16),
+            jax.ShapeDtypeStruct(context.shape, BF16),
+        ),
+        in_specs=[afar] * 4,
+        out_specs=(pl.BlockSpec(memory_space=VMEM),) * 4,
+        scratch_shapes=[
+            VMEM(context.shape, BF16),
+            dma((4,)),
+            dma((4 * PARTS + 1,)),
+            dma((4 * PARTS + 1,)),
+        ],
+        compiler_params=params(1, 12 << 20),
+        name="project",
+    )(context, residual, cotangent, own)
+
+
 def expert_kernel(
-    context, residual, cotangent, own, slots, win, wout,
-    out, stream, normed, expo, whole, x, act, gpre,
-    ctx, res, cot, slots_here, natural,
+    ctx, cot, whole, total, slots, win, wout,
+    out, stream, normed, spread32, pulled, x, act, gpre,
+    slots_here, natural, expo,
     pairs, came, blocks, wi, wo, slope, o,
     halves, chip, paired, crossing, blocks2, pairs2, came2,
-    s1, r1, s2, r2, sa, ra, sb, rb, sc, rc, sw, sp, rp,
+    s1, r1, s2, r2, sa, ra, sb, rb, sc, rc, sw,
 ):
     z, core, xy = place()
     zh = lax.div(z, 2)
@@ -184,72 +290,18 @@
     partner = at_core(flip(core))
     width = x.shape[-1]
     hidden = act.shape[-1]
-    quarter = own.shape[0]
-    half = quarter // 2
-    entered = greet([at_z(mate(z)), at_z(cross(z)), partner], xy)
-
-    def block_rows(block, start, size):
-        return whole.at[pl.ds(pl.multiple_of(block * quarter + start, half), size)]
-
-    block = 2 * zl + core
-    load_ctx = pltpu.make_async_copy(context, ctx, sw.at[2])
-    load_own = pltpu.make_async_copy(own, block_rows(block, 0, quarter), sw.at[3])
-    load_res = pltpu.make_async_copy(residual, res, sw.at[4])
-    load_cot = pltpu.make_async_copy(cotangent, cot, sw.at[5])
+    entered = greet([at_z(mate(z)), at_z(cross(z)), at_z(far(z)), partner], xy)
+    load_slots = pltpu.make_async_copy(slots, slots_here, sw.at[2])
     load_in = pltpu.make_async_copy(win, wi, sw.at[0])
     load_out = pltpu.make_async_copy(wout, wo, sw.at[1])
-    load_slots = pltpu.make_async_copy(slots, slots_here, sw.at[6])
     load_slots.start()
-    load_own.start()
-    load_ctx.start()
-    load_res.start()
+    load_in.start()
+    load_out.start()
+    add_block(ctx, whole, 2 * flip(zl) + core, slope, lambda b: total[b])
+    add_block(ctx, whole, 2 * flip(zl) + flip(core), slope, lambda b: slope[b])
     load_slots.wait()
     unit32, _ = unit_of(slots_here)
     unit = unit32.astype(BF16)
-    entered()
-
-    across = 2 * flip(zl) + core
-    w_mate = remote(
-        own.at[pl.ds(0, half)], block_rows(block, 0, half), sp.at[0], rp.at[0], at_z(mate(z))
-    )
-    w_cross = remote(
-        own.at[pl.ds(half, half)], block_rows(block, half, half), sp.at[1], rp.at[1], at_z(cross(z))
-    )
-    w_core = remote(own, block_rows(block, 0, quarter), sp.at[2], rp.at[2], partner)
-    w_first = remote(
-        block_rows(across, 0, half), block_rows(across, 0, half), sp.at[3], rp.at[3], partner
-    )
-    w_second = remote(
-        block_rows(across, half, half), block_rows(across, half, half), sp.at[4], rp.at[4], partner
-    )
-    w_mate.start()
-    w_cross.start()
-    w_core.start()
-    load_cot.start()
-    load_in.start()
-    load_out.start()
-    load_ctx.wait()
-    load_res.wait()
-    load_own.wait()
-
-    def project(block, first=False):
-        rows = whole[pl.ds(pl.multiple_of(block * quarter, quarter), quarter), :]
-        for b in range(2):
-            columns = ctx[b, :, pl.ds(pl.multiple_of(block * quarter, quarter), quarter)]
-            start = res[b].astype(F32) if first else slope[b]
-            slope[b] = start + times(columns, rows)
-
-    project(block, True)
-    w_core.wait_recv()
-    project(2 * zl + flip(core))
-    w_mate.wait_recv()
-    w_first.start()
-    w_cross.wait_recv()
-    w_second.start()
-    project(across)
-    w_first.wait_recv()
-    w_second.wait_recv()
-    project(2 * flip(zl) + flip(core))
 
     def settle(i, carry):
         for b in range(2):
@@ -266,8 +318,9 @@
         rows = normed[b]
         ex = jnp.exp(factor * times_t(unit, rows))
         expo[b] = ex
-        dispatch = (ex / jnp.sum(ex, axis=1, keepdims=True)).astype(BF16)
-        natural[0, 64 * b : 64 * b + 64] = times(dispatch, rows).astype(BF16)
+        dispatch32 = ex / jnp.sum(ex, axis=1, keepdims=True)
+        spread32[b] = dispatch32
+        natural[0, 64 * b : 64 * b + 64] = times(dispatch32.astype(BF16), rows).astype(BF16)
     pairs[0] = reorder(to_pairs, natural[0])
 
     def swap(kind):
@@ -284,42 +337,47 @@
             rows8(pairs, kind, xy), rows8(came, kind, xy), s1.at[kind, 0]
         )
 
+    entered()
     keep(0).start()
     xy_start(*swap(0))
-    load_cot.wait()
     for b in range(2):
         ex = expo[b]
-        combine = (ex / jnp.sum(ex, axis=0, keepdims=True)).astype(BF16)
-        natural[1, 64 * b : 64 * b + 64] = times(combine, cot[b]).astype(BF16)
+        combine32 = ex / jnp.sum(ex, axis=0, keepdims=True)
+        expo[b] = combine32
+        natural[1, 64 * b : 64 * b + 64] = times(combine32.astype(BF16), cot[b]).astype(BF16)
     pairs[1] = reorder(to_pairs, natural[1])
     keep(1).start()
     xy_start(*swap(1))
 
-    def there(kind, zz):
-        return x.at[kind, :, zz, core]
-
-    def send(kind, number, src, zz, device):
-        return remote(src, there(kind, zz), s2.at[kind, number], r2.at[kind, number], device)
+    def there(kind, e, zz):
+        return x.at[kind, e, zz, core]
+
+    def send(kind, e, number, src, zz, device):
+        return remote(
+            src, there(kind, e, zz), s2.at[kind, e, number], r2.at[kind, e, number], device
+        )
 
     c, m, f = cross(z), mate(z), far(z)
 
-    def to_mate(kind):
-        return send(kind, 0, blocks.at[kind, zh], z, at_z(m))
-
-    def to_cross(kind):
-        return send(kind, 1, blocks.at[kind, flip(zh)], z, at_z(c))
-
-    def on_mate(kind):
-        return send(kind, 2, there(kind, c), c, at_z(m))
-
-    def to_core(kind, number):
+    def to_mate(kind, e):
+        return send(kind, e, 0, blocks.at[kind, zh, e], z, at_z(m))
+
+    def to_cross(kind, e):
+        return send(kind, e, 1, blocks.at[kind, flip(zh), e], z, at_z(c))
+
+    def on_mate(kind, e):
+        return send(kind, e, 2, there(kind, e, c), c, at_z(m))
+
+    def to_core(kind, e, number):
         if number == 3:
-            return send(kind, 3, blocks.at[kind, zh], z, partner)
+            return send(kind, e, 3, blocks.at[kind, zh, e], z, partner)
         zz = (c, m, f)[number - 4]
-        return send(kind, number, there(kind, zz), zz, partner)
-
-    def mine(kind):
-        return pltpu.make_async_copy(blocks.at[kind, zh], there(kind, z), s2.at[kind, 7])
+        return send(kind, e, number, there(kind, e, zz), zz, partner)
+
+    def mine(kind, e):
+        return pltpu.make_async_copy(
+            blocks.at[kind, zh, e], there(kind, e, z), s2.at[kind, e, 7]
+        )
 
     def spread(kind):
         keep(kind).wait()
@@ -328,42 +386,34 @@
         for i in range(2):
             for e in range(2):
                 blocks[kind, i, e] = ordered[i * 64 + e * 32 : i * 64 + e * 32 + 32]
-        to_cross(kind).start()
-        to_mate(kind).start()
-        to_core(kind, 3).start()
-        mine(kind).start()
-
-    def relay(kind):
-        to_cross(kind).wait_recv()
-        on_mate(kind).start()
-        to_core(kind, 4).start()
-        to_mate(kind).wait_recv()
-        to_core(kind, 5).start()
-
-    def relay_last(kind):
-        on_mate(kind).wait_recv()
-        to_core(kind, 6).start()
-
-    def arrived(kind):
-        mine(kind).wait()
+        for e in range(2):
+            to_cross(kind, e).start()
+            to_mate(kind, e).start()
+            to_core(kind, e, 3).start()
+            mine(kind, e).start()
+
+    def relay(kind, e):
+        to_cross(kind, e).wait_recv()
+        on_mate(kind, e).start()
+        to_core(kind, e, 4).start()
+        to_mate(kind, e).wait_recv()
+        to_core(kind, e, 5).start()
+
+    def relay_last(kind, e):
+        on_mate(kind, e).wait_recv()
+        to_core(kind, e, 6).start()
+
+    def arrived(kind, e):
+        mine(kind, e).wait()
         for number in range(3, 7):
-            to_core(kind, number).wait_recv()
-
-    def sent(kind):
-        to_mate(kind).wait_send()
-        to_cross(kind).wait_send()
-        on_mate(kind).wait_send()
+            to_core(kind, e, number).wait_recv()
+
+    def sent(kind, e):
+        to_mate(kind, e).wait_send()
+        to_cross(kind, e).wait_send()
+        on_mate(kind, e).wait_send()
         for number in range(3, 7):
-            to_core(kind, number).wait_send()
-
-    spread(0)
-    spread(1)
-    relay(0)
-    relay(1)
-    relay_last(0)
-    arrived(0)
-    load_in.wait()
-    load_out.wait()
+            to_core(kind, e, number).wait_send()
 
     def rows_of(kind, e):
         return x[kind, e].reshape(256, width)
@@ -400,15 +450,25 @@
             o.at[kind, e, :, flip(core)], halves.at[kind, e], sa.at[kind, e], ra.at[kind, e], partner
         )
 
-    def home_mate(kind):
+    def home_mate(kind, e):
         return [
-            remote(chip.at[kind, zz], paired.at[kind, i], sb.at[kind, i], rb.at[kind, i], at_z(m))
+            remote(
+                chip.at[kind, zz, e],
+                paired.at[kind, i, e],
+                sb.at[kind, e, i],
+                rb.at[kind, e, i],
+                at_z(m),
+            )
             for i, zz in enumerate((f, m))
         ]
 
-    def home_cross(kind):
+    def home_cross(kind, e):
         return remote(
-            crossing.at[kind], blocks2.at[kind, zh], sb.at[kind, 2], rb.at[kind, 2], at_z(c)
+            crossing.at[kind, e],
+            blocks2.at[kind, zh, e],
+            sb.at[kind, e, 2],
+            rb.at[kind, e, 2],
+            at_z(c),
         )
 
     def home_swap(kind):
@@ -425,32 +485,30 @@
             rows8(pairs2, kind, xy), rows8(came2, kind, xy), sc.at[kind, 0]
         )
 
-    def chip_sum(kind):
+    def chip_sum(kind, e):
+        home_core(kind, e).wait()
+        for zz in range(4):
+            chip[kind, zz, e] = (
+                o[kind, e, zz, core].astype(F32) + halves[kind, e, zz].astype(F32)
+            ).astype(BF16)
+        home_mate(kind, e)[0].start()
+
+    def pass_on(kind, e):
+        home_mate(kind, e)[0].wait_recv()
+        crossing[kind, e] = (
+            chip[kind, c, e].astype(F32) + paired[kind, 0, e].astype(F32)
+        ).astype(BF16)
+        home_cross(kind, e).start()
+
+    def pair_sum(kind, e):
+        home_mate(kind, e)[1].wait_recv()
+        blocks2[kind, zh, e] = (
+            chip[kind, z, e].astype(F32) + paired[kind, 1, e].astype(F32)
+        ).astype(BF16)
+
+    def home(kind):
         for e in range(2):
-            home_core(kind, e).wait()
-            for zz in range(4):
-                chip[kind, zz, e] = (
-                    o[kind, e, zz, core].astype(F32) + halves[kind, e, zz].astype(F32)
-                ).astype(BF16)
-        for copy in home_mate(kind):
-            copy.start()
-
-    def pair_sum(kind):
-        on, own = home_mate(kind)
-        on.wait_recv()
-        for e in range(2):
-            crossing[kind, e] = (
-                chip[kind, c, e].astype(F32) + paired[kind, 0, e].astype(F32)
-            ).astype(BF16)
-        home_cross(kind).start()
-        own.wait_recv()
-        for e in range(2):
-            blocks2[kind, zh, e] = (
-                chip[kind, z, e].astype(F32) + paired[kind, 1, e].astype(F32)
-            ).astype(BF16)
-
-    def home(kind):
-        home_cross(kind).wait_recv()
+            home_cross(kind, e).wait_recv()
         rows = jnp.concatenate([blocks2[kind, i, e] for i in range(2) for e in range(2)], axis=0)
         pairs2[kind] = reorder(from_blocks, rows)
         home_keep(kind).start()
@@ -461,98 +519,71 @@
         xy_wait(*home_swap(kind))
         out[kind] = reorder(from_pairs, came2[kind])
 
+    spread(0)
+    spread(1)
+    relay(0, 0)
+    relay(0, 1)
+    relay_last(0, 0)
+    relay(1, 0)
+    relay_last(0, 1)
+    relay(1, 1)
+    load_in.wait()
+    load_out.wait()
+    arrived(0, 0)
     up(0)
+    relay_last(1, 0)
+    arrived(0, 1)
     up(1)
-    relay_last(1)
+    relay_last(1, 1)
     for e in range(2):
         down(e)
         home_core(0, e).start()
-    arrived(1)
+    arrived(1, 0)
     back_down(0)
+    back_up(0)
+    home_core(1, 0).start()
+    chip_sum(0, 0)
+    chip_sum(0, 1)
+    arrived(1, 1)
     back_down(1)
-    chip_sum(0)
+    back_up(1)
+    home_core(1, 1).start()
+    chip_sum(1, 0)
+    pass_on(0, 0)
+    pass_on(0, 1)
+    chip_sum(1, 1)
     for e in range(2):
-        back_up(e)
-        home_core(1, e).start()
-    chip_sum(1)
-    pair_sum(0)
-    pair_sum(1)
+        home_mate(0, e)[1].start()
+    for e in range(2):
+        home_mate(1, e)[1].start()
+    pass_on(1, 0)
+    pass_on(1, 1)
+    for e in range(2):
+        pair_sum(0, e)
     home(0)
+    for e in range(2):
+        pair_sum(1, e)
     home(1)
     landed(0)
+    for b in range(2):
+        combine32 = expo[b]
+        grad_combine = times_t(out[0, 64 * b : 64 * b + 64], cot[b])
+        pulled[b] = combine32 * (
+            grad_combine - jnp.sum(combine32 * grad_combine, axis=0, keepdims=True)
+        )
     landed(1)
-    for copy in (w_mate, w_cross, w_core, w_first, w_second):
-        copy.wait_send()
     for kind in range(2):
-        sent(kind)
-        for copy in home_mate(kind):
-            copy.wait_send()
-        home_cross(kind).wait_send()
-
-
-def experts(context, residual, cotangent, own, slots, expert_in, expert_out):
-    width = context.shape[-1]
-    hidden = expert_in.shape[-1]
-    dma = pltpu.SemaphoreType.DMA
-    here = pl.BlockSpec(memory_space=VMEM)
-    afar = pl.BlockSpec(memory_space=pltpu.HBM)
-    return pl.pallas_call(
-        expert_kernel,
-        out_shape=(
-            jax.ShapeDtypeStruct((2, 128, width), BF16),
-            jax.ShapeDtypeStruct(context.shape, BF16),
-            jax.ShapeDtypeStruct(context.shape, BF16),
-            jax.ShapeDtypeStruct((2, 64, 256), F32),
-            jax.ShapeDtypeStruct((width, width), BF16),
-            jax.ShapeDtypeStruct((2, 2, 4, 2, 32, width), BF16),
-            jax.ShapeDtypeStruct((2, 256, hidden), BF16),
-            jax.ShapeDtypeStruct((2, 256, hidden), BF16),
-        ),
-        in_specs=[afar] * 7,
-        out_specs=(here,) * 8,
-        scratch_shapes=[
-            VMEM(context.shape, BF16),
-            VMEM(context.shape, BF16),
-            VMEM(context.shape, BF16),
-            VMEM(slots.shape, BF16),
-            VMEM((2, 128, width), BF16),
-            VMEM((2, 128, width), BF16),
-            VMEM((2, 128, width), BF16),
-            VMEM((2, 2, 2, 32, width), BF16),
-            VMEM(expert_in.shape, BF16),
-            VMEM(expert_out.shape, BF16),
-            VMEM((2, 256, hidden), F32),
-            VMEM((2, 2, 4, 2, 32, width), BF16),
-            VMEM((2, 2, 4, 32, width), BF16),
-            VMEM((2, 4, 2, 32, width), BF16),
-            VMEM((2, 2, 2, 32, width), BF16),
-            VMEM((2, 2, 32, width), BF16),
-            VMEM((2, 2, 2, 32, width), BF16),
-            VMEM((2, 128, width), BF16),
-            VMEM((2, 128, width), BF16),
-            dma((2, 16)),
-            dma((2, 16)),
-            dma((2, 8)),
-            dma((2, 8)),
-            dma((2, 2)),
-            dma((2, 2)),
-            dma((2, 3)),
-            dma((2, 3)),
-            dma((2, 16)),
-            dma((2, 16)),
-            dma((7,)),
-            dma((5,)),
-            dma((5,)),
-        ],
-        compiler_params=params(2, 36 << 20),
-        name="experts",
-    )(context, residual, cotangent, own, slots, expert_in, expert_out)
+        for e in range(2):
+            sent(kind, e)
+            for copy in home_mate(kind, e):
+                copy.wait_send()
+            home_cross(kind, e).wait_send()
 
 
 def sum_kernel(
-    back, stream, normed, expo, whole, slots, context, cotangent,
+    back, stream, normed, spread32, pulled, whole, ctx, cot, slots,
     gctx, gres, out, u_out,
-    ctx, cot, slots_here, gn, unit_part,
+    slots_here, gn, unit_part,
     gs, ga, mine, gq, gb, gh, gc, gt, gf, gv, gall,
     ua, uw, uc, ut, uz, uv, uall, uother,
     sw, sg, rg, su, ru, s1, r1, s2, r2, s3, r3, s4, r4,
@@ -561,7 +592,6 @@
     zl = lax.rem(z, 2)
     partner = at_core(flip(core))
     ring = [at_z(lax.rem(z + d, 4)) for d in range(1, 4)]
-    entered = greet([*ring, partner], xy)
     width = stream.shape[-1]
     quarter = width // 4
     half = quarter // 2
@@ -569,27 +599,16 @@
     wide = width // 4
     cut = width // PIECES
     factor = logit_scale / math.sqrt(width)
-    load_ctx = pltpu.make_async_copy(context, ctx, sw.at[0])
-    load_cot = pltpu.make_async_copy(cotangent, cot, sw.at[1])
-    load_slots = pltpu.make_async_copy(slots, slots_here, sw.at[2])
+    load_slots = pltpu.make_async_copy(slots, slots_here, sw.at[0])
     load_slots.start()
-    load_cot.start()
-    load_ctx.start()
     load_slots.wait()
     unit32, norm = unit_of(slots_here)
     unit = unit32.astype(BF16)
-    load_cot.wait()
     for b in range(2):
-        ex = expo[b]
-        dispatch32 = ex / jnp.sum(ex, axis=1, keepdims=True)
-        combine32 = ex / jnp.sum(ex, axis=0, keepdims=True)
+        dispatch32 = spread32[b]
         grad_in = back[1, 64 * b : 64 * b + 64]
-        grad_combine = times_t(back[0, 64 * b : 64 * b + 64], cot[b])
         grad_dispatch = times_t(grad_in, normed[b])
-        grad_logits = combine32 * (
-            grad_combine - jnp.sum(combine32 * grad_combine, axis=0, keepdims=True)
-        )
-        grad_logits = grad_logits + dispatch32 * (
+        grad_logits = pulled[b] + dispatch32 * (
             grad_dispatch - jnp.sum(dispatch32 * grad_dispatch, axis=1, keepdims=True)
         )
         grad_logits = grad_logits.astype(BF16)
@@ -598,7 +617,6 @@
             rows = part[32 * i : 32 * i + 32]
             unit_part[i] = rows if b == 0 else unit_part[i] + rows
         gn[b] = t_times(dispatch32.astype(BF16), grad_in) + factor * t_times(grad_logits, unit)
-    entered()
     u_core = remote(unit_part.at[flip(core)], ua, su.at[0], ru.at[0], partner)
     u_core.start()
 
@@ -617,7 +635,6 @@
 
     lax.fori_loop(0, 4, settle, 0)
 
-    load_ctx.wait()
 
     def proj(block, h):
         left = ctx[:, :, pl.ds(pl.multiple_of(block * quarter, quarter), quarter)]
@@ -777,8 +794,22 @@
         finish(h)
 
 
-def sums(back, stream, normed, expo, whole, slots, context, cotangent):
-    width = stream.shape[-1]
+def layer_kernel(ctx, cot, whole, total, slots, win, wout, *refs):
+    x, act, gpre, gctx, gres, gproj, gslots, back, stream, normed, spread32, pulled = refs[:12]
+    first, second = refs[12 : 12 + FIRST], refs[12 + FIRST :]
+    expert_kernel(
+        ctx, cot, whole, total, slots, win, wout,
+        back, stream, normed, spread32, pulled, x, act, gpre, *first,
+    )
+    sum_kernel(
+        back, stream, normed, spread32, pulled, whole, ctx, cot, slots,
+        gctx, gres, gproj, gslots, *second,
+    )
+
+
+def layer(ctx, cot, whole, total, slots, expert_in, expert_out):
+    width = ctx.shape[-1]
+    hidden = expert_in.shape[-1]
     rows = width // 4
     chunk = rows // 16
     wide = width // 4
@@ -786,58 +817,99 @@
     dma = pltpu.SemaphoreType.DMA
     here = pl.BlockSpec(memory_space=VMEM)
     afar = pl.BlockSpec(memory_space=pltpu.HBM)
+    first = [
+        VMEM(slots.shape, BF16),
+        VMEM((2, 128, width), BF16),
+        VMEM((2, 64, 256), F32),
+        VMEM((2, 128, width), BF16),
+        VMEM((2, 128, width), BF16),
+        VMEM((2, 2, 2, 32, width), BF16),
+        VMEM(expert_in.shape, BF16),
+        VMEM(expert_out.shape, BF16),
+        VMEM((2, 256, hidden), F32),
+        VMEM((2, 2, 4, 2, 32, width), BF16),
+        VMEM((2, 2, 4, 32, width), BF16),
+        VMEM((2, 4, 2, 32, width), BF16),
+        VMEM((2, 2, 2, 32, width), BF16),
+        VMEM((2, 2, 32, width), BF16),
+        VMEM((2, 2, 2, 32, width), BF16),
+        VMEM((2, 128, width), BF16),
+        VMEM((2, 128, width), BF16),
+        dma((2, 16)),
+        dma((2, 16)),
+        dma((2, 2, 8)),
+        dma((2, 2, 8)),
+        dma((2, 2)),
+        dma((2, 2)),
+        dma((2, 2, 3)),
+        dma((2, 2, 3)),
+        dma((2, 16)),
+        dma((2, 16)),
+        dma((3,)),
+    ]
+    second = [
+        VMEM(slots.shape, BF16),
+        VMEM(ctx.shape, F32),
+        VMEM((2, 32, width), F32),
+        VMEM((PIECES, 2, rows, cut), BF16),
+        VMEM((PIECES, 2, rows, cut), BF16),
+        VMEM((PIECES, rows, cut), F32),
+        VMEM((PIECES, rows, cut), BF16),
+        VMEM((PIECES, rows, cut), BF16),
+        VMEM((PIECES, rows, cut), BF16),
+        VMEM((PIECES, 16, chunk, cut), BF16),
+        VMEM((PIECES, chunk, cut), BF16),
+        VMEM((PIECES, chunk, cut), BF16),
+        VMEM((PIECES, chunk, cut), BF16),
+        VMEM((PIECES, 16, chunk, cut), BF16),
+        VMEM((32, width), F32),
+        VMEM((16, 8, wide), F32),
+        VMEM((16, 8, wide), F32),
+        VMEM((8, wide), F32),
+        VMEM((4, 8, wide), F32),
+        VMEM((8, wide), F32),
+        VMEM((16, 8, wide), F32),
+        VMEM((16, 8, wide), F32),
+        dma((1,)),
+        dma((PIECES, 5)),
+        dma((PIECES, 5)),
+        dma((6,)),
+        dma((6,)),
+        dma((16,)),
+        dma((16,)),
+        dma((PIECES, 16)),
+        dma((PIECES, 16)),
+        dma((16,)),
+        dma((16,)),
+        dma((PIECES, 16)),
+        dma((PIECES, 16)),
+    ]
+    assert len(first) == FIRST
     return pl.pallas_call(
-        sum_kernel,
+        layer_kernel,
         out_shape=(
-            jax.ShapeDtypeStruct(context.shape, BF16),
-            jax.ShapeDtypeStruct(context.shape, BF16),
+            jax.ShapeDtypeStruct((2, 2, 4, 2, 32, width), BF16),
+            jax.ShapeDtypeStruct((2, 256, hidden), BF16),
+            jax.ShapeDtypeStruct((2, 256, hidden), BF16),
+            jax.ShapeDtypeStruct(ctx.shape, BF16),
+            jax.ShapeDtypeStruct(ctx.shape, BF16),
             jax.ShapeDtypeStruct((rows, width), F32),
             jax.ShapeDtypeStruct((64, width), F32),
         ),
-        in_specs=[here] * 5 + [afar] * 3,
-        out_specs=(here,) * 4,
+        in_specs=[here] * 4 + [afar] * 3,
+        out_specs=(here,) * 7,
         scratch_shapes=[
-            VMEM(context.shape, BF16),
-            VMEM(context.shape, BF16),
-            VMEM(slots.shape, BF16),
-            VMEM(context.shape, F32),
-            VMEM((2, 32, width), F32),
-            VMEM((PIECES, 2, rows, cut), BF16),
-            VMEM((PIECES, 2, rows, cut), BF16),
-            VMEM((PIECES, rows, cut), F32),
-            VMEM((PIECES, rows, cut), BF16),
-            VMEM((PIECES, rows, cut), BF16),
-            VMEM((PIECES, rows, cut), BF16),
-            VMEM((PIECES, 16, chunk, cut), BF16),
-            VMEM((PIECES, chunk, cut), BF16),
-            VMEM((PIECES, chunk, cut), BF16),
-            VMEM((PIECES, chunk, cut), BF16),
-            VMEM((PIECES, 16, chunk, cut), BF16),
-            VMEM((32, width), F32),
-            VMEM((16, 8, wide), F32),
-            VMEM((16, 8, wide), F32),
-            VMEM((8, wide), F32),
-            VMEM((4, 8, wide), F32),
-            VMEM((8, wide), F32),
-            VMEM((16, 8, wide), F32),
-            VMEM((16, 8, wide), F32),
-            dma((3,)),
-            dma((PIECES, 5)),
-            dma((PIECES, 5)),
-            dma((6,)),
-            dma((6,)),
-            dma((16,)),
-            dma((16,)),
-            dma((PIECES, 16)),
-            dma((PIECES, 16)),
-            dma((16,)),
-            dma((16,)),
-            dma((PIECES, 16)),
-            dma((PIECES, 16)),
+            VMEM((2, 128, width), BF16),
+            VMEM(ctx.shape, BF16),
+            VMEM(ctx.shape, BF16),
+            VMEM((2, 64, 256), F32),
+            VMEM((2, 64, 256), F32),
+            *first,
+            *second,
         ],
-        compiler_params=params(4, 28 << 20),
-        name="sums",
-    )(back, stream, normed, expo, whole, slots, context, cotangent)
+        compiler_params=params(2, 40 << 20),
+        name="layer",
+    )(ctx, cot, whole, total, slots, expert_in, expert_out)
 
 
 def result_kernel(
@@ -908,13 +980,9 @@
         pltpu.with_memory_space_constraint(a, pltpu.HBM)
         for a in (context, residual, cotangent, proj_weight, slots, expert_in, expert_out)
     )
-    back, stream, normed, expo, whole, x, act, gpre = experts(
-        context, residual, cotangent, proj_weight, slots, expert_in, expert_out
-    )
-    four = sums(back, stream, normed, expo, whole, slots, context, cotangent)
-    grad_context, grad_residual, grad_proj, grad_slots, grad_in, grad_out = results(
-        x, act, gpre, *four
-    )
+    whole, total, ctx, cot = project(context, residual, cotangent, proj_weight)
+    made = layer(ctx, cot, whole, total, slots, expert_in, expert_out)
+    grad_context, grad_residual, grad_proj, grad_slots, grad_in, grad_out = results(*made)
     return grad_context, grad_residual, grad_proj, grad_slots.T, grad_in, grad_out
 
 

time: 107 us -> 103 us (0.963)
  Pallas kernels: 106 us -> 102 us
    pallas_call x2, Pallas kernels: 102 us -> 97.5 us  [the longest x1 84.8 us: layer(): pl.pallas_call(layer_kernel, out_shape=(jax.ShapeDtypeStruct((2, 2, 4, 2,...]
where the time goes in v5:
time: 103 us
  Pallas kernels  102 us (99%)
    pallas_call x1, Pallas kernels, layer(): pl.pallas_call(layer_kernel, out_shape=(jax.ShapeDtypeStruct((2, 2, 4, 2,...  84.8 us
    pallas_call x1, Pallas kernels, project(): pl.pallas_call(project_kernel, out_shape=(jax.ShapeDtypeStruct((width, wi...  12.6 us
    pallas_call x1, Pallas kernels, results(): pl.pallas_call(result_kernel, out_shape=tuple((jax.ShapeDtypeStruct(a.sha...  4.43 us

profile of v5, /device:TPU:0, one launch (start us, length us, event | category | flops | bytes accessed | tf_op | source)
XLA Modules:
  0.0 102.7 jit_solution(3943212228490352024)
XLA Ops:
  0.6 12.6 %project.1 = (bf16[1024,1024]{1,0:T(8,128)(2,1)S(1)}, f32[2,256,1024]{2,1,0:T(8,128)S(1)}, bf16[2,256,1024]{2,1,0:T(8,128)(2,1)S(1)}, bf16[2,256,1024]{2,1,0:T(8,128)(2,1)S(1)}) custom-call(bf16[2,256,1024]{2,1,0:T(8,128)(2,1)} %context.1, bf16[2,256,1024]{2,1,0:T(8,128)(2,1)} %residual.1, bf16[2,256,1024]{2,1,0:T(8,128)(2,1)} %cotangent.1, ...), custom_call_target="tpu_custom_call" | custom-call | tf_op jit(solution)/shard_map/project/pallas_call | solution.py:258
  13.3 84.8 %layer.1 = (bf16[2,2,4,2,32,1024]{5,4,3,2,1,0:T(8,128)(2,1)S(1)}, bf16[2,256,1024]{2,1,0:T(8,128)(2,1)S(1)}, bf16[2,256,1024]{2,1,0:T(8,128)(2,1)S(1)}, bf16[2,2...) custom-call(bf16[2,256,1024]{2,1,0:T(8,128)(2,1)S(1)} %get-tuple-ele, ...), custom_call_target="tpu_custom_call" | custom-call | tf_op jit(solution)/shard_map/layer/pallas_call | solution.py:888
  98.1 4.4 %results.1 = (bf16[2,256,1024]{2,1,0:T(8,128)(2,1)}, bf16[2,256,1024]{2,1,0:T(8,128)(2,1)}, f32[256,1024]{1,0:T(8,128)}, f32[64,1024]{1,0:T(8,128)}, bf16[2,1024...) custom-call(bf16[2,2,4,2,32,1024]{5,4,3,2,1,0:T(8,128)(2,1)S(1)} %get-tuple-element.27.x, ...), custom_call_target="tpu_custom_call" | custom-call | tf_op jit(solution)/shard_map/results/pallas_call | solution.py:958
